TPU v7x, 32 devices: a whole 2x2x4 slice. The times are simulated.
32 devices in a mesh: frame: 16 (over z, y, core), row: 2 (over x).
Axes of the slice: x: 2, y: 2, z: 4, core: 2. Of those that a mesh axis runs over, the one named last changes fastest.
Arguments:
- spatial_q: bfloat16 [16, 256, 3072], P('frame', 'row'), may hold values from -6 to 6
- spatial_k: bfloat16 [16, 256, 3072], P('frame', 'row'), may hold values from -6 to 6
- spatial_v: bfloat16 [16, 256, 3072], P('frame', 'row'), may hold values from -6 to 6
- norm_gain: float32 [3072], replicated, may hold values from 0.5 to 1.5
- temporal_weight: bfloat16 [3072, 3, 3072], P(None, None, 'row'), may hold values from -0.625 to 0.625
Outputs:
- temporal_out: bfloat16 [16, 256, 3072], P('frame', 'row')
All inputs are finite; a program needn't handle non-finite values.
Results may differ from a plain program's by a relative error of at most 0.0083.
Values may be sent and summed in bfloat16 or wider, within the bound.
No kernel may reach another device: no remote copies, remote signals or barrier semaphores. Data moves between devices by JAX's collectives and lax.ppermute only.
A program may use at most 64 MiB of HBM per device.

v0:
```python
import math
from functools import partial

import jax
import jax.numpy as jnp
from jax import lax
from jax.experimental import pallas as pl
from jax.experimental.pallas import tpu as pltpu
from jax.sharding import PartitionSpec as P

D = 3072
HEADS = 24
AGENTS = 128
HEAD = D // HEADS
SCALE = HEAD ** (-0.5)
EXPONENT = SCALE * math.log2(math.e)

epsilon = 1e-06


def dot(left, right):
    return jnp.dot(left, right, preferred_element_type=jnp.float32)


def dot_nt(left, right):
    return lax.dot_general(
        left, right, (((1,), (1,)), ((), ())), preferred_element_type=jnp.float32
    )


def weighted(scores):
    weights = jnp.exp2((scores - jnp.max(scores, axis=1, keepdims=True)) * EXPONENT)
    return weights, 1.0 / jnp.sum(weights, axis=1, keepdims=True)


def spatial_kernel(base, q, k, v, *rest, heads, pool, tiled):
    received, gain, out = rest[:-2], rest[-2], rest[-1]
    ways = len(received) + 1
    tokens = q.shape[1]
    agent = lax.broadcasted_iota(jnp.int32, (tokens // pool, tokens), 0)
    token = lax.broadcasted_iota(jnp.int32, (tokens // pool, tokens), 1)
    member = ((token >= agent * pool) & (token < (agent + 1) * pool)).astype(jnp.bfloat16)
    split = [slice(h * HEAD, (h + 1) * HEAD) for h in range(heads)]
    pooled = [dot(member, block) for block in [q[0]] + [ref[0] for ref in received]]
    pooled = (jnp.concatenate(pooled) * (1.0 / pool)).astype(jnp.bfloat16)
    agents = [pooled[:, cols] for cols in split]
    queries = [jnp.concatenate([q[0, :, cols]] + [r[0, :, cols] for r in received]) for cols in split]
    keys = [jnp.concatenate([k[0, :, cols]] + [r[1, :, cols] for r in received]) for cols in split]
    values = [jnp.concatenate([v[0, :, cols]] + [r[2, :, cols] for r in received]) for cols in split]
    agent_scores = [dot_nt(a, b) for a, b in zip(agents, keys)]
    token_scores = [dot_nt(a, b) for a, b in zip(queries, agents)]
    agent_weights = [weighted(x) for x in agent_scores]
    token_weights = [weighted(x) for x in token_scores]
    agent_values = [
        (dot(w.astype(jnp.bfloat16), x) * r).astype(jnp.bfloat16)
        for (w, r), x in zip(agent_weights, values)
    ]
    results = [dot((w * r).astype(jnp.bfloat16), x) for (w, r), x in zip(token_weights, agent_values)]
    for cols, result in zip(split, results):
        result = (result * gain[:, cols]).astype(jnp.bfloat16)
        for j in range(ways):
            block = result[j * tokens : (j + 1) * tokens]
            if tiled:
                out[:, j, :, cols] = block.reshape(out.shape[0], out.shape[2], HEAD)
            else:
                out[j, :, cols] = block


def spatial(q, k, v, received, gain, base, frames, width, heads):
    tokens = q.shape[1]
    ways = len(received) + 1
    slot = tokens // frames
    pool = tokens * ways // AGENTS
    step = heads * HEAD
    tiled = slot % 8 == 0
    own = pl.BlockSpec((1, tokens, step), lambda i, base: (0, 0, base[0] // heads + i))
    other = pl.BlockSpec((3, tokens, step), lambda i, base: (0, 0, i))
    if tiled:
        shape = (frames, ways, slot, width)
        out_spec = pl.BlockSpec((frames, ways, slot, step), lambda i, base: (0, 0, 0, i))
    else:
        shape = (ways, tokens, width)
        out_spec = pl.BlockSpec((ways, tokens, step), lambda i, base: (0, 0, i))
    out = pl.pallas_call(
        partial(spatial_kernel, heads=heads, pool=pool, tiled=tiled),
        out_shape=jax.ShapeDtypeStruct(shape, jnp.bfloat16),
        grid_spec=pltpu.PrefetchScalarGridSpec(
            num_scalar_prefetch=1,
            grid=(width // step,),
            in_specs=[own] * 3
            + [other] * len(received)
            + [pl.BlockSpec((1, step), lambda i, base: (0, base[0] // heads + i))],
            out_specs=out_spec,
        ),
        cost_estimate=pl.CostEstimate(
            flops=10 * tokens * ways * AGENTS * width,
            bytes_accessed=10 * tokens * ways * width,
            transcendentals=2 * tokens * ways * width,
        ),
        compiler_params=pltpu.CompilerParams(vmem_limit_bytes=12 << 20),
        name="spatial",
    )(base, q, k, v, *received, gain)
    if not tiled:
        out = out.reshape(ways, frames, slot, width).transpose(1, 0, 2, 3)
    return out


def rows_of(ref, block, cols, tokens, tiled):
    if tiled:
        return ref[:, block, :, cols].reshape(tokens, -1)
    return ref[block, :, cols]


def squares(x, inverse):
    y = x.astype(jnp.float32) * inverse
    y = y * y
    total = y[:, :HEAD]
    for at in range(HEAD, y.shape[1], HEAD):
        total = total + y[:, at : at + HEAD]
    return total


def project_kernel(at, *refs, pieces, arrays, first, tokens, ways, tiled):
    xs = refs[:arrays]
    if first:
        w, inverse, acc, ss, held = refs[arrays:]
    else:
        w, inverse, acc_in, ss_in, acc, ss, held = refs[arrays:]
    depth = held.shape[1]
    step = pl.program_id(0)
    for i, (which, col, shift) in enumerate(pieces):

        @pl.when(step == i)
        def _():
            for j in range(ways):
                held[j * tokens : (j + 1) * tokens, :] = rows_of(
                    xs[which], (j - shift) % ways, slice(col, col + depth), tokens, tiled
                )

    @pl.when(step == 0)
    def _():
        acc[...] = jnp.zeros_like(acc) if first else acc_in[...]
        ss[...] = jnp.zeros_like(ss) if first else ss_in[...]

    ss[...] += squares(held[...], inverse[...])
    width = w.shape[2]
    tile = width // 3 if width % 3 == 0 else width
    for c in range(3):
        for n in range(0, width, tile):
            cols = slice(n, n + tile)
            acc[c, :, cols] += dot(held[...], w[c, :, cols])


def project(pieces, arrays, at, weight, inverse, depth, carried, tokens, ways, tiled):
    rows = tokens * ways
    width = weight.shape[2]
    whole = lambda shape: pl.BlockSpec(shape, lambda i, at: (0,) * len(shape))
    acc_shape, ss_shape = (3, rows, width), (rows, HEAD)
    in_specs = [whole(x.shape) for x in arrays] + [
        pl.BlockSpec((3, depth, width), lambda i, at: (0, at[i], 0)),
        pl.BlockSpec((1, depth), lambda i, at: (0, at[i])),
    ]
    operands = list(arrays) + [weight, inverse]
    if carried is not None:
        in_specs += [whole(acc_shape), whole(ss_shape)]
        operands += list(carried)
    return pl.pallas_call(
        partial(
            project_kernel,
            pieces=pieces,
            arrays=len(arrays),
            first=carried is None,
            tokens=tokens,
            ways=ways,
            tiled=tiled,
        ),
        out_shape=(
            jax.ShapeDtypeStruct(acc_shape, jnp.float32),
            jax.ShapeDtypeStruct(ss_shape, jnp.float32),
        ),
        grid_spec=pltpu.PrefetchScalarGridSpec(
            num_scalar_prefetch=1,
            grid=(len(pieces),),
            in_specs=in_specs,
            out_specs=(whole(acc_shape), whole(ss_shape)),
            scratch_shapes=[pltpu.VMEM((rows, depth), jnp.bfloat16)],
        ),
        cost_estimate=pl.CostEstimate(
            flops=6 * rows * depth * len(pieces) * width,
            bytes_accessed=6 * depth * len(pieces) * width + 8 * 3 * rows * width,
            transcendentals=0,
        ),
        compiler_params=pltpu.CompilerParams(vmem_limit_bytes=32 << 20),
        name="project",
    )(at, *operands)


def temporal_kernel(at, *refs, count, heads, tokens, ways, slot, tiled, pieces, columns):
    xs = refs[: len(columns)]
    ws = refs[len(columns) : len(columns) + count]
    inverses = refs[len(columns) + count : len(columns) + 2 * count]
    acc, ss = refs[len(columns) + 2 * count : len(columns) + 2 * count + 2]
    out, held, rstd = refs[-3:]
    depth = held.shape[2]

    @pl.when(pl.program_id(0) == 0)
    def _():
        total = ss[...]
        for i, (which, col, shift) in enumerate(pieces):
            for j in range(ways):
                held[i, j * tokens : (j + 1) * tokens, :] = rows_of(
                    xs[which], (j - shift) % ways, slice(col, col + depth), tokens, tiled
                )
            total = total + squares(held[i], inverses[i][...])
        mean = jnp.sum(total, axis=1, keepdims=True) * (1.0 / D)
        rstd[...] = jnp.broadcast_to(lax.rsqrt(mean + epsilon), rstd.shape)

    row = lax.broadcasted_iota(jnp.int32, (tokens, tokens), 0)
    col = lax.broadcasted_iota(jnp.int32, (tokens, tokens), 1)
    same = lax.rem(row, slot) == lax.rem(col, slot)
    qkv = []
    for c in range(3):
        value = acc[c]
        for i in range(count):
            value = value + dot(held[i], ws[i][c])
        qkv.append(value)
    qkv = [(x * jnp.concatenate([rstd[...]] * heads, axis=1)).astype(jnp.bfloat16) for x in qkv]
    split = [
        (j, slice(j * tokens, (j + 1) * tokens), slice(h * HEAD, (h + 1) * HEAD))
        for h in range(heads)
        for j in range(ways)
    ]
    scores = [
        jnp.where(same, dot_nt(qkv[0][rows, cols], qkv[1][rows, cols]), -1e30)
        for _, rows, cols in split
    ]
    weights = [weighted(x) for x in scores]
    me = at[count]
    for (j, rows, cols), (w, r) in zip(split, weights):
        result = dot((w * r).astype(jnp.bfloat16), qkv[2][rows, cols]).astype(jnp.bfloat16)
        target = lax.rem(me + ways - j, ways)
        if tiled:
            out[:, target, :, cols] = result.reshape(out.shape[0], slot, HEAD)
        else:
            out[target, :, cols] = result


def temporal(pieces, arrays, at, weight, inverse, depth, carried, tokens, ways, slot, tiled):
    rows = tokens * ways
    width = weight.shape[2]
    count = len(pieces)
    frames = tokens // slot
    heads = math.gcd(width // HEAD, 6)
    step = heads * HEAD
    if tiled:
        shape = (frames, ways, slot, width)
        out_spec = pl.BlockSpec((frames, ways, slot, step), lambda n, at: (0, 0, 0, n))
    else:
        shape = (ways, tokens, width)
        out_spec = pl.BlockSpec((ways, tokens, step), lambda n, at: (0, 0, n))
    whole = lambda shape: pl.BlockSpec(shape, lambda n, at: (0,) * len(shape))
    at_piece = lambda i: pl.BlockSpec((3, depth, step), lambda n, at: (0, at[i], n))
    gain_piece = lambda i: pl.BlockSpec((1, depth), lambda n, at: (0, at[i]))
    out = pl.pallas_call(
        partial(
            temporal_kernel,
            count=count,
            heads=heads,
            tokens=tokens,
            ways=ways,
            slot=slot,
            tiled=tiled,
            pieces=pieces,
            columns=tuple(range(len(arrays))),
        ),
        out_shape=jax.ShapeDtypeStruct(shape, jnp.bfloat16),
        grid_spec=pltpu.PrefetchScalarGridSpec(
            num_scalar_prefetch=1,
            grid=(width // step,),
            in_specs=[whole(x.shape) for x in arrays]
            + [at_piece(i) for i in range(count)]
            + [gain_piece(i) for i in range(count)]
            + [
                pl.BlockSpec((3, rows, step), lambda n, at: (0, 0, n)),
                whole((rows, HEAD)),
            ],
            out_specs=out_spec,
            scratch_shapes=[
                pltpu.VMEM((count, rows, depth), jnp.bfloat16),
                pltpu.VMEM((rows, HEAD), jnp.float32),
            ],
        ),
        cost_estimate=pl.CostEstimate(
            flops=6 * rows * depth * count * width,
            bytes_accessed=6 * depth * count * width + 4 * 3 * rows * width,
            transcendentals=rows * width,
        ),
        compiler_params=pltpu.CompilerParams(vmem_limit_bytes=24 << 20),
        name="temporal",
    )(at, *arrays, *[weight] * count, *[inverse] * count, *carried)
    if not tiled:
        out = out.reshape(ways, frames, slot, width).transpose(1, 0, 2, 3)
    return out


def local(spatial_q, spatial_k, spatial_v, norm_gain, temporal_weight):
    frames = lax.axis_size("frame")
    ways = lax.axis_size("row")
    me = lax.axis_index("row").astype(jnp.int32)
    tokens = spatial_q.shape[1]
    slot = tokens // frames
    tiled = slot % 8 == 0
    width = temporal_weight.shape[2]
    group = width // HEAD
    unit = group // 4 if group % 4 == 0 else 1
    depth = unit * HEAD
    units = group // unit
    chunks = (range(0, units - units // 2), range(units - units // 2, units))
    weight = jnp.transpose(temporal_weight, (1, 0, 2))
    gain = norm_gain.reshape(1, -1)
    inverse = 1.0 / gain

    def shift(x, k):
        return lax.ppermute(x, "row", [(i, (i + k) % ways) for i in range(ways)])

    received = []
    for chunk in chunks:
        parts = []
        for k in range(1, ways):
            column = lax.rem(me + k, ways) * width + chunk[0] * depth
            stack = [
                lax.dynamic_slice_in_dim(x[0], column, len(chunk) * depth, axis=1)
                for x in (spatial_q, spatial_k, spatial_v)
            ]
            parts.append(shift(jnp.stack(stack), k))
        received.append(parts)

    pieces = {}
    for chunk, parts in zip(chunks, received):
        base = (me * group + chunk[0] * unit).reshape(1)
        heads = math.gcd(group, chunk[0] * unit, len(chunk) * unit)
        out = spatial(
            spatial_q,
            spatial_k,
            spatial_v,
            parts,
            gain,
            base,
            frames,
            len(chunk) * depth,
            min(heads, unit),
        )
        moved = lax.all_to_all(out, "frame", split_axis=0, concat_axis=0, tiled=True)
        for n, u in enumerate(chunk):
            pieces[u, 0] = (moved, n * depth)
        for k in range(1, ways):
            shared = shift(moved, k)
            for n, u in enumerate(chunk):
                pieces[u, k] = (shared, n * depth)

    def gather(wanted):
        listed, arrays, at = [], [], []
        for u, k in wanted:
            array, column = pieces[u, k]
            where = [i for i, x in enumerate(arrays) if x is array]
            if not where:
                where = [len(arrays)]
                arrays.append(array)
            listed.append((where[0], column, k))
            at.append(lax.rem(me + ways - k, ways) * units + u)
        if not tiled:
            arrays = [x.transpose(1, 0, 2, 3).reshape(ways, tokens, -1) for x in arrays]
        return tuple(listed), arrays, jnp.stack(at + [me])

    sizes = dict(tokens=tokens, ways=ways, tiled=tiled)
    early = [(u, 0) for u in chunks[0]]
    late = [(u, k) for k in range(1, ways) for u in chunks[0]] + [(u, 0) for u in chunks[1]]
    final = [(u, k) for k in range(1, ways) for u in chunks[1]]
    carried = project(*gather(early), weight, inverse, depth, None, **sizes)
    carried = project(*gather(late), weight, inverse, depth, carried, **sizes)
    out = temporal(*gather(final), weight, inverse, depth, carried, slot=slot, **sizes)
    out = out.reshape(frames * ways, slot, width)
    out = lax.all_to_all(out, ("frame", "row"), split_axis=0, concat_axis=0, tiled=True)
    out = out.reshape(frames, ways, slot, width).transpose(0, 2, 1, 3)
    return out.reshape(1, tokens, ways * width)


def solution(mesh):
    return jax.shard_map(
        local,
        mesh=mesh,
        in_specs=(
            P("frame", "row", None),
            P("frame", "row", None),
            P("frame", "row", None),
            P(),
            P(None, None, "row"),
        ),
        out_specs=P("frame", "row", None),
        check_vma=False,
    )
```

profile of v0, /device:TPU:1, one launch (start us, length us, event | category | flops | bytes accessed | tf_op | source)
XLA Modules:
  0.0 119.0 jit_solution(9515316866045183577)
XLA Ops:
  0.0 0.0 copy-start.1
  0.0 0.0 copy-start.3
  0.0 0.0 copy-start.5
  0.0 0.0 copy-start.7
  0.0 1.2 %constant_dynamic-slice_fusion.2 = (bf16[1,128,768]{2,1,0:T(8,128)(2,1)S(1)}, bf16[1,128,768]{2,1,0:T(8,128)(2,1)S(1)}) fusion(bf16[1,128,3072]{2,1,0:T(8,128)(2,1)} %q.3, s32[]{:T(128)S(6)} %select_n.5, s32[]{:T(128)S(6)} %select_n.4), kind=kLoop, calls=%fused_computation.5 | loop fusion | bytes 786440 | tf_op jit(solution)/shard_map/dynamic_slice | solution.py:332
  1.2 2.0 %constant_dynamic-slice_fusion = (bf16[1,128,768]{2,1,0:T(8,128)(2,1)S(1)}, bf16[1,128,768]{2,1,0:T(8,128)(2,1)S(1)}, bf16[1,128,768]{2,1,0:T(8,128)(2,1)}, bf16[1,128,768]{2,1,0:T(8,128)(2,1)S(1)}) fusion(bf16[1,128,3072]{2,1,0:T(8,128)(2,1)} %v.3, s32[]{:T(128)S(6)} %select_n.5, s32[]{:T(128)S(6)} %select_n.4, bf16[1,128,3072]{2,1,0:T(8,128)(2,1)} %k.3), kind=kLoop, calls=%fused_computation.3 | loop fusion | bytes 1572872 | tf_op jit(solution)/shard_map/dynamic_slice | solution.py:332
  3.2 0.9 pad_maximum_fusion.1
  4.1 2.0 %collective-permute-start.2 = (bf16[3,128,768]{2,1,0:T(8,128)(2,1)}, bf16[3,128,768]{2,1,0:T(8,128)(2,1)S(1)}, u32[]{:S(2)}, u32[]{:S(2)}) collective-permute-start(bf16[3,128,768]{2,1,0:T(8,128)(2,1)} %pad_maximum_fusion.1), channel_id=1, source_target_pairs={{0,1},{1,0},{2,3},{3,2},{4,5},{5,4},{6,7},{7,6},{8,9},{9,8},{10,11... | collective-permute-start | bytes 1769480 | tf_op jit(solution)/shard_map/ppermute | solution.py:324
  6.1 13.2 %collective-permute-done.2.rest_0_ = bf16[3,128,768]{2,1,0:T(8,128)(2,1)S(1)} collective-permute-done((bf16[3,128,768]{2,1,0:T(8,128)(2,1)}, bf16[3,128,768]{2,1,0:T(8,128)(2,1)S(1)}, u32[]{:S(2)}, u32[]{:S(2)}) %collective-permute-start.2) | collective-permute-done | bytes 589856 | tf_op jit(solution)/shard_map/ppermute | solution.py:324
  19.4 0.0 copy-start
  19.4 1.1 copy-done
  20.5 0.0 copy-start.2
  20.5 1.1 copy-done.2
  21.6 0.0 copy-start.4
  21.6 1.1 copy-done.4
  22.8 0.0 copy-start.6
  22.8 0.7 copy-done.6
  23.5 2.6 %spatial.3 = bf16[16,2,8,768]{3,2,1,0:T(8,128)(2,1)} custom-call(s32[1]{0:T(128)} %bitcast.11.base, bf16[1,128,3072]{2,1,0:T(8,128)(2,1)S(1)} %copy-done, bf16[1,128,3072]{2,1,0:T(8,128)(2,1)S(1)} %copy-done.2, bf16[1,128,3072]{2,1,0:T(8,128)(2,1)S(1)} %copy-done.4, bf16[3,128,768]{2,1,0:T(8,128)(2,1)S(1)} %collective-permute-done.2.rest_0_, ...), custom_call_target="tpu_custom_call" | custom-call | flops 251658240 | bytes 1966080 | tf_op jit(solution)/shard_map/spatial/pallas_call | solution.py:84
  26.0 7.3 %all-to-all-start.1 = ((bf16[16,2,8,768]{3,2,1,0:T(8,128)(2,1)}), bf16[16,2,8,768]{3,2,1,0:T(8,128)(2,1)S(1)}, u32[]{:S(2)}, u32[]{:S(2)}) async-start(bf16[16,2,8,768]{3,2,1,0:T(8,128)(2,1)} %spatial.3), calls=%async_computation.1 | async-start | bytes 786432 | tf_op jit(solution)/shard_map/all_to_all | solution.py:353
  33.4 1.8 %pad_maximum_fusion = bf16[3,128,768]{2,1,0:T(8,128)(2,1)} fusion(bf16[1,128,768]{2,1,0:T(8,128)(2,1)S(1)} %get-tuple-element.18, bf16[1,128,768]{2,1,0:T(8,128)(2,1)} %get-tuple-element.19, bf16[1,128,768]{2,1,0:T(8,128)(2,1)S(1)} %get-tuple-element.14), kind=kLoop, calls=%fused_computation | loop fusion | flops 589824 | bytes 1179648 | tf_op jit(solution)/shard_map/stack | solution.py:335
  35.2 1.2 %collective-permute-start = (bf16[3,128,768]{2,1,0:T(8,128)(2,1)}, bf16[3,128,768]{2,1,0:T(8,128)(2,1)S(1)}, u32[]{:S(2)}, u32[]{:S(2)}) collective-permute-start(bf16[3,128,768]{2,1,0:T(8,128)(2,1)} %pad_maximum_fusion), channel_id=1, source_target_pairs={{0,1},{1,0},{2,3},{3,2},{4,5},{5,4},{6,7},{7,6},{8,9},{9,8},{10,11... | collective-permute-start | bytes 1769480 | tf_op jit(solution)/shard_map/ppermute | solution.py:324
  36.4 13.8 %collective-permute-done.rest_0_ = bf16[3,128,768]{2,1,0:T(8,128)(2,1)S(1)} collective-permute-done((bf16[3,128,768]{2,1,0:T(8,128)(2,1)}, bf16[3,128,768]{2,1,0:T(8,128)(2,1)S(1)}, u32[]{:S(2)}, u32[]{:S(2)}) %collective-permute-start) | collective-permute-done | bytes 589856 | tf_op jit(solution)/shard_map/ppermute | solution.py:324
  50.2 0.0 copy-done.1
  50.2 0.0 copy-done.3
  50.2 0.0 copy-done.5
  50.2 0.0 copy-done.7
  50.2 2.6 %spatial.2 = bf16[16,2,8,768]{3,2,1,0:T(8,128)(2,1)} custom-call(s32[1]{0:T(128)} %bitcast.3.base, bf16[1,128,3072]{2,1,0:T(8,128)(2,1)S(1)} %copy-done.1, bf16[1,128,3072]{2,1,0:T(8,128)(2,1)S(1)} %copy-done.3, bf16[1,128,3072]{2,1,0:T(8,128)(2,1)S(1)} %copy-done.5, bf16[3,128,768]{2,1,0:T(8,128)(2,1)S(1)} %collective-permute-done.rest_0_, ...), custom_call_target="tpu_custom_call" | custom-call | flops 251658240 | bytes 1966080 | tf_op jit(solution)/shard_map/spatial/pallas_call | solution.py:84
  52.8 0.0 all-to-all-done.1.refs_0_
  52.8 6.6 %all-to-all-start = ((bf16[16,2,8,768]{3,2,1,0:T(8,128)(2,1)}), bf16[16,2,8,768]{3,2,1,0:T(8,128)(2,1)S(1)}, u32[]{:S(2)}, u32[]{:S(2)}) async-start(bf16[16,2,8,768]{3,2,1,0:T(8,128)(2,1)} %spatial.2), calls=%async_computation | async-start | bytes 786432 | tf_op jit(solution)/shard_map/all_to_all | solution.py:353
  59.4 0.1 stack.59.at
  59.4 0.1 add_add_fusion.1.at
  59.5 0.1 add_add_fusion.at
  59.6 1.2 %collective-permute-start.3 = (bf16[16,2,8,768]{3,2,1,0:T(8,128)(2,1)S(1)}, bf16[16,2,8,768]{3,2,1,0:T(8,128)(2,1)S(1)}, u32[]{:S(2)}, u32[]{:S(2)}) collective-permute-start(bf16[16,2,8,768]{3,2,1,0:T(8,128)(2,1)S(1)} %all-to-all-done.1.refs_0_), channel_id=1, source_target_pairs={{0,1},{1,0},{2,3},{3,2},{4,5},{5,4},{6,7},{7,6},{8,9},{9,8},{10,11... | collective-permute-start | bytes 1179656 | tf_op jit(solution)/shard_map/ppermute | solution.py:324
  60.8 10.4 %all-to-all-done.refs_1_ = bf16[16,2,8,768]{3,2,1,0:T(8,128)(2,1)S(1)} async-done(((bf16[16,2,8,768]{3,2,1,0:T(8,128)(2,1)}), bf16[16,2,8,768]{3,2,1,0:T(8,128)(2,1)S(1)}, u32[]{:S(2)}, u32[]{:S(2)}) %all-to-all-start) | async-done | bytes 393248 | tf_op jit(solution)/shard_map/all_to_all | solution.py:353
  71.2 1.2 %collective-permute-start.1 = (bf16[16,2,8,768]{3,2,1,0:T(8,128)(2,1)S(1)}, bf16[16,2,8,768]{3,2,1,0:T(8,128)(2,1)S(1)}, u32[]{:S(2)}, u32[]{:S(2)}) collective-permute-start(bf16[16,2,8,768]{3,2,1,0:T(8,128)(2,1)S(1)} %all-to-all-done.refs_1_), channel_id=1, source_target_pairs={{0,1},{1,0},{2,3},{3,2},{4,5},{5,4},{6,7},{7,6},{8,9},{9,8},{10,11... | collective-permute-start | bytes 1179656 | tf_op jit(solution)/shard_map/ppermute | solution.py:324
  72.4 5.8 %project.2 = (f32[3,256,1536]{2,1,0:T(8,128)S(1)}, f32[256,128]{1,0:T(8,128)S(1)}) custom-call(s32[3]{0:T(128)S(1)} %add_add_fusion.1.at, bf16[16,2,8,768]{3,2,1,0:T(8,128)(2,1)S(1)} %all-to-all-done.1.refs_0_, bf16[3,3072,1536]{2,1,0:T(8,128)(2,1)} %bitcast.27, f32[1,3072]{1,0:T(1,128)S(1)} %bitcast.21), custom_call_target="tpu_custom_call" | custom-call | flops 1811939328 | bytes 16515072 | tf_op jit(solution)/shard_map/project/pallas_call | solution.py:167
  78.2 0.0 collective-permute-done.3.refs_0_
  78.2 9.4 %project.3 = (f32[3,256,1536]{2,1,0:T(8,128)S(1)}, f32[256,128]{1,0:T(8,128)S(1)}) custom-call(s32[5]{0:T(128)S(1)} %stack.59.at, bf16[16,2,8,768]{3,2,1,0:T(8,128)(2,1)S(1)} %collective-permute-done.3.refs_0_, bf16[16,2,8,768]{3,2,1,0:T(8,128)(2,1)S(1)} %all-to-all-done.refs_1_, bf16[3,3072,1536]{2,1,0:T(8,128)(2,1)} %bitcast.28, f32[1,3072]{1,0:T(1,128)S(1)} %bitcast.22, ...), custom_call_target="tpu_custom_call" | custom-call | flops 3623878656 | bytes 23592960 | tf_op jit(solution)/shard_map/project/pallas_call | solution.py:167
  87.6 0.0 collective-permute-done.1.refs_0_
  87.6 6.9 %temporal.1 = bf16[16,2,8,1536]{3,2,1,0:T(8,128)(2,1)S(1)} custom-call(s32[3]{0:T(128)S(1)} %add_add_fusion.at, bf16[16,2,8,768]{3,2,1,0:T(8,128)(2,1)S(1)} %collective-permute-done.1.refs_0_, bf16[3,3072,1536]{2,1,0:T(8,128)(2,1)} %bitcast.29, bf16[3,3072,1536]{2,1,0:T(8,128)(2,1)} %bitcast.30, f32[1,3072]{1,0:T(1,128)S(1)} %bitcast.23, ...), custom_call_target="tpu_custom_call" | custom-call | flops 1811939328 | bytes 11796480 | tf_op jit(solution)/shard_map/temporal/pallas_call | solution.py:264
  94.5 23.6 %all_to_all.15 = bf16[32,8,1536]{2,1,0:T(8,128)(2,1)S(1)} all-to-all(bf16[32,8,1536]{2,1,0:T(8,128)(2,1)S(1)} %bitcast.20), channel_id=1, replica_groups=mesh['frame'=16,'row'=2] {'frame','row'}, dimensions={0} | all-to-all | bytes 1572864 | tf_op jit(solution)/shard_map/all_to_all | solution.py:383
  118.1 0.9 copy.7
  (1 shorter events, 0.0 us)
Async XLA Ops:
  0.0 50.2 %copy-start.1 = (bf16[1,128,3072]{2,1,0:T(8,128)(2,1)S(1)}, bf16[1,128,3072]{2,1,0:T(8,128)(2,1)}, u32[]{:S(2)}) copy-start(bf16[1,128,3072]{2,1,0:T(8,128)(2,1)} %q.3) | copy-start | bytes 2359300
  0.0 50.2 %copy-start.3 = (bf16[1,128,3072]{2,1,0:T(8,128)(2,1)S(1)}, bf16[1,128,3072]{2,1,0:T(8,128)(2,1)}, u32[]{:S(2)}) copy-start(bf16[1,128,3072]{2,1,0:T(8,128)(2,1)} %k.3) | copy-start | bytes 2359300
  0.0 50.2 %copy-start.5 = (bf16[1,128,3072]{2,1,0:T(8,128)(2,1)S(1)}, bf16[1,128,3072]{2,1,0:T(8,128)(2,1)}, u32[]{:S(2)}) copy-start(bf16[1,128,3072]{2,1,0:T(8,128)(2,1)} %v.3) | copy-start | bytes 2359300
  0.0 50.2 %copy-start.7 = (f32[3072]{0:T(1024)S(1)}, f32[3072]{0:T(1024)}, u32[]{:S(2)}) copy-start(f32[3072]{0:T(1024)} %param.8) | copy-start | bytes 36868
  4.1 15.3 %collective-permute-start.2 = (bf16[3,128,768]{2,1,0:T(8,128)(2,1)}, bf16[3,128,768]{2,1,0:T(8,128)(2,1)S(1)}, u32[]{:S(2)}, u32[]{:S(2)}) collective-permute-start(bf16[3,128,768]{2,1,0:T(8,128)(2,1)} %pad_maximum_fusion.1), channel_id=1, source_target_pairs={{0,1},{1,0},{2,3},{3,2},{4,5},{5,4},{6,7},{7,6},{8,9},{9,8},{10,11... | collective-permute-start | bytes 1769480 | tf_op jit(solution)/shard_map/ppermute | solution.py:324
  19.4 1.1 copy-start
  20.5 1.1 copy-start.2
  21.6 1.1 copy-start.4
  22.8 0.7 copy-start.6
  26.0 26.8 %all-to-all-start.1 = ((bf16[16,2,8,768]{3,2,1,0:T(8,128)(2,1)}), bf16[16,2,8,768]{3,2,1,0:T(8,128)(2,1)S(1)}, u32[]{:S(2)}, u32[]{:S(2)}) async-start(bf16[16,2,8,768]{3,2,1,0:T(8,128)(2,1)} %spatial.3), calls=%async_computation.1 | async-start | bytes 786432 | tf_op jit(solution)/shard_map/all_to_all | solution.py:353
  35.2 15.0 %collective-permute-start = (bf16[3,128,768]{2,1,0:T(8,128)(2,1)}, bf16[3,128,768]{2,1,0:T(8,128)(2,1)S(1)}, u32[]{:S(2)}, u32[]{:S(2)}) collective-permute-start(bf16[3,128,768]{2,1,0:T(8,128)(2,1)} %pad_maximum_fusion), channel_id=1, source_target_pairs={{0,1},{1,0},{2,3},{3,2},{4,5},{5,4},{6,7},{7,6},{8,9},{9,8},{10,11... | collective-permute-start | bytes 1769480 | tf_op jit(solution)/shard_map/ppermute | solution.py:324
  52.8 18.5 %all-to-all-start = ((bf16[16,2,8,768]{3,2,1,0:T(8,128)(2,1)}), bf16[16,2,8,768]{3,2,1,0:T(8,128)(2,1)S(1)}, u32[]{:S(2)}, u32[]{:S(2)}) async-start(bf16[16,2,8,768]{3,2,1,0:T(8,128)(2,1)} %spatial.2), calls=%async_computation | async-start | bytes 786432 | tf_op jit(solution)/shard_map/all_to_all | solution.py:353
  59.6 18.6 %collective-permute-start.3 = (bf16[16,2,8,768]{3,2,1,0:T(8,128)(2,1)S(1)}, bf16[16,2,8,768]{3,2,1,0:T(8,128)(2,1)S(1)}, u32[]{:S(2)}, u32[]{:S(2)}) collective-permute-start(bf16[16,2,8,768]{3,2,1,0:T(8,128)(2,1)S(1)} %all-to-all-done.1.refs_0_), channel_id=1, source_target_pairs={{0,1},{1,0},{2,3},{3,2},{4,5},{5,4},{6,7},{7,6},{8,9},{9,8},{10,11... | collective-permute-start | bytes 1179656 | tf_op jit(solution)/shard_map/ppermute | solution.py:324
  71.2 16.4 %collective-permute-start.1 = (bf16[16,2,8,768]{3,2,1,0:T(8,128)(2,1)S(1)}, bf16[16,2,8,768]{3,2,1,0:T(8,128)(2,1)S(1)}, u32[]{:S(2)}, u32[]{:S(2)}) collective-permute-start(bf16[16,2,8,768]{3,2,1,0:T(8,128)(2,1)S(1)} %all-to-all-done.refs_1_), channel_id=1, source_target_pairs={{0,1},{1,0},{2,3},{3,2},{4,5},{5,4},{6,7},{7,6},{8,9},{9,8},{10,11... | collective-permute-start | bytes 1179656 | tf_op jit(solution)/shard_map/ppermute | solution.py:324
where the time goes:
time: 120 us; the launch traced here: 119 us
  waiting for transfers between devices  37.4 us (31%)
  Pallas kernels  27.2 us (23%)
  blocking collectives  23.6 us (20%)
  starting transfers between devices  19.6 us (16%)
  local copies, waits for them, and re-layouts  8.24 us (7%)
  other arithmetic  2.84 us (2%)
    ppermute x4, waiting for transfers between devices, shift(): return lax.ppermute(x, 'row', [(i, (i + k) % ways) for i in range(ways)])  27 us
    all_to_all x1, blocking collectives, local(): lax.all_to_all(out, ('frame', 'row'), split_axis=0, concat_axis=0, tiled=...  23.6 us
    pallas_call x2, Pallas kernels, project(): pl.pallas_call(partial(project_kernel, pieces=pieces, arrays=len(arrays),...  15.2 us
    all_to_all x2, starting transfers between devices, local(): lax.all_to_all(out, 'frame', split_axis=0, concat_axis=0, tiled=True)  13.9 us
    all_to_all x2, waiting for transfers between devices, local(): lax.all_to_all(out, 'frame', split_axis=0, concat_axis=0, tiled=True)  10.4 us
    pallas_call x1, Pallas kernels, temporal(): pl.pallas_call(partial(temporal_kernel, count=count, heads=heads, tokens=...  6.89 us
    ppermute x4, starting transfers between devices, shift(): return lax.ppermute(x, 'row', [(i, (i + k) % ways) for i in range(ways)])  5.67 us
    pallas_call x2, Pallas kernels, spatial(): pl.pallas_call(partial(spatial_kernel, heads=heads, pool=pool, tiled=tile...  5.14 us
  transfers between devices with their start and end apart: 6, of which 3 were waited for; matrix products, arithmetic and copies ran while one was open for 2% of the time, Pallas kernels for 15%

commit v1 on v0

--- a/solution.py
+++ b/solution.py
@@ -151,14 +151,14 @@
             acc[c, :, cols] += dot(held[...], w[c, :, cols])
 
 
-def project(pieces, arrays, at, weight, inverse, depth, carried, tokens, ways, tiled):
+def project(pieces, arrays, at, place, weight, inverse, depth, carried, tokens, ways, tiled):
     rows = tokens * ways
     width = weight.shape[2]
     whole = lambda shape: pl.BlockSpec(shape, lambda i, at: (0,) * len(shape))
     acc_shape, ss_shape = (3, rows, width), (rows, HEAD)
     in_specs = [whole(x.shape) for x in arrays] + [
-        pl.BlockSpec((3, depth, width), lambda i, at: (0, at[i], 0)),
-        pl.BlockSpec((1, depth), lambda i, at: (0, at[i])),
+        pl.BlockSpec((3, depth, width), lambda i, at: (0, at[place[0] + i * place[1]], 0)),
+        pl.BlockSpec((1, depth), lambda i, at: (0, at[place[0] + i * place[1]])),
     ]
     operands = list(arrays) + [weight, inverse]
     if carried is not None:
@@ -189,6 +189,9 @@
             flops=6 * rows * depth * len(pieces) * width,
             bytes_accessed=6 * depth * len(pieces) * width + 8 * 3 * rows * width,
             transcendentals=0,
+        ),
+        input_output_aliases=(
+            {} if carried is None else {len(arrays) + 3: 0, len(arrays) + 4: 1}
         ),
         compiler_params=pltpu.CompilerParams(vmem_limit_bytes=32 << 20),
         name="project",
@@ -235,7 +238,7 @@
         for _, rows, cols in split
     ]
     weights = [weighted(x) for x in scores]
-    me = at[count]
+    me = at[at.shape[0] - 1]
     for (j, rows, cols), (w, r) in zip(split, weights):
         result = dot((w * r).astype(jnp.bfloat16), qkv[2][rows, cols]).astype(jnp.bfloat16)
         target = lax.rem(me + ways - j, ways)
@@ -245,7 +248,7 @@
             out[target, :, cols] = result
 
 
-def temporal(pieces, arrays, at, weight, inverse, depth, carried, tokens, ways, slot, tiled):
+def temporal(pieces, arrays, at, place, weight, inverse, depth, carried, tokens, ways, slot, tiled):
     rows = tokens * ways
     width = weight.shape[2]
     count = len(pieces)
@@ -259,8 +262,8 @@
         shape = (ways, tokens, width)
         out_spec = pl.BlockSpec((ways, tokens, step), lambda n, at: (0, 0, n))
     whole = lambda shape: pl.BlockSpec(shape, lambda n, at: (0,) * len(shape))
-    at_piece = lambda i: pl.BlockSpec((3, depth, step), lambda n, at: (0, at[i], n))
-    gain_piece = lambda i: pl.BlockSpec((1, depth), lambda n, at: (0, at[i]))
+    at_piece = lambda i: pl.BlockSpec((3, depth, step), lambda n, at: (0, at[place[0] + i * place[1]], n))
+    gain_piece = lambda i: pl.BlockSpec((1, depth), lambda n, at: (0, at[place[0] + i * place[1]]))
     out = pl.pallas_call(
         partial(
             temporal_kernel,
@@ -303,6 +306,45 @@
     return out
 
 
+def pack_kernel(at, q, k, v, out):
+    for i, ref in enumerate((q, k, v)):
+        out[i] = ref[0]
+
+
+def pack(q, k, v, at, width):
+    tokens = q.shape[1]
+    count = at.shape[0]
+    return pl.pallas_call(
+        pack_kernel,
+        out_shape=jax.ShapeDtypeStruct((3, tokens, count * width), q.dtype),
+        grid_spec=pltpu.PrefetchScalarGridSpec(
+            num_scalar_prefetch=1,
+            grid=(count,),
+            in_specs=[pl.BlockSpec((1, tokens, width), lambda i, at: (0, 0, at[i]))] * 3,
+            out_specs=pl.BlockSpec((3, tokens, width), lambda i, at: (0, 0, i)),
+        ),
+        compiler_params=pltpu.CompilerParams(vmem_limit_bytes=8 << 20),
+        name="pack",
+    )(at, q, k, v)
+
+
+def split_kernel(moved, *outs):
+    for n, out in enumerate(outs):
+        out[...] = moved[..., n * out.shape[-1] : (n + 1) * out.shape[-1]]
+
+
+def split(moved, count):
+    if count == 1:
+        return (moved,)
+    shape = moved.shape[:-1] + (moved.shape[-1] // count,)
+    return pl.pallas_call(
+        split_kernel,
+        out_shape=(jax.ShapeDtypeStruct(shape, moved.dtype),) * count,
+        compiler_params=pltpu.CompilerParams(vmem_limit_bytes=8 << 20),
+        name="split",
+    )(moved)
+
+
 def local(spatial_q, spatial_k, spatial_v, norm_gain, temporal_weight):
     frames = lax.axis_size("frame")
     ways = lax.axis_size("row")
@@ -312,77 +354,81 @@
     tiled = slot % 8 == 0
     width = temporal_weight.shape[2]
     group = width // HEAD
-    unit = group // 4 if group % 4 == 0 else 1
-    depth = unit * HEAD
-    units = group // unit
-    chunks = (range(0, units - units // 2), range(units - units // 2, units))
+    count = chunk_count(group)
+    heads = group // count
+    depth = heads * HEAD
     weight = jnp.transpose(temporal_weight, (1, 0, 2))
+    spatial_q, spatial_k, spatial_v = (
+        pltpu.with_memory_space_constraint(x, pltpu.HBM) for x in (spatial_q, spatial_k, spatial_v)
+    )
     gain = norm_gain.reshape(1, -1)
     inverse = 1.0 / gain
 
     def shift(x, k):
         return lax.ppermute(x, "row", [(i, (i + k) % ways) for i in range(ways)])
 
+    chunks = [c for c in (range(0, 1), range(1, count)) if c]
     received = []
     for chunk in chunks:
         parts = []
         for k in range(1, ways):
-            column = lax.rem(me + k, ways) * width + chunk[0] * depth
-            stack = [
-                lax.dynamic_slice_in_dim(x[0], column, len(chunk) * depth, axis=1)
-                for x in (spatial_q, spatial_k, spatial_v)
-            ]
-            parts.append(shift(jnp.stack(stack), k))
+            at = lax.rem(me + k, ways) * count + jnp.arange(chunk[0], chunk[-1] + 1)
+            packed = pack(spatial_q, spatial_k, spatial_v, at.astype(jnp.int32), depth)
+            parts.append(shift(packed, k))
         received.append(parts)
 
     pieces = {}
     for chunk, parts in zip(chunks, received):
-        base = (me * group + chunk[0] * unit).reshape(1)
-        heads = math.gcd(group, chunk[0] * unit, len(chunk) * unit)
+        base = (me * group + chunk[0] * heads).reshape(1)
+        span = len(chunk) * depth
         out = spatial(
-            spatial_q,
-            spatial_k,
-            spatial_v,
-            parts,
-            gain,
-            base,
-            frames,
-            len(chunk) * depth,
-            min(heads, unit),
+            spatial_q, spatial_k, spatial_v, parts, gain, base, frames, span, heads
         )
         moved = lax.all_to_all(out, "frame", split_axis=0, concat_axis=0, tiled=True)
-        for n, u in enumerate(chunk):
-            pieces[u, 0] = (moved, n * depth)
-        for k in range(1, ways):
-            shared = shift(moved, k)
-            for n, u in enumerate(chunk):
-                pieces[u, k] = (shared, n * depth)
+        for u, part in zip(chunk, split(moved, len(chunk))):
+            pieces[u, 0] = (part, 0)
+            for k in range(1, ways):
+                pieces[u, k] = (shift(part, k), 0)
+
+    table = [lax.rem(me + ways - k, ways) * count + u for k in range(ways) for u in range(count)]
+    table = jnp.stack(table + [me])
 
     def gather(wanted):
-        listed, arrays, at = [], [], []
+        listed, arrays = [], []
         for u, k in wanted:
             array, column = pieces[u, k]
-            where = [i for i, x in enumerate(arrays) if x is array]
+            where = [n for n, x in enumerate(arrays) if x is array]
             if not where:
                 where = [len(arrays)]
                 arrays.append(array)
             listed.append((where[0], column, k))
-            at.append(lax.rem(me + ways - k, ways) * units + u)
         if not tiled:
             arrays = [x.transpose(1, 0, 2, 3).reshape(ways, tokens, -1) for x in arrays]
-        return tuple(listed), arrays, jnp.stack(at + [me])
-
+        at = [k * count + u for u, k in wanted]
+        stride = at[1] - at[0] if len(at) > 1 else 0
+        assert at == [at[0] + n * stride for n in range(len(at))]
+        return tuple(listed), arrays, table, (at[0], stride)
+
+    own = lambda units: [(u, 0) for u in units]
+    other = lambda units: [(u, k) for u in units for k in range(1, ways)]
+    last = count - 1
+    steps = [own(chunks[0]) + other(u for u in chunks[0] if u < last)]
+    steps += [own(chunk) for chunk in chunks[1:]]
+    steps += [other([u]) for u in range(1, last)]
     sizes = dict(tokens=tokens, ways=ways, tiled=tiled)
-    early = [(u, 0) for u in chunks[0]]
-    late = [(u, k) for k in range(1, ways) for u in chunks[0]] + [(u, 0) for u in chunks[1]]
-    final = [(u, k) for k in range(1, ways) for u in chunks[1]]
-    carried = project(*gather(early), weight, inverse, depth, None, **sizes)
-    carried = project(*gather(late), weight, inverse, depth, carried, **sizes)
-    out = temporal(*gather(final), weight, inverse, depth, carried, slot=slot, **sizes)
+    carried = None
+    for wanted in steps:
+        carried = project(*gather(wanted), weight, inverse, depth, carried, **sizes)
+    final = gather(other([last]))
+    out = temporal(*final, weight, inverse, depth, carried, slot=slot, **sizes)
     out = out.reshape(frames * ways, slot, width)
     out = lax.all_to_all(out, ("frame", "row"), split_axis=0, concat_axis=0, tiled=True)
     out = out.reshape(frames, ways, slot, width).transpose(0, 2, 1, 3)
     return out.reshape(1, tokens, ways * width)
+
+
+def chunk_count(group):
+    return 3 if group % 3 == 0 else math.gcd(group, 2)
 
 
 def solution(mesh):

time: 120 us -> 105 us (0.88)
  waiting for transfers between devices: 37.4 us -> 25.4 us
  local copies, waits for them, and re-layouts: 8.24 us -> 0.97 us
  Pallas kernels: 27.2 us -> 31.7 us
  other arithmetic: 2.84 us -> 0.01 us
  blocking collectives: 23.6 us -> 25.5 us
    ppermute x4 -> x5, waiting for transfers between devices: 27 us -> 12.6 us  [shift(): return lax.ppermute(x, 'row', [(i, (i + k) % ways) for i in range(ways)])]
    unnamed x17 -> x3, local copies, waits for them, and re-layouts: 5 us -> 0.88 us
    dynamic_slice x2 -> x0, local copies, waits for them, and re-layouts: 3.16 us -> none  [local(): lax.dynamic_slice_in_dim(x[0], column, len(chunk) * depth, axis=1)]
    pallas_call x0 -> x3, Pallas kernels: none -> 2.99 us  [the longest x2 2.95 us: pack(): pl.pallas_call(pack_kernel, out_shape=jax.ShapeDtypeStruct((3, tokens, co...]
    another operation x4 -> x0, other arithmetic: 2.84 us -> none  [the longest x2 2.69 us: local(): parts.append(shift(jnp.stack(stack), k))]
    all_to_all x2, waiting for transfers between devices: 10.4 us -> 12.9 us  [local(): lax.all_to_all(out, 'frame', split_axis=0, concat_axis=0, tiled=True)]
    pallas_call x2 -> x3, Pallas kernels: 15.2 us -> 17.1 us  [project(): pl.pallas_call(partial(project_kernel, pieces=pieces, arrays=len(arrays),...]
    all_to_all x1, blocking collectives: 23.6 us -> 25.5 us  [local(): lax.all_to_all(out, ('frame', 'row'), split_axis=0, concat_axis=0, tiled=...]
  transfers between devices with their start and end apart: 6 -> 7, of which waited for: 3 -> 4; matrix products, arithmetic and copies ran while one was open for 2% -> 0% of each run, Pallas kernels for 15% -> 24%
where the time goes in v1:
time: 105 us; the launch traced here: 104 us
  Pallas kernels  31.7 us (30%)
  blocking collectives  25.5 us (24%)
  waiting for transfers between devices  25.4 us (24%)
  starting transfers between devices  20.6 us (20%)
    all_to_all x1, blocking collectives, local(): lax.all_to_all(out, ('frame', 'row'), split_axis=0, concat_axis=0, tiled=...  25.5 us
    pallas_call x3, Pallas kernels, project(): pl.pallas_call(partial(project_kernel, pieces=pieces, arrays=len(arrays),...  17.1 us
    all_to_all x2, starting transfers between devices, local(): lax.all_to_all(out, 'frame', split_axis=0, concat_axis=0, tiled=True)  15.7 us
    all_to_all x2, waiting for transfers between devices, local(): lax.all_to_all(out, 'frame', split_axis=0, concat_axis=0, tiled=True)  12.9 us
    ppermute x5, waiting for transfers between devices, shift(): return lax.ppermute(x, 'row', [(i, (i + k) % ways) for i in range(ways)])  12.6 us
    pallas_call x2, Pallas kernels, spatial(): pl.pallas_call(partial(spatial_kernel, heads=heads, pool=pool, tiled=tile...  6.25 us
    pallas_call x1, Pallas kernels, temporal(): pl.pallas_call(partial(temporal_kernel, count=count, heads=heads, tokens=...  5.4 us
    ppermute x5, starting transfers between devices, shift(): return lax.ppermute(x, 'row', [(i, (i + k) % ways) for i in range(ways)])  4.99 us
  transfers between devices with their start and end apart: 7, of which 4 were waited for; matrix products, arithmetic and copies ran while one was open for 0% of the time, Pallas kernels for 24%

profile of v1, /device:TPU:1, one launch (start us, length us, event | category | flops | bytes accessed | tf_op | source)
XLA Modules:
  0.0 104.4 jit_solution(6383007339856729974)
XLA Ops:
  0.0 0.0 copy-start
  0.0 1.1 %pack.3 = bf16[3,128,512]{2,1,0:T(8,128)(2,1)S(1)} custom-call(s32[1]{0:T(128)} %bitcast.3.at, bf16[1,128,3072]{2,1,0:T(8,128)(2,1)} %q.7, bf16[1,128,3072]{2,1,0:T(8,128)(2,1)} %k.7, bf16[1,128,3072]{2,1,0:T(8,128)(2,1)} %v.7), custom_call_target="tpu_custom_call" | custom-call | tf_op jit(solution)/shard_map/pack/pallas_call | solution.py:317
  1.1 2.1 %collective-permute-start.3 = (bf16[3,128,512]{2,1,0:T(8,128)(2,1)S(1)}, bf16[3,128,512]{2,1,0:T(8,128)(2,1)S(1)}, u32[]{:S(2)}, u32[]{:S(2)}) collective-permute-start(bf16[3,128,512]{2,1,0:T(8,128)(2,1)S(1)} %pack.3), channel_id=1, source_target_pairs={{0,1},{1,0},{2,3},{3,2},{4,5},{5,4},{6,7},{7,6},{8,9},{9,8},{10,11... | collective-permute-start | bytes 1179656 | tf_op jit(solution)/shard_map/ppermute | solution.py:368
  3.2 1.9 %pack.2 = bf16[3,128,1024]{2,1,0:T(8,128)(2,1)S(1)} custom-call(s32[2]{0:T(128)S(1)} %add_add_fusion.at, bf16[1,128,3072]{2,1,0:T(8,128)(2,1)} %q.7, bf16[1,128,3072]{2,1,0:T(8,128)(2,1)} %k.7, bf16[1,128,3072]{2,1,0:T(8,128)(2,1)} %v.7), custom_call_target="tpu_custom_call" | custom-call | tf_op jit(solution)/shard_map/pack/pallas_call | solution.py:317
  5.1 0.1 collective-permute-start
  5.2 6.8 %collective-permute-done.3.rest_0_ = bf16[3,128,512]{2,1,0:T(8,128)(2,1)S(1)} collective-permute-done((bf16[3,128,512]{2,1,0:T(8,128)(2,1)S(1)}, bf16[3,128,512]{2,1,0:T(8,128)(2,1)S(1)}, u32[]{:S(2)}, u32[]{:S(2)}) %collective-permute-start.3) | collective-permute-done | bytes 393248 | tf_op jit(solution)/shard_map/ppermute | solution.py:368
  12.0 0.0 copy-done
  12.0 2.6 %spatial.3 = bf16[16,2,8,512]{3,2,1,0:T(8,128)(2,1)} custom-call(s32[1]{0:T(128)} %bitcast.11.base, bf16[1,128,3072]{2,1,0:T(8,128)(2,1)} %q.7, bf16[1,128,3072]{2,1,0:T(8,128)(2,1)} %k.7, bf16[1,128,3072]{2,1,0:T(8,128)(2,1)} %v.7, bf16[3,128,512]{2,1,0:T(8,128)(2,1)S(1)} %collective-permute-done.3.rest_0_, f32[1,3072]{1,0:T(1,128)S(1)} %bitcast.23), custom_call_target="tpu_custom_call" | custom-call | flops 167772160 | bytes 1310720 | tf_op jit(solution)/shard_map/spatial/pallas_call | solution.py:84
  14.6 8.5 %all-to-all-start.1 = ((bf16[16,2,8,512]{3,2,1,0:T(8,128)(2,1)}), bf16[16,2,8,512]{3,2,1,0:T(8,128)(2,1)S(1)}, u32[]{:S(2)}, u32[]{:S(2)}) async-start(bf16[16,2,8,512]{3,2,1,0:T(8,128)(2,1)} %spatial.3), calls=%async_computation.1 | async-start | bytes 524288 | tf_op jit(solution)/shard_map/all_to_all | solution.py:387
  23.1 5.7 %collective-permute-done.rest_0_ = bf16[3,128,1024]{2,1,0:T(8,128)(2,1)S(1)} collective-permute-done((bf16[3,128,1024]{2,1,0:T(8,128)(2,1)S(1)}, bf16[3,128,1024]{2,1,0:T(8,128)(2,1)S(1)}, u32[]{:S(2)}, u32[]{:S(2)}) %collective-permute-start) | collective-permute-done | bytes 786464 | tf_op jit(solution)/shard_map/ppermute | solution.py:368
  28.8 3.6 %spatial.2 = bf16[16,2,8,1024]{3,2,1,0:T(8,128)(2,1)} custom-call(s32[1]{0:T(128)} %bitcast.7.base, bf16[1,128,3072]{2,1,0:T(8,128)(2,1)} %q.7, bf16[1,128,3072]{2,1,0:T(8,128)(2,1)} %k.7, bf16[1,128,3072]{2,1,0:T(8,128)(2,1)} %v.7, bf16[3,128,1024]{2,1,0:T(8,128)(2,1)S(1)} %collective-permute-done.rest_0_, f32[1,3072]{1,0:T(1,128)S(1)} %bitcast.24), custom_call_target="tpu_custom_call" | custom-call | flops 335544320 | bytes 2621440 | tf_op jit(solution)/shard_map/spatial/pallas_call | solution.py:84
  32.5 0.2 all-to-all-done.1.refs_0_
  32.6 7.2 %all-to-all-start = ((bf16[16,2,8,1024]{3,2,1,0:T(8,128)(2,1)}), bf16[16,2,8,1024]{3,2,1,0:T(8,128)(2,1)S(1)}, u32[]{:S(2)}, u32[]{:S(2)}) async-start(bf16[16,2,8,1024]{3,2,1,0:T(8,128)(2,1)} %spatial.2), calls=%async_computation | async-start | bytes 1048576 | tf_op jit(solution)/shard_map/all_to_all | solution.py:387
  39.8 1.2 %collective-permute-start.4 = (bf16[16,2,8,512]{3,2,1,0:T(8,128)(2,1)S(1)}, bf16[16,2,8,512]{3,2,1,0:T(8,128)(2,1)S(1)}, u32[]{:S(2)}, u32[]{:S(2)}) collective-permute-start(bf16[16,2,8,512]{3,2,1,0:T(8,128)(2,1)S(1)} %all-to-all-done.1.refs_0_), channel_id=1, source_target_pairs={{0,1},{1,0},{2,3},{3,2},{4,5},{5,4},{6,7},{7,6},{8,9},{9,8},{10,11... | collective-permute-start | bytes 786440 | tf_op jit(solution)/shard_map/ppermute | solution.py:368
  41.0 0.1 stack.31.at
  41.1 12.7 %all-to-all-done.moved = bf16[16,2,8,1024]{3,2,1,0:T(8,128)(2,1)S(1)} async-done(((bf16[16,2,8,1024]{3,2,1,0:T(8,128)(2,1)}), bf16[16,2,8,1024]{3,2,1,0:T(8,128)(2,1)S(1)}, u32[]{:S(2)}, u32[]{:S(2)}) %all-to-all-start) | async-done | bytes 524320 | tf_op jit(solution)/shard_map/all_to_all | solution.py:387
  53.8 1.3 %collective-permute-start.2 = (bf16[16,2,8,512]{3,2,1,0:T(8,128)(2,1)S(1)}, bf16[16,2,8,512]{3,2,1,0:T(8,128)(2,1)S(1)}, u32[]{:S(2)}, u32[]{:S(2)}) collective-permute-start(bf16[16,2,8,512]{3,2,1,0:T(8,128)(2,1)S(1)} %get-tuple-element.14.refs_0_), channel_id=1, source_target_pairs={{0,1},{1,0},{2,3},{3,2},{4,5},{5,4},{6,7},{7,6},{8,9},{9,8},{10,11... | collective-permute-start | bytes 786440 | tf_op jit(solution)/shard_map/ppermute | solution.py:368
  55.1 0.0 collective-permute-done.4.refs_1_
  55.1 6.2 %project.3 = (f32[3,256,1536]{2,1,0:T(8,128)S(1)}, f32[256,128]{1,0:T(8,128)S(1)}) custom-call(s32[7]{0:T(128)S(1)} %stack.31.at, bf16[16,2,8,512]{3,2,1,0:T(8,128)(2,1)S(1)} %all-to-all-done.1.refs_0_, bf16[16,2,8,512]{3,2,1,0:T(8,128)(2,1)S(1)} %collective-permute-done.4.refs_1_, bf16[3,3072,1536]{2,1,0:T(8,128)(2,1)} %bitcast.25, f32[1,3072]{1,0:T(1,128)S(1)} %bitcast.19), custom_call_target="tpu_custom_call" | custom-call | flops 2415919104 | bytes 18874368 | tf_op jit(solution)/shard_map/project/pallas_call | solution.py:167
  61.3 0.3 collective-permute-start.1
  61.6 6.5 %project.4 = (f32[3,256,1536]{2,1,0:T(8,128)S(1)}, f32[256,128]{1,0:T(8,128)S(1)}) custom-call(s32[7]{0:T(128)S(1)} %stack.31.at, bf16[16,2,8,512]{3,2,1,0:T(8,128)(2,1)S(1)} %get-tuple-element.14.refs_0_, bf16[16,2,8,512]{3,2,1,0:T(8,128)(2,1)S(1)} %get-tuple-element.13.refs_1_, ...), custom_call_target="tpu_custom_call", output_to_operand_aliasing={{0}: (5, {}), {1}: (6, {})} | custom-call | flops 2415919104 | bytes 18874368 | tf_op jit(solution)/shard_map/project/pallas_call | solution.py:167
  68.1 0.0 collective-permute-done.2.refs_0_
  68.1 4.5 %project.5 = (f32[3,256,1536]{2,1,0:T(8,128)S(1)}, f32[256,128]{1,0:T(8,128)S(1)}) custom-call(s32[7]{0:T(128)S(1)} %stack.31.at, bf16[16,2,8,512]{3,2,1,0:T(8,128)(2,1)S(1)} %collective-permute-done.2.refs_0_, bf16[3,3072,1536]{2,1,0:T(8,128)(2,1)} %bitcast.27, f32[1,3072]{1,0:T(1,128)S(1)} %bitcast.21, ...), custom_call_target="tpu_custom_call", output_to_operand_aliasing={{0}: (4, {}), {1}: (5, {})} | custom-call | flops 1207959552 | bytes 14155776 | tf_op jit(solution)/shard_map/project/pallas_call | solution.py:167
  72.6 0.0 collective-permute-done.1.refs_0_
  72.6 5.4 %temporal.1 = bf16[16,2,8,1536]{3,2,1,0:T(8,128)(2,1)S(1)} custom-call(s32[7]{0:T(128)S(1)} %stack.31.at, bf16[16,2,8,512]{3,2,1,0:T(8,128)(2,1)S(1)} %collective-permute-done.1.refs_0_, bf16[3,3072,1536]{2,1,0:T(8,128)(2,1)} %bitcast.28, f32[1,3072]{1,0:T(1,128)S(1)} %bitcast.22, f32[3,256,1536]{2,1,0:T(8,128)S(1)} %get-tuple-element.19.refs_3_, ...), custom_call_target="tpu_custom_call" | custom-call | flops 1207959552 | bytes 9437184 | tf_op jit(solution)/shard_map/temporal/pallas_call | solution.py:267
  78.0 25.5 %all_to_all.15 = bf16[32,8,1536]{2,1,0:T(8,128)(2,1)S(1)} all-to-all(bf16[32,8,1536]{2,1,0:T(8,128)(2,1)S(1)} %bitcast.18), channel_id=1, replica_groups=mesh['frame'=16,'row'=2] {'frame','row'}, dimensions={0} | all-to-all | bytes 1572864 | tf_op jit(solution)/shard_map/all_to_all | solution.py:425
  103.5 0.9 copy.15
  (3 shorter events, 0.0 us)
Async XLA Ops:
  0.0 12.0 %copy-start = (f32[3072]{0:T(1024)S(1)}, f32[3072]{0:T(1024)}, u32[]{:S(2)}) copy-start(f32[3072]{0:T(1024)} %param.8) | copy-start | bytes 36868
  1.1 10.9 %collective-permute-start.3 = (bf16[3,128,512]{2,1,0:T(8,128)(2,1)S(1)}, bf16[3,128,512]{2,1,0:T(8,128)(2,1)S(1)}, u32[]{:S(2)}, u32[]{:S(2)}) collective-permute-start(bf16[3,128,512]{2,1,0:T(8,128)(2,1)S(1)} %pack.3), channel_id=1, source_target_pairs={{0,1},{1,0},{2,3},{3,2},{4,5},{5,4},{6,7},{7,6},{8,9},{9,8},{10,11... | collective-permute-start | bytes 1179656 | tf_op jit(solution)/shard_map/ppermute | solution.py:368
  5.1 23.8 %collective-permute-start = (bf16[3,128,1024]{2,1,0:T(8,128)(2,1)S(1)}, bf16[3,128,1024]{2,1,0:T(8,128)(2,1)S(1)}, u32[]{:S(2)}, u32[]{:S(2)}) collective-permute-start(bf16[3,128,1024]{2,1,0:T(8,128)(2,1)S(1)} %pack.2), channel_id=1, source_target_pairs={{0,1},{1,0},{2,3},{3,2},{4,5},{5,4},{6,7},{7,6},{8,9},{9,8},{10,11... | collective-permute-start | bytes 2359304 | tf_op jit(solution)/shard_map/ppermute | solution.py:368
  14.6 18.0 %all-to-all-start.1 = ((bf16[16,2,8,512]{3,2,1,0:T(8,128)(2,1)}), bf16[16,2,8,512]{3,2,1,0:T(8,128)(2,1)S(1)}, u32[]{:S(2)}, u32[]{:S(2)}) async-start(bf16[16,2,8,512]{3,2,1,0:T(8,128)(2,1)} %spatial.3), calls=%async_computation.1 | async-start | bytes 524288 | tf_op jit(solution)/shard_map/all_to_all | solution.py:387
  32.6 21.2 %all-to-all-start = ((bf16[16,2,8,1024]{3,2,1,0:T(8,128)(2,1)}), bf16[16,2,8,1024]{3,2,1,0:T(8,128)(2,1)S(1)}, u32[]{:S(2)}, u32[]{:S(2)}) async-start(bf16[16,2,8,1024]{3,2,1,0:T(8,128)(2,1)} %spatial.2), calls=%async_computation | async-start | bytes 1048576 | tf_op jit(solution)/shard_map/all_to_all | solution.py:387
  39.8 15.3 %collective-permute-start.4 = (bf16[16,2,8,512]{3,2,1,0:T(8,128)(2,1)S(1)}, bf16[16,2,8,512]{3,2,1,0:T(8,128)(2,1)S(1)}, u32[]{:S(2)}, u32[]{:S(2)}) collective-permute-start(bf16[16,2,8,512]{3,2,1,0:T(8,128)(2,1)S(1)} %all-to-all-done.1.refs_0_), channel_id=1, source_target_pairs={{0,1},{1,0},{2,3},{3,2},{4,5},{5,4},{6,7},{7,6},{8,9},{9,8},{10,11... | collective-permute-start | bytes 786440 | tf_op jit(solution)/shard_map/ppermute | solution.py:368
  53.8 14.2 %collective-permute-start.2 = (bf16[16,2,8,512]{3,2,1,0:T(8,128)(2,1)S(1)}, bf16[16,2,8,512]{3,2,1,0:T(8,128)(2,1)S(1)}, u32[]{:S(2)}, u32[]{:S(2)}) collective-permute-start(bf16[16,2,8,512]{3,2,1,0:T(8,128)(2,1)S(1)} %get-tuple-element.14.refs_0_), channel_id=1, source_target_pairs={{0,1},{1,0},{2,3},{3,2},{4,5},{5,4},{6,7},{7,6},{8,9},{9,8},{10,11... | collective-permute-start | bytes 786440 | tf_op jit(solution)/shard_map/ppermute | solution.py:368
  61.3 11.3 %collective-permute-start.1 = (bf16[16,2,8,512]{3,2,1,0:T(8,128)(2,1)S(1)}, bf16[16,2,8,512]{3,2,1,0:T(8,128)(2,1)S(1)}, u32[]{:S(2)}, u32[]{:S(2)}) collective-permute-start(bf16[16,2,8,512]{3,2,1,0:T(8,128)(2,1)S(1)} %get-tuple-element.13.refs_1_), channel_id=1, source_target_pairs={{0,1},{1,0},{2,3},{3,2},{4,5},{5,4},{6,7},{7,6},{8,9},{9,8},{10,11... | collective-permute-start | bytes 786440 | tf_op jit(solution)/shard_map/ppermute | solution.py:368

commit v2 on v1

--- a/solution.py
+++ b/solution.py
@@ -127,42 +127,58 @@
     else:
         w, inverse, acc_in, ss_in, acc, ss, held = refs[arrays:]
     depth = held.shape[1]
-    step = pl.program_id(0)
+    step, c = pl.program_id(0), pl.program_id(1)
     for i, (which, col, shift) in enumerate(pieces):
 
-        @pl.when(step == i)
+        @pl.when((step == i) & (c == 0))
         def _():
             for j in range(ways):
                 held[j * tokens : (j + 1) * tokens, :] = rows_of(
                     xs[which], (j - shift) % ways, slice(col, col + depth), tokens, tiled
                 )
-
-    @pl.when(step == 0)
-    def _():
-        acc[...] = jnp.zeros_like(acc) if first else acc_in[...]
-        ss[...] = jnp.zeros_like(ss) if first else ss_in[...]
-
-    ss[...] += squares(held[...], inverse[...])
+            before = ss[...] if i else (jnp.zeros_like(ss) if first else ss_in[...])
+            ss[...] = before + squares(held[...], inverse[...])
+
     width = w.shape[2]
     tile = width // 3 if width % 3 == 0 else width
-    for c in range(3):
+    if first:
+
+        @pl.when(step == 0)
+        def _():
+            for n in range(0, width, tile):
+                cols = slice(n, n + tile)
+                acc[c, :, cols] = dot(held[...], w[0, :, cols])
+
+        @pl.when(step > 0)
+        def _():
+            for n in range(0, width, tile):
+                cols = slice(n, n + tile)
+                acc[c, :, cols] += dot(held[...], w[0, :, cols])
+
+    else:
+
+        @pl.when(step == 0)
+        def _():
+            acc[c] = acc_in[0]
+
         for n in range(0, width, tile):
             cols = slice(n, n + tile)
-            acc[c, :, cols] += dot(held[...], w[c, :, cols])
+            acc[c, :, cols] += dot(held[...], w[0, :, cols])
 
 
 def project(pieces, arrays, at, place, weight, inverse, depth, carried, tokens, ways, tiled):
     rows = tokens * ways
     width = weight.shape[2]
-    whole = lambda shape: pl.BlockSpec(shape, lambda i, at: (0,) * len(shape))
+    whole = lambda shape: pl.BlockSpec(shape, lambda i, c, at: (0,) * len(shape))
     acc_shape, ss_shape = (3, rows, width), (rows, HEAD)
     in_specs = [whole(x.shape) for x in arrays] + [
-        pl.BlockSpec((3, depth, width), lambda i, at: (0, at[place[0] + i * place[1]], 0)),
-        pl.BlockSpec((1, depth), lambda i, at: (0, at[place[0] + i * place[1]])),
+        pl.BlockSpec((1, depth, width), lambda i, c, at: (c, at[place + i], 0)),
+        pl.BlockSpec((1, depth), lambda i, c, at: (0, at[place + i])),
     ]
     operands = list(arrays) + [weight, inverse]
     if carried is not None:
-        in_specs += [whole(acc_shape), whole(ss_shape)]
+        fetch = lambda i, c, at: (jnp.where(i == 0, c, 2), 0, 0)
+        in_specs += [pl.BlockSpec((1, rows, width), fetch), whole(ss_shape)]
         operands += list(carried)
     return pl.pallas_call(
         partial(
@@ -180,7 +196,7 @@
         ),
         grid_spec=pltpu.PrefetchScalarGridSpec(
             num_scalar_prefetch=1,
-            grid=(len(pieces),),
+            grid=(len(pieces), 3),
             in_specs=in_specs,
             out_specs=(whole(acc_shape), whole(ss_shape)),
             scratch_shapes=[pltpu.VMEM((rows, depth), jnp.bfloat16)],
@@ -189,9 +205,6 @@
             flops=6 * rows * depth * len(pieces) * width,
             bytes_accessed=6 * depth * len(pieces) * width + 8 * 3 * rows * width,
             transcendentals=0,
-        ),
-        input_output_aliases=(
-            {} if carried is None else {len(arrays) + 3: 0, len(arrays) + 4: 1}
         ),
         compiler_params=pltpu.CompilerParams(vmem_limit_bytes=32 << 20),
         name="project",
@@ -262,8 +275,8 @@
         shape = (ways, tokens, width)
         out_spec = pl.BlockSpec((ways, tokens, step), lambda n, at: (0, 0, n))
     whole = lambda shape: pl.BlockSpec(shape, lambda n, at: (0,) * len(shape))
-    at_piece = lambda i: pl.BlockSpec((3, depth, step), lambda n, at: (0, at[place[0] + i * place[1]], n))
-    gain_piece = lambda i: pl.BlockSpec((1, depth), lambda n, at: (0, at[place[0] + i * place[1]]))
+    at_piece = lambda i: pl.BlockSpec((3, depth, step), lambda n, at: (0, at[place + i], n))
+    gain_piece = lambda i: pl.BlockSpec((1, depth), lambda n, at: (0, at[place + i]))
     out = pl.pallas_call(
         partial(
             temporal_kernel,
@@ -390,36 +403,29 @@
             for k in range(1, ways):
                 pieces[u, k] = (shift(part, k), 0)
 
-    table = [lax.rem(me + ways - k, ways) * count + u for k in range(ways) for u in range(count)]
+    other = lambda units: [(u, k) for u in units for k in range(1, ways)]
+    last = count - 1
+    ready = [(u, 0) for u in range(count)] + other(range(min(1, last)))
+    steps = [ready] + [other([u]) for u in range(1, last)] + [other([last])]
+    table = [lax.rem(me + ways - k, ways) * count + u for wanted in steps for u, k in wanted]
     table = jnp.stack(table + [me])
 
-    def gather(wanted):
+    def gather(step):
         listed, arrays = [], []
-        for u, k in wanted:
+        for u, k in steps[step]:
             array, column = pieces[u, k]
-            where = [n for n, x in enumerate(arrays) if x is array]
-            if not where:
-                where = [len(arrays)]
+            if all(array is not x for x in arrays):
                 arrays.append(array)
-            listed.append((where[0], column, k))
+            listed.append(([array is x for x in arrays].index(True), column, k))
         if not tiled:
             arrays = [x.transpose(1, 0, 2, 3).reshape(ways, tokens, -1) for x in arrays]
-        at = [k * count + u for u, k in wanted]
-        stride = at[1] - at[0] if len(at) > 1 else 0
-        assert at == [at[0] + n * stride for n in range(len(at))]
-        return tuple(listed), arrays, table, (at[0], stride)
-
-    own = lambda units: [(u, 0) for u in units]
-    other = lambda units: [(u, k) for u in units for k in range(1, ways)]
-    last = count - 1
-    steps = [own(chunks[0]) + other(u for u in chunks[0] if u < last)]
-    steps += [own(chunk) for chunk in chunks[1:]]
-    steps += [other([u]) for u in range(1, last)]
+        return tuple(listed), arrays, table, sum(len(x) for x in steps[:step])
+
     sizes = dict(tokens=tokens, ways=ways, tiled=tiled)
     carried = None
-    for wanted in steps:
-        carried = project(*gather(wanted), weight, inverse, depth, carried, **sizes)
-    final = gather(other([last]))
+    for i in range(len(steps) - 1):
+        carried = project(*gather(i), weight, inverse, depth, carried, **sizes)
+    final = gather(len(steps) - 1)
     out = temporal(*final, weight, inverse, depth, carried, slot=slot, **sizes)
     out = out.reshape(frames * ways, slot, width)
     out = lax.all_to_all(out, ("frame", "row"), split_axis=0, concat_axis=0, tiled=True)

time: 105 us -> 107 us (1.019)
  Pallas kernels: 31.7 us -> 33.4 us
    pallas_call x3 -> x2, Pallas kernels: 17.1 us -> 18.8 us  [project(): pl.pallas_call(partial(project_kernel, pieces=pieces, arrays=len(arrays),...]
  transfers between devices with their start and end apart: 7 -> 7, of which waited for: 4 -> 4; matrix products, arithmetic and copies ran while one was open for 0% -> 0% of each run, Pallas kernels for 24% -> 25%
where the time goes in v2:
time: 107 us; the launch traced here: 106 us
  Pallas kernels  33.4 us (31%)
  blocking collectives  25.5 us (24%)
  waiting for transfers between devices  25.4 us (24%)
  starting transfers between devices  20.6 us (19%)
    all_to_all x1, blocking collectives, local(): lax.all_to_all(out, ('frame', 'row'), split_axis=0, concat_axis=0, tiled=...  25.5 us
    pallas_call x2, Pallas kernels, project(): pl.pallas_call(partial(project_kernel, pieces=pieces, arrays=len(arrays),...  18.8 us
    all_to_all x2, starting transfers between devices, local(): lax.all_to_all(out, 'frame', split_axis=0, concat_axis=0, tiled=True)  15.6 us
    all_to_all x2, waiting for transfers between devices, local(): lax.all_to_all(out, 'frame', split_axis=0, concat_axis=0, tiled=True)  12.9 us
    ppermute x5, waiting for transfers between devices, shift(): return lax.ppermute(x, 'row', [(i, (i + k) % ways) for i in range(ways)])  12.6 us
    pallas_call x2, Pallas kernels, spatial(): pl.pallas_call(partial(spatial_kernel, heads=heads, pool=pool, tiled=tile...  6.26 us
    pallas_call x1, Pallas kernels, temporal(): pl.pallas_call(partial(temporal_kernel, count=count, heads=heads, tokens=...  5.4 us
    ppermute x5, starting transfers between devices, shift(): return lax.ppermute(x, 'row', [(i, (i + k) % ways) for i in range(ways)])  4.93 us
  transfers between devices with their start and end apart: 7, of which 4 were waited for; matrix products, arithmetic and copies ran while one was open for 0% of the time, Pallas kernels for 25%

profile of v2, /device:TPU:1, one launch (start us, length us, event | category | flops | bytes accessed | tf_op | source)
XLA Modules:
  0.0 106.0 jit_solution(8374244881843278997)
XLA Ops:
  0.0 0.0 copy-start
  0.0 1.1 %pack.3 = bf16[3,128,512]{2,1,0:T(8,128)(2,1)S(1)} custom-call(s32[1]{0:T(128)} %bitcast.3.at, bf16[1,128,3072]{2,1,0:T(8,128)(2,1)} %q.7, bf16[1,128,3072]{2,1,0:T(8,128)(2,1)} %k.7, bf16[1,128,3072]{2,1,0:T(8,128)(2,1)} %v.7), custom_call_target="tpu_custom_call" | custom-call | tf_op jit(solution)/shard_map/pack/pallas_call | solution.py:330
  1.1 2.1 %collective-permute-start.3 = (bf16[3,128,512]{2,1,0:T(8,128)(2,1)S(1)}, bf16[3,128,512]{2,1,0:T(8,128)(2,1)S(1)}, u32[]{:S(2)}, u32[]{:S(2)}) collective-permute-start(bf16[3,128,512]{2,1,0:T(8,128)(2,1)S(1)} %pack.3), channel_id=1, source_target_pairs={{0,1},{1,0},{2,3},{3,2},{4,5},{5,4},{6,7},{7,6},{8,9},{9,8},{10,11... | collective-permute-start | bytes 1179656 | tf_op jit(solution)/shard_map/ppermute | solution.py:381
  3.2 1.9 %pack.2 = bf16[3,128,1024]{2,1,0:T(8,128)(2,1)S(1)} custom-call(s32[2]{0:T(128)S(1)} %add_add_fusion.at, bf16[1,128,3072]{2,1,0:T(8,128)(2,1)} %q.7, bf16[1,128,3072]{2,1,0:T(8,128)(2,1)} %k.7, bf16[1,128,3072]{2,1,0:T(8,128)(2,1)} %v.7), custom_call_target="tpu_custom_call" | custom-call | tf_op jit(solution)/shard_map/pack/pallas_call | solution.py:330
  5.1 0.1 collective-permute-start
  5.2 6.8 %collective-permute-done.3.rest_0_ = bf16[3,128,512]{2,1,0:T(8,128)(2,1)S(1)} collective-permute-done((bf16[3,128,512]{2,1,0:T(8,128)(2,1)S(1)}, bf16[3,128,512]{2,1,0:T(8,128)(2,1)S(1)}, u32[]{:S(2)}, u32[]{:S(2)}) %collective-permute-start.3) | collective-permute-done | bytes 393248 | tf_op jit(solution)/shard_map/ppermute | solution.py:381
  12.0 0.0 copy-done
  12.0 2.7 %spatial.3 = bf16[16,2,8,512]{3,2,1,0:T(8,128)(2,1)} custom-call(s32[1]{0:T(128)} %bitcast.11.base, bf16[1,128,3072]{2,1,0:T(8,128)(2,1)} %q.7, bf16[1,128,3072]{2,1,0:T(8,128)(2,1)} %k.7, bf16[1,128,3072]{2,1,0:T(8,128)(2,1)} %v.7, bf16[3,128,512]{2,1,0:T(8,128)(2,1)S(1)} %collective-permute-done.3.rest_0_, f32[1,3072]{1,0:T(1,128)S(1)} %bitcast.22), custom_call_target="tpu_custom_call" | custom-call | flops 167772160 | bytes 1310720 | tf_op jit(solution)/shard_map/spatial/pallas_call | solution.py:84
  14.6 8.5 %all-to-all-start.1 = ((bf16[16,2,8,512]{3,2,1,0:T(8,128)(2,1)}), bf16[16,2,8,512]{3,2,1,0:T(8,128)(2,1)S(1)}, u32[]{:S(2)}, u32[]{:S(2)}) async-start(bf16[16,2,8,512]{3,2,1,0:T(8,128)(2,1)} %spatial.3), calls=%async_computation.1 | async-start | bytes 524288 | tf_op jit(solution)/shard_map/all_to_all | solution.py:400
  23.1 5.7 %collective-permute-done.rest_0_ = bf16[3,128,1024]{2,1,0:T(8,128)(2,1)S(1)} collective-permute-done((bf16[3,128,1024]{2,1,0:T(8,128)(2,1)S(1)}, bf16[3,128,1024]{2,1,0:T(8,128)(2,1)S(1)}, u32[]{:S(2)}, u32[]{:S(2)}) %collective-permute-start) | collective-permute-done | bytes 786464 | tf_op jit(solution)/shard_map/ppermute | solution.py:381
  28.8 3.6 %spatial.2 = bf16[16,2,8,1024]{3,2,1,0:T(8,128)(2,1)} custom-call(s32[1]{0:T(128)} %bitcast.7.base, bf16[1,128,3072]{2,1,0:T(8,128)(2,1)} %q.7, bf16[1,128,3072]{2,1,0:T(8,128)(2,1)} %k.7, bf16[1,128,3072]{2,1,0:T(8,128)(2,1)} %v.7, bf16[3,128,1024]{2,1,0:T(8,128)(2,1)S(1)} %collective-permute-done.rest_0_, f32[1,3072]{1,0:T(1,128)S(1)} %bitcast.23), custom_call_target="tpu_custom_call" | custom-call | flops 335544320 | bytes 2621440 | tf_op jit(solution)/shard_map/spatial/pallas_call | solution.py:84
  32.5 0.2 all-to-all-done.1.refs_0_
  32.6 7.2 %all-to-all-start = ((bf16[16,2,8,1024]{3,2,1,0:T(8,128)(2,1)}), bf16[16,2,8,1024]{3,2,1,0:T(8,128)(2,1)S(1)}, u32[]{:S(2)}, u32[]{:S(2)}) async-start(bf16[16,2,8,1024]{3,2,1,0:T(8,128)(2,1)} %spatial.2), calls=%async_computation | async-start | bytes 1048576 | tf_op jit(solution)/shard_map/all_to_all | solution.py:400
  39.8 1.2 %collective-permute-start.4 = (bf16[16,2,8,512]{3,2,1,0:T(8,128)(2,1)S(1)}, bf16[16,2,8,512]{3,2,1,0:T(8,128)(2,1)S(1)}, u32[]{:S(2)}, u32[]{:S(2)}) collective-permute-start(bf16[16,2,8,512]{3,2,1,0:T(8,128)(2,1)S(1)} %all-to-all-done.1.refs_0_), channel_id=1, source_target_pairs={{0,1},{1,0},{2,3},{3,2},{4,5},{5,4},{6,7},{7,6},{8,9},{9,8},{10,11... | collective-permute-start | bytes 786440 | tf_op jit(solution)/shard_map/ppermute | solution.py:381
  41.0 0.1 stack.31.at
  41.1 12.7 %all-to-all-done.moved = bf16[16,2,8,1024]{3,2,1,0:T(8,128)(2,1)S(1)} async-done(((bf16[16,2,8,1024]{3,2,1,0:T(8,128)(2,1)}), bf16[16,2,8,1024]{3,2,1,0:T(8,128)(2,1)S(1)}, u32[]{:S(2)}, u32[]{:S(2)}) %all-to-all-start) | async-done | bytes 524320 | tf_op jit(solution)/shard_map/all_to_all | solution.py:400
  53.8 1.3 %collective-permute-start.1 = (bf16[16,2,8,512]{3,2,1,0:T(8,128)(2,1)S(1)}, bf16[16,2,8,512]{3,2,1,0:T(8,128)(2,1)S(1)}, u32[]{:S(2)}, u32[]{:S(2)}) collective-permute-start(bf16[16,2,8,512]{3,2,1,0:T(8,128)(2,1)S(1)} %get-tuple-element.11.refs_2_), channel_id=1, source_target_pairs={{0,1},{1,0},{2,3},{3,2},{4,5},{5,4},{6,7},{7,6},{8,9},{9,8},{10,11... | collective-permute-start | bytes 786440 | tf_op jit(solution)/shard_map/ppermute | solution.py:381
  55.1 0.3 collective-permute-start.2
  55.4 0.0 collective-permute-done.4.refs_3_
  55.4 14.1 %project.2 = (f32[3,256,1536]{2,1,0:T(8,128)S(1)}, f32[256,128]{1,0:T(8,128)S(1)}) custom-call(s32[7]{0:T(128)S(1)} %stack.31.at, bf16[16,2,8,512]{3,2,1,0:T(8,128)(2,1)S(1)} %all-to-all-done.1.refs_0_, bf16[16,2,8,512]{3,2,1,0:T(8,128)(2,1)S(1)} %get-tuple-element.12.refs_1_, bf16[16,2,8,512]{3,2,1,0:T(8,128)(2,1)S(1)} %get-tuple-element.11.refs_2_, ...), custom_call_target="tpu_custom_call" | custom-call | flops 4831838208 | bytes 28311552 | tf_op jit(solution)/shard_map/project/pallas_call | solution.py:183
  69.5 0.0 collective-permute-done.2.refs_0_
  69.5 4.7 %project.3 = (f32[3,256,1536]{2,1,0:T(8,128)S(1)}, f32[256,128]{1,0:T(8,128)S(1)}) custom-call(s32[7]{0:T(128)S(1)} %stack.31.at, bf16[16,2,8,512]{3,2,1,0:T(8,128)(2,1)S(1)} %collective-permute-done.2.refs_0_, bf16[3,3072,1536]{2,1,0:T(8,128)(2,1)} %bitcast.25, f32[1,3072]{1,0:T(1,128)S(1)} %bitcast.20, f32[3,256,1536]{2,1,0:T(8,128)S(1)} %get-tuple-element.13.refs_3_, ...), custom_call_target="tpu_custom_call" | custom-call | flops 1207959552 | bytes 14155776 | tf_op jit(solution)/shard_map/project/pallas_call | solution.py:183
  74.2 0.0 collective-permute-done.1.refs_0_
  74.2 5.4 %temporal.1 = bf16[16,2,8,1536]{3,2,1,0:T(8,128)(2,1)S(1)} custom-call(s32[7]{0:T(128)S(1)} %stack.31.at, bf16[16,2,8,512]{3,2,1,0:T(8,128)(2,1)S(1)} %collective-permute-done.1.refs_0_, bf16[3,3072,1536]{2,1,0:T(8,128)(2,1)} %bitcast.26, f32[1,3072]{1,0:T(1,128)S(1)} %bitcast.21, f32[3,256,1536]{2,1,0:T(8,128)S(1)} %get-tuple-element.15.refs_3_, ...), custom_call_target="tpu_custom_call" | custom-call | flops 1207959552 | bytes 9437184 | tf_op jit(solution)/shard_map/temporal/pallas_call | solution.py:280
  79.6 25.5 %all_to_all.15 = bf16[32,8,1536]{2,1,0:T(8,128)(2,1)S(1)} all-to-all(bf16[32,8,1536]{2,1,0:T(8,128)(2,1)S(1)} %bitcast.18), channel_id=1, replica_groups=mesh['frame'=16,'row'=2] {'frame','row'}, dimensions={0} | all-to-all | bytes 1572864 | tf_op jit(solution)/shard_map/all_to_all | solution.py:431
  105.1 0.9 copy.7
  (3 shorter events, 0.0 us)
Async XLA Ops:
  0.0 12.0 %copy-start = (f32[3072]{0:T(1024)S(1)}, f32[3072]{0:T(1024)}, u32[]{:S(2)}) copy-start(f32[3072]{0:T(1024)} %param.8) | copy-start | bytes 36868
  1.1 10.9 %collective-permute-start.3 = (bf16[3,128,512]{2,1,0:T(8,128)(2,1)S(1)}, bf16[3,128,512]{2,1,0:T(8,128)(2,1)S(1)}, u32[]{:S(2)}, u32[]{:S(2)}) collective-permute-start(bf16[3,128,512]{2,1,0:T(8,128)(2,1)S(1)} %pack.3), channel_id=1, source_target_pairs={{0,1},{1,0},{2,3},{3,2},{4,5},{5,4},{6,7},{7,6},{8,9},{9,8},{10,11... | collective-permute-start | bytes 1179656 | tf_op jit(solution)/shard_map/ppermute | solution.py:381
  5.1 23.8 %collective-permute-start = (bf16[3,128,1024]{2,1,0:T(8,128)(2,1)S(1)}, bf16[3,128,1024]{2,1,0:T(8,128)(2,1)S(1)}, u32[]{:S(2)}, u32[]{:S(2)}) collective-permute-start(bf16[3,128,1024]{2,1,0:T(8,128)(2,1)S(1)} %pack.2), channel_id=1, source_target_pairs={{0,1},{1,0},{2,3},{3,2},{4,5},{5,4},{6,7},{7,6},{8,9},{9,8},{10,11... | collective-permute-start | bytes 2359304 | tf_op jit(solution)/shard_map/ppermute | solution.py:381
  14.6 18.0 %all-to-all-start.1 = ((bf16[16,2,8,512]{3,2,1,0:T(8,128)(2,1)}), bf16[16,2,8,512]{3,2,1,0:T(8,128)(2,1)S(1)}, u32[]{:S(2)}, u32[]{:S(2)}) async-start(bf16[16,2,8,512]{3,2,1,0:T(8,128)(2,1)} %spatial.3), calls=%async_computation.1 | async-start | bytes 524288 | tf_op jit(solution)/shard_map/all_to_all | solution.py:400
  32.6 21.2 %all-to-all-start = ((bf16[16,2,8,1024]{3,2,1,0:T(8,128)(2,1)}), bf16[16,2,8,1024]{3,2,1,0:T(8,128)(2,1)S(1)}, u32[]{:S(2)}, u32[]{:S(2)}) async-start(bf16[16,2,8,1024]{3,2,1,0:T(8,128)(2,1)} %spatial.2), calls=%async_computation | async-start | bytes 1048576 | tf_op jit(solution)/shard_map/all_to_all | solution.py:400
  39.8 15.6 %collective-permute-start.4 = (bf16[16,2,8,512]{3,2,1,0:T(8,128)(2,1)S(1)}, bf16[16,2,8,512]{3,2,1,0:T(8,128)(2,1)S(1)}, u32[]{:S(2)}, u32[]{:S(2)}) collective-permute-start(bf16[16,2,8,512]{3,2,1,0:T(8,128)(2,1)S(1)} %all-to-all-done.1.refs_0_), channel_id=1, source_target_pairs={{0,1},{1,0},{2,3},{3,2},{4,5},{5,4},{6,7},{7,6},{8,9},{9,8},{10,11... | collective-permute-start | bytes 786440 | tf_op jit(solution)/shard_map/ppermute | solution.py:381
  53.8 20.3 %collective-permute-start.1 = (bf16[16,2,8,512]{3,2,1,0:T(8,128)(2,1)S(1)}, bf16[16,2,8,512]{3,2,1,0:T(8,128)(2,1)S(1)}, u32[]{:S(2)}, u32[]{:S(2)}) collective-permute-start(bf16[16,2,8,512]{3,2,1,0:T(8,128)(2,1)S(1)} %get-tuple-element.11.refs_2_), channel_id=1, source_target_pairs={{0,1},{1,0},{2,3},{3,2},{4,5},{5,4},{6,7},{7,6},{8,9},{9,8},{10,11... | collective-permute-start | bytes 786440 | tf_op jit(solution)/shard_map/ppermute | solution.py:381
  55.1 14.4 %collective-permute-start.2 = (bf16[16,2,8,512]{3,2,1,0:T(8,128)(2,1)S(1)}, bf16[16,2,8,512]{3,2,1,0:T(8,128)(2,1)S(1)}, u32[]{:S(2)}, u32[]{:S(2)}) collective-permute-start(bf16[16,2,8,512]{3,2,1,0:T(8,128)(2,1)S(1)} %get-tuple-element.12.refs_1_), channel_id=1, source_target_pairs={{0,1},{1,0},{2,3},{3,2},{4,5},{5,4},{6,7},{7,6},{8,9},{9,8},{10,11... | collective-permute-start | bytes 786440 | tf_op jit(solution)/shard_map/ppermute | solution.py:381

commit v3 on v2

--- a/solution.py
+++ b/solution.py
@@ -120,104 +120,95 @@
     return total
 
 
-def project_kernel(at, *refs, pieces, arrays, first, tokens, ways, tiled):
+VMEM = pl.BlockSpec(memory_space=pltpu.VMEM)
+AHEAD = 4
+
+
+def project_kernel(at, *refs, pieces, arrays, tokens, ways, tiled):
     xs = refs[:arrays]
-    if first:
-        w, inverse, acc, ss, held = refs[arrays:]
-    else:
-        w, inverse, acc_in, ss_in, acc, ss, held = refs[arrays:]
-    depth = held.shape[1]
-    step, c = pl.program_id(0), pl.program_id(1)
+    weight, gain, acc, ss, kept, held, buffer, sems = refs[arrays:]
+    count, _, depth, width = buffer.shape
+    copies = []
+    for i in range(count + kept.shape[0]):
+        rows = pl.ds(pl.multiple_of(at[i] * depth, HEAD), depth)
+        target = buffer.at[i] if i < count else kept.at[i - count]
+        for c in range(3):
+            copies.append(
+                pltpu.make_async_copy(weight.at[c, rows, :], target.at[c], sems.at[3 * i + c])
+            )
+    for copy in copies[:AHEAD]:
+        copy.start()
+    total = None
+    tile = width // 3 if width % 3 == 0 else width
     for i, (which, col, shift) in enumerate(pieces):
-
-        @pl.when((step == i) & (c == 0))
-        def _():
-            for j in range(ways):
-                held[j * tokens : (j + 1) * tokens, :] = rows_of(
-                    xs[which], (j - shift) % ways, slice(col, col + depth), tokens, tiled
-                )
-            before = ss[...] if i else (jnp.zeros_like(ss) if first else ss_in[...])
-            ss[...] = before + squares(held[...], inverse[...])
-
-    width = w.shape[2]
-    tile = width // 3 if width % 3 == 0 else width
-    if first:
-
-        @pl.when(step == 0)
-        def _():
+        for j in range(ways):
+            held[i, j * tokens : (j + 1) * tokens, :] = rows_of(
+                xs[which], (j - shift) % ways, slice(col, col + depth), tokens, tiled
+            )
+        part = squares(held[i], 1.0 / gain[:, pl.ds(pl.multiple_of(at[i] * depth, HEAD), depth)])
+        total = part if total is None else total + part
+        for c in range(3):
+            copies[3 * i + c].wait()
+            if 3 * i + c + AHEAD < len(copies):
+                copies[3 * i + c + AHEAD].start()
             for n in range(0, width, tile):
                 cols = slice(n, n + tile)
-                acc[c, :, cols] = dot(held[...], w[0, :, cols])
-
-        @pl.when(step > 0)
-        def _():
-            for n in range(0, width, tile):
-                cols = slice(n, n + tile)
-                acc[c, :, cols] += dot(held[...], w[0, :, cols])
-
-    else:
-
-        @pl.when(step == 0)
-        def _():
-            acc[c] = acc_in[0]
-
-        for n in range(0, width, tile):
-            cols = slice(n, n + tile)
-            acc[c, :, cols] += dot(held[...], w[0, :, cols])
-
-
-def project(pieces, arrays, at, place, weight, inverse, depth, carried, tokens, ways, tiled):
+                value = dot(held[i], buffer[i, c, :, cols])
+                if i == 0:
+                    acc[c, :, cols] = value
+                else:
+                    acc[c, :, cols] += value
+    ss[...] = total
+    for n in range(3 * count + AHEAD, len(copies)):
+        copies[n].start()
+    for copy in copies[3 * count :]:
+        copy.wait()
+
+
+def project(pieces, arrays, at, after, weight, gain, depth, tokens, ways, tiled):
     rows = tokens * ways
     width = weight.shape[2]
-    whole = lambda shape: pl.BlockSpec(shape, lambda i, c, at: (0,) * len(shape))
-    acc_shape, ss_shape = (3, rows, width), (rows, HEAD)
-    in_specs = [whole(x.shape) for x in arrays] + [
-        pl.BlockSpec((1, depth, width), lambda i, c, at: (c, at[place + i], 0)),
-        pl.BlockSpec((1, depth), lambda i, c, at: (0, at[place + i])),
-    ]
-    operands = list(arrays) + [weight, inverse]
-    if carried is not None:
-        fetch = lambda i, c, at: (jnp.where(i == 0, c, 2), 0, 0)
-        in_specs += [pl.BlockSpec((1, rows, width), fetch), whole(ss_shape)]
-        operands += list(carried)
+    count = len(pieces)
     return pl.pallas_call(
         partial(
             project_kernel,
             pieces=pieces,
             arrays=len(arrays),
-            first=carried is None,
             tokens=tokens,
             ways=ways,
             tiled=tiled,
         ),
         out_shape=(
-            jax.ShapeDtypeStruct(acc_shape, jnp.float32),
-            jax.ShapeDtypeStruct(ss_shape, jnp.float32),
+            pltpu.VMEM((3, rows, width), jnp.float32),
+            pltpu.VMEM((rows, HEAD), jnp.float32),
+            pltpu.VMEM((after, 3, depth, width), weight.dtype),
         ),
         grid_spec=pltpu.PrefetchScalarGridSpec(
             num_scalar_prefetch=1,
-            grid=(len(pieces), 3),
-            in_specs=in_specs,
-            out_specs=(whole(acc_shape), whole(ss_shape)),
-            scratch_shapes=[pltpu.VMEM((rows, depth), jnp.bfloat16)],
+            grid=(),
+            in_specs=[VMEM] * len(arrays) + [pl.BlockSpec(memory_space=pl.ANY), VMEM],
+            out_specs=(VMEM, VMEM, VMEM),
+            scratch_shapes=[
+                pltpu.VMEM((count, rows, depth), jnp.bfloat16),
+                pltpu.VMEM((count, 3, depth, width), weight.dtype),
+                pltpu.SemaphoreType.DMA((3 * (count + after),)),
+            ],
         ),
         cost_estimate=pl.CostEstimate(
-            flops=6 * rows * depth * len(pieces) * width,
-            bytes_accessed=6 * depth * len(pieces) * width + 8 * 3 * rows * width,
+            flops=6 * rows * depth * count * width,
+            bytes_accessed=6 * depth * (count + after) * width,
             transcendentals=0,
         ),
-        compiler_params=pltpu.CompilerParams(vmem_limit_bytes=32 << 20),
+        compiler_params=pltpu.CompilerParams(vmem_limit_bytes=30 << 20),
         name="project",
-    )(at, *operands)
-
-
-def temporal_kernel(at, *refs, count, heads, tokens, ways, slot, tiled, pieces, columns):
-    xs = refs[: len(columns)]
-    ws = refs[len(columns) : len(columns) + count]
-    inverses = refs[len(columns) + count : len(columns) + 2 * count]
-    acc, ss = refs[len(columns) + 2 * count : len(columns) + 2 * count + 2]
-    out, held, rstd = refs[-3:]
+    )(at, *arrays, weight, gain)
+
+
+def temporal_kernel(at, *refs, pieces, arrays, first, heads, tokens, ways, slot, tiled):
+    xs = refs[:arrays]
+    gain, acc, ss, ws, out, held, rstd = refs[arrays:]
     depth = held.shape[2]
+    step = heads * HEAD
 
     @pl.when(pl.program_id(0) == 0)
     def _():
@@ -227,20 +218,22 @@
                 held[i, j * tokens : (j + 1) * tokens, :] = rows_of(
                     xs[which], (j - shift) % ways, slice(col, col + depth), tokens, tiled
                 )
-            total = total + squares(held[i], inverses[i][...])
+            lanes = pl.ds(pl.multiple_of(at[first + i] * depth, HEAD), depth)
+            total = total + squares(held[i], 1.0 / gain[:, lanes])
         mean = jnp.sum(total, axis=1, keepdims=True) * (1.0 / D)
         rstd[...] = jnp.broadcast_to(lax.rsqrt(mean + epsilon), rstd.shape)
 
     row = lax.broadcasted_iota(jnp.int32, (tokens, tokens), 0)
     col = lax.broadcasted_iota(jnp.int32, (tokens, tokens), 1)
     same = lax.rem(row, slot) == lax.rem(col, slot)
+    part = pl.ds(pl.multiple_of(pl.program_id(0) * step, step), step)
+    factor = jnp.concatenate([rstd[...]] * heads, axis=1)
     qkv = []
     for c in range(3):
-        value = acc[c]
-        for i in range(count):
-            value = value + dot(held[i], ws[i][c])
-        qkv.append(value)
-    qkv = [(x * jnp.concatenate([rstd[...]] * heads, axis=1)).astype(jnp.bfloat16) for x in qkv]
+        value = acc[c, :, part]
+        for i in range(len(pieces)):
+            value = value + dot(held[i], ws[i, c, :, part])
+        qkv.append((value * factor).astype(jnp.bfloat16))
     split = [
         (j, slice(j * tokens, (j + 1) * tokens), slice(h * HEAD, (h + 1) * HEAD))
         for h in range(heads)
@@ -251,7 +244,7 @@
         for _, rows, cols in split
     ]
     weights = [weighted(x) for x in scores]
-    me = at[at.shape[0] - 1]
+    me = at[first + len(pieces)]
     for (j, rows, cols), (w, r) in zip(split, weights):
         result = dot((w * r).astype(jnp.bfloat16), qkv[2][rows, cols]).astype(jnp.bfloat16)
         target = lax.rem(me + ways - j, ways)
@@ -261,12 +254,11 @@
             out[target, :, cols] = result
 
 
-def temporal(pieces, arrays, at, place, weight, inverse, depth, carried, tokens, ways, slot, tiled):
+def temporal(pieces, arrays, at, first, gain, depth, carried, tokens, ways, slot, tiled):
     rows = tokens * ways
-    width = weight.shape[2]
-    count = len(pieces)
+    width = carried[0].shape[2]
     frames = tokens // slot
-    heads = math.gcd(width // HEAD, 6)
+    heads = math.gcd(width // HEAD, FINAL_HEADS)
     step = heads * HEAD
     if tiled:
         shape = (frames, ways, slot, width)
@@ -274,49 +266,44 @@
     else:
         shape = (ways, tokens, width)
         out_spec = pl.BlockSpec((ways, tokens, step), lambda n, at: (0, 0, n))
-    whole = lambda shape: pl.BlockSpec(shape, lambda n, at: (0,) * len(shape))
-    at_piece = lambda i: pl.BlockSpec((3, depth, step), lambda n, at: (0, at[place + i], n))
-    gain_piece = lambda i: pl.BlockSpec((1, depth), lambda n, at: (0, at[place + i]))
+    operands = [*arrays, gain, *carried]
     out = pl.pallas_call(
         partial(
             temporal_kernel,
-            count=count,
+            pieces=pieces,
+            arrays=len(arrays),
+            first=first,
             heads=heads,
             tokens=tokens,
             ways=ways,
             slot=slot,
             tiled=tiled,
-            pieces=pieces,
-            columns=tuple(range(len(arrays))),
         ),
         out_shape=jax.ShapeDtypeStruct(shape, jnp.bfloat16),
         grid_spec=pltpu.PrefetchScalarGridSpec(
             num_scalar_prefetch=1,
             grid=(width // step,),
-            in_specs=[whole(x.shape) for x in arrays]
-            + [at_piece(i) for i in range(count)]
-            + [gain_piece(i) for i in range(count)]
-            + [
-                pl.BlockSpec((3, rows, step), lambda n, at: (0, 0, n)),
-                whole((rows, HEAD)),
-            ],
+            in_specs=[VMEM] * len(operands),
             out_specs=out_spec,
             scratch_shapes=[
-                pltpu.VMEM((count, rows, depth), jnp.bfloat16),
+                pltpu.VMEM((len(pieces), rows, depth), jnp.bfloat16),
                 pltpu.VMEM((rows, HEAD), jnp.float32),
             ],
         ),
         cost_estimate=pl.CostEstimate(
-            flops=6 * rows * depth * count * width,
-            bytes_accessed=6 * depth * count * width + 4 * 3 * rows * width,
+            flops=6 * rows * depth * len(pieces) * width,
+            bytes_accessed=2 * rows * width,
             transcendentals=rows * width,
         ),
-        compiler_params=pltpu.CompilerParams(vmem_limit_bytes=24 << 20),
+        compiler_params=pltpu.CompilerParams(vmem_limit_bytes=16 << 20),
         name="temporal",
-    )(at, *arrays, *[weight] * count, *[inverse] * count, *carried)
+    )(at, *operands)
     if not tiled:
         out = out.reshape(ways, frames, slot, width).transpose(1, 0, 2, 3)
     return out
+
+
+FINAL_HEADS = 6
 
 
 def pack_kernel(at, q, k, v, out):
@@ -339,23 +326,6 @@
         compiler_params=pltpu.CompilerParams(vmem_limit_bytes=8 << 20),
         name="pack",
     )(at, q, k, v)
-
-
-def split_kernel(moved, *outs):
-    for n, out in enumerate(outs):
-        out[...] = moved[..., n * out.shape[-1] : (n + 1) * out.shape[-1]]
-
-
-def split(moved, count):
-    if count == 1:
-        return (moved,)
-    shape = moved.shape[:-1] + (moved.shape[-1] // count,)
-    return pl.pallas_call(
-        split_kernel,
-        out_shape=(jax.ShapeDtypeStruct(shape, moved.dtype),) * count,
-        compiler_params=pltpu.CompilerParams(vmem_limit_bytes=8 << 20),
-        name="split",
-    )(moved)
 
 
 def local(spatial_q, spatial_k, spatial_v, norm_gain, temporal_weight):
@@ -370,12 +340,13 @@
     count = chunk_count(group)
     heads = group // count
     depth = heads * HEAD
-    weight = jnp.transpose(temporal_weight, (1, 0, 2))
+    weight = pltpu.with_memory_space_constraint(
+        jnp.transpose(temporal_weight, (1, 0, 2)), pltpu.HBM
+    )
     spatial_q, spatial_k, spatial_v = (
         pltpu.with_memory_space_constraint(x, pltpu.HBM) for x in (spatial_q, spatial_k, spatial_v)
     )
     gain = norm_gain.reshape(1, -1)
-    inverse = 1.0 / gain
 
     def shift(x, k):
         return lax.ppermute(x, "row", [(i, (i + k) % ways) for i in range(ways)])
@@ -398,15 +369,14 @@
             spatial_q, spatial_k, spatial_v, parts, gain, base, frames, span, heads
         )
         moved = lax.all_to_all(out, "frame", split_axis=0, concat_axis=0, tiled=True)
-        for u, part in zip(chunk, split(moved, len(chunk))):
-            pieces[u, 0] = (part, 0)
-            for k in range(1, ways):
-                pieces[u, k] = (shift(part, k), 0)
+        shared = [moved] + [shift(moved, k) for k in range(1, ways)]
+        for n, u in enumerate(chunk):
+            for k in range(ways):
+                pieces[u, k] = (shared[k], n * depth)
 
     other = lambda units: [(u, k) for u in units for k in range(1, ways)]
-    last = count - 1
-    ready = [(u, 0) for u in range(count)] + other(range(min(1, last)))
-    steps = [ready] + [other([u]) for u in range(1, last)] + [other([last])]
+    ready = [(u, 0) for u in range(count)] + [key for c in chunks[:-1] for key in other(c)]
+    steps = [ready, other(chunks[-1])]
     table = [lax.rem(me + ways - k, ways) * count + u for wanted in steps for u, k in wanted]
     table = jnp.stack(table + [me])
 
@@ -419,14 +389,11 @@
             listed.append(([array is x for x in arrays].index(True), column, k))
         if not tiled:
             arrays = [x.transpose(1, 0, 2, 3).reshape(ways, tokens, -1) for x in arrays]
-        return tuple(listed), arrays, table, sum(len(x) for x in steps[:step])
+        return tuple(listed), arrays, table
 
     sizes = dict(tokens=tokens, ways=ways, tiled=tiled)
-    carried = None
-    for i in range(len(steps) - 1):
-        carried = project(*gather(i), weight, inverse, depth, carried, **sizes)
-    final = gather(len(steps) - 1)
-    out = temporal(*final, weight, inverse, depth, carried, slot=slot, **sizes)
+    carried = project(*gather(0), len(steps[1]), weight, gain, depth, **sizes)
+    out = temporal(*gather(1), len(ready), gain, depth, carried, slot=slot, **sizes)
     out = out.reshape(frames * ways, slot, width)
     out = lax.all_to_all(out, ("frame", "row"), split_axis=0, concat_axis=0, tiled=True)
     out = out.reshape(frames, ways, slot, width).transpose(0, 2, 1, 3)

time: 107 us -> 99.3 us (0.928)
  Pallas kernels: 33.4 us -> 25.1 us
  starting transfers between devices: 20.6 us -> 19.5 us
    pallas_call x2 -> x1, Pallas kernels: 18.8 us -> 10.9 us  [project(): pl.pallas_call(partial(project_kernel, pieces=pieces, arrays=len(arrays),...]
    pallas_call x2 -> x1, Pallas kernels: 5.43 us -> 4.98 us  [temporal(): pl.pallas_call(partial(temporal_kernel, pieces=pieces, arrays=len(arrays)...]
    ppermute x5 -> x4, starting transfers between devices: 4.93 us -> 4.61 us  [shift(): return lax.ppermute(x, 'row', [(i, (i + k) % ways) for i in range(ways)])]
    ppermute x5 -> x4, waiting for transfers between devices: 12.6 us -> 12.7 us  [shift(): return lax.ppermute(x, 'row', [(i, (i + k) % ways) for i in range(ways)])]
  transfers between devices with their start and end apart: 7 -> 6, of which waited for: 4 -> 5; matrix products, arithmetic and copies ran while one was open for 0% -> 0% of each run, Pallas kernels for 25% -> 19%
where the time goes in v3:
time: 99.3 us; the launch traced here: 98.9 us
  waiting for transfers between devices  26.4 us (27%)
  blocking collectives  26.1 us (26%)
  Pallas kernels  25.1 us (25%)
  starting transfers between devices  19.5 us (20%)
  local copies, waits for them, and re-layouts  1.67 us (2%)
    all_to_all x1, blocking collectives, local(): lax.all_to_all(out, ('frame', 'row'), split_axis=0, concat_axis=0, tiled=...  26.1 us
    all_to_all x2, starting transfers between devices, local(): lax.all_to_all(out, 'frame', split_axis=0, concat_axis=0, tiled=True)  14.9 us
    all_to_all x2, waiting for transfers between devices, local(): lax.all_to_all(out, 'frame', split_axis=0, concat_axis=0, tiled=True)  13.7 us
    ppermute x4, waiting for transfers between devices, shift(): return lax.ppermute(x, 'row', [(i, (i + k) % ways) for i in range(ways)])  12.7 us
    pallas_call x1, Pallas kernels, project(): pl.pallas_call(partial(project_kernel, pieces=pieces, arrays=len(arrays),...  10.9 us
    pallas_call x2, Pallas kernels, spatial(): pl.pallas_call(partial(spatial_kernel, heads=heads, pool=pool, tiled=tile...  6.28 us
    pallas_call x1, Pallas kernels, temporal(): pl.pallas_call(partial(temporal_kernel, pieces=pieces, arrays=len(arrays)...  4.98 us
    ppermute x4, starting transfers between devices, shift(): return lax.ppermute(x, 'row', [(i, (i + k) % ways) for i in range(ways)])  4.61 us
  transfers between devices with their start and end apart: 6, of which 5 were waited for; matrix products, arithmetic and copies ran while one was open for 0% of the time, Pallas kernels for 19%

profile of v3, /device:TPU:1, one launch (start us, length us, event | category | flops | bytes accessed | tf_op | source)
XLA Modules:
  0.0 98.9 jit_solution(10541226522561567152)
XLA Ops:
  0.0 0.0 copy-start.1
  0.0 1.1 %pack.3 = bf16[3,128,512]{2,1,0:T(8,128)(2,1)S(1)} custom-call(s32[1]{0:T(128)} %bitcast.3.at, bf16[1,128,3072]{2,1,0:T(8,128)(2,1)} %q.7, bf16[1,128,3072]{2,1,0:T(8,128)(2,1)} %k.7, bf16[1,128,3072]{2,1,0:T(8,128)(2,1)} %v.7), custom_call_target="tpu_custom_call" | custom-call | tf_op jit(solution)/shard_map/pack/pallas_call | solution.py:317
  1.1 2.1 %collective-permute-start.2 = (bf16[3,128,512]{2,1,0:T(8,128)(2,1)S(1)}, bf16[3,128,512]{2,1,0:T(8,128)(2,1)S(1)}, u32[]{:S(2)}, u32[]{:S(2)}) collective-permute-start(bf16[3,128,512]{2,1,0:T(8,128)(2,1)S(1)} %pack.3), channel_id=1, source_target_pairs={{0,1},{1,0},{2,3},{3,2},{4,5},{5,4},{6,7},{7,6},{8,9},{9,8},{10,11... | collective-permute-start | bytes 1179656 | tf_op jit(solution)/shard_map/ppermute | solution.py:352
  3.2 1.9 %pack.2 = bf16[3,128,1024]{2,1,0:T(8,128)(2,1)S(1)} custom-call(s32[2]{0:T(128)S(1)} %add_add_fusion.at, bf16[1,128,3072]{2,1,0:T(8,128)(2,1)} %q.7, bf16[1,128,3072]{2,1,0:T(8,128)(2,1)} %k.7, bf16[1,128,3072]{2,1,0:T(8,128)(2,1)} %v.7), custom_call_target="tpu_custom_call" | custom-call | tf_op jit(solution)/shard_map/pack/pallas_call | solution.py:317
  5.1 0.1 collective-permute-start
  5.2 6.8 %collective-permute-done.2.rest_0_ = bf16[3,128,512]{2,1,0:T(8,128)(2,1)S(1)} collective-permute-done((bf16[3,128,512]{2,1,0:T(8,128)(2,1)S(1)}, bf16[3,128,512]{2,1,0:T(8,128)(2,1)S(1)}, u32[]{:S(2)}, u32[]{:S(2)}) %collective-permute-start.2) | collective-permute-done | bytes 393248 | tf_op jit(solution)/shard_map/ppermute | solution.py:352
  12.0 0.0 copy-start
  12.0 0.7 copy-done
  12.7 2.7 %spatial.3 = bf16[16,2,8,512]{3,2,1,0:T(8,128)(2,1)} custom-call(s32[1]{0:T(128)} %bitcast.9.base, bf16[1,128,3072]{2,1,0:T(8,128)(2,1)} %q.7, bf16[1,128,3072]{2,1,0:T(8,128)(2,1)} %k.7, bf16[1,128,3072]{2,1,0:T(8,128)(2,1)} %v.7, bf16[3,128,512]{2,1,0:T(8,128)(2,1)S(1)} %collective-permute-done.2.rest_0_, f32[1,3072]{1,0:T(1,128)S(1)} %bitcast.18), custom_call_target="tpu_custom_call" | custom-call | flops 167772160 | bytes 1310720 | tf_op jit(solution)/shard_map/spatial/pallas_call | solution.py:84
  15.4 8.5 %all-to-all-start.1 = ((bf16[16,2,8,512]{3,2,1,0:T(8,128)(2,1)}), bf16[16,2,8,512]{3,2,1,0:T(8,128)(2,1)S(1)}, u32[]{:S(2)}, u32[]{:S(2)}) async-start(bf16[16,2,8,512]{3,2,1,0:T(8,128)(2,1)} %spatial.3), calls=%async_computation.1 | async-start | bytes 524288 | tf_op jit(solution)/shard_map/all_to_all | solution.py:371
  23.8 5.0 %collective-permute-done.rest_0_ = bf16[3,128,1024]{2,1,0:T(8,128)(2,1)S(1)} collective-permute-done((bf16[3,128,1024]{2,1,0:T(8,128)(2,1)S(1)}, bf16[3,128,1024]{2,1,0:T(8,128)(2,1)S(1)}, u32[]{:S(2)}, u32[]{:S(2)}) %collective-permute-start) | collective-permute-done | bytes 786464 | tf_op jit(solution)/shard_map/ppermute | solution.py:352
  28.8 0.0 copy-done.1
  28.8 3.6 %spatial.2 = bf16[16,2,8,1024]{3,2,1,0:T(8,128)(2,1)} custom-call(s32[1]{0:T(128)} %bitcast.7.base, bf16[1,128,3072]{2,1,0:T(8,128)(2,1)} %q.7, bf16[1,128,3072]{2,1,0:T(8,128)(2,1)} %k.7, bf16[1,128,3072]{2,1,0:T(8,128)(2,1)} %v.7, bf16[3,128,1024]{2,1,0:T(8,128)(2,1)S(1)} %collective-permute-done.rest_0_, f32[1,3072]{1,0:T(1,128)S(1)} %bitcast.19), custom_call_target="tpu_custom_call" | custom-call | flops 335544320 | bytes 2621440 | tf_op jit(solution)/shard_map/spatial/pallas_call | solution.py:84
  32.5 0.9 all-to-all-done.1.refs_0_
  33.4 6.5 %all-to-all-start = ((bf16[16,2,8,1024]{3,2,1,0:T(8,128)(2,1)}), bf16[16,2,8,1024]{3,2,1,0:T(8,128)(2,1)S(1)}, u32[]{:S(2)}, u32[]{:S(2)}) async-start(bf16[16,2,8,1024]{3,2,1,0:T(8,128)(2,1)} %spatial.2), calls=%async_computation | async-start | bytes 1048576 | tf_op jit(solution)/shard_map/all_to_all | solution.py:371
  39.8 1.2 %collective-permute-start.3 = (bf16[16,2,8,512]{3,2,1,0:T(8,128)(2,1)S(1)}, bf16[16,2,8,512]{3,2,1,0:T(8,128)(2,1)S(1)}, u32[]{:S(2)}, u32[]{:S(2)}) collective-permute-start(bf16[16,2,8,512]{3,2,1,0:T(8,128)(2,1)S(1)} %all-to-all-done.1.refs_0_), channel_id=1, source_target_pairs={{0,1},{1,0},{2,3},{3,2},{4,5},{5,4},{6,7},{7,6},{8,9},{9,8},{10,11... | collective-permute-start | bytes 786440 | tf_op jit(solution)/shard_map/ppermute | solution.py:352
  41.0 12.8 %all-to-all-done.refs_1_ = bf16[16,2,8,1024]{3,2,1,0:T(8,128)(2,1)S(1)} async-done(((bf16[16,2,8,1024]{3,2,1,0:T(8,128)(2,1)}), bf16[16,2,8,1024]{3,2,1,0:T(8,128)(2,1)S(1)}, u32[]{:S(2)}, u32[]{:S(2)}) %all-to-all-start) | async-done | bytes 524320 | tf_op jit(solution)/shard_map/all_to_all | solution.py:371
  53.8 1.2 %collective-permute-start.1 = (bf16[16,2,8,1024]{3,2,1,0:T(8,128)(2,1)S(1)}, bf16[16,2,8,1024]{3,2,1,0:T(8,128)(2,1)S(1)}, u32[]{:S(2)}, u32[]{:S(2)}) collective-permute-start(bf16[16,2,8,1024]{3,2,1,0:T(8,128)(2,1)S(1)} %all-to-all-done.refs_1_), channel_id=1, source_target_pairs={{0,1},{1,0},{2,3},{3,2},{4,5},{5,4},{6,7},{7,6},{8,9},{9,8},{10,11... | collective-permute-start | bytes 1572872 | tf_op jit(solution)/shard_map/ppermute | solution.py:352
  55.0 0.1 stack.31.at
  55.1 0.0 collective-permute-done.3.refs_2_
  55.1 10.9 %project.1 = (f32[3,256,1536]{2,1,0:T(8,128)S(1)}, f32[256,128]{1,0:T(8,128)S(1)}, bf16[2,3,512,1536]{3,2,1,0:T(8,128)(2,1)S(1)}) custom-call(s32[7]{0:T(128)S(1)} %stack.31.at, bf16[16,2,8,512]{3,2,1,0:T(8,128)(2,1)S(1)} %all-to-all-done.1.refs_0_, bf16[16,2,8,1024]{3,2,1,0:T(8,128)(2,1)S(1)} %all-to-all-done.refs_1_, ...), custom_call_target="tpu_custom_call" | custom-call | flops 4831838208 | bytes 28311552 | tf_op jit(solution)/shard_map/project/pallas_call | solution.py:172
  66.1 0.9 collective-permute-done.1.refs_0_
  66.9 5.0 %temporal.1 = bf16[16,2,8,1536]{3,2,1,0:T(8,128)(2,1)S(1)} custom-call(s32[7]{0:T(128)S(1)} %stack.31.at, bf16[16,2,8,1024]{3,2,1,0:T(8,128)(2,1)S(1)} %collective-permute-done.1.refs_0_, f32[1,3072]{1,0:T(1,128)S(1)} %bitcast.21, f32[3,256,1536]{2,1,0:T(8,128)S(1)} %get-tuple-element.8.refs_2_, f32[256,128]{1,0:T(8,128)S(1)} %get-tuple-element.9.refs_3_, ...), custom_call_target="tpu_custom_call" | custom-call | flops 2415919104 | bytes 786432 | tf_op jit(solution)/shard_map/temporal/pallas_call | solution.py:270
  71.9 26.1 %all_to_all.15 = bf16[32,8,1536]{2,1,0:T(8,128)(2,1)S(1)} all-to-all(bf16[32,8,1536]{2,1,0:T(8,128)(2,1)S(1)} %bitcast.17), channel_id=1, replica_groups=mesh['frame'=16,'row'=2] {'frame','row'}, dimensions={0} | all-to-all | bytes 1572864 | tf_op jit(solution)/shard_map/all_to_all | solution.py:398
  98.0 0.9 copy.7
  (1 shorter events, 0.0 us)
Async XLA Ops:
  0.0 28.8 %copy-start.1 = (f32[3072]{0:T(1024)S(1)}, f32[3072]{0:T(1024)}, u32[]{:S(2)}) copy-start(f32[3072]{0:T(1024)} %param.8) | copy-start | bytes 36868
  1.1 10.9 %collective-permute-start.2 = (bf16[3,128,512]{2,1,0:T(8,128)(2,1)S(1)}, bf16[3,128,512]{2,1,0:T(8,128)(2,1)S(1)}, u32[]{:S(2)}, u32[]{:S(2)}) collective-permute-start(bf16[3,128,512]{2,1,0:T(8,128)(2,1)S(1)} %pack.3), channel_id=1, source_target_pairs={{0,1},{1,0},{2,3},{3,2},{4,5},{5,4},{6,7},{7,6},{8,9},{9,8},{10,11... | collective-permute-start | bytes 1179656 | tf_op jit(solution)/shard_map/ppermute | solution.py:352
  5.1 23.8 %collective-permute-start = (bf16[3,128,1024]{2,1,0:T(8,128)(2,1)S(1)}, bf16[3,128,1024]{2,1,0:T(8,128)(2,1)S(1)}, u32[]{:S(2)}, u32[]{:S(2)}) collective-permute-start(bf16[3,128,1024]{2,1,0:T(8,128)(2,1)S(1)} %pack.2), channel_id=1, source_target_pairs={{0,1},{1,0},{2,3},{3,2},{4,5},{5,4},{6,7},{7,6},{8,9},{9,8},{10,11... | collective-permute-start | bytes 2359304 | tf_op jit(solution)/shard_map/ppermute | solution.py:352
  12.0 0.7 copy-start
  15.4 18.0 %all-to-all-start.1 = ((bf16[16,2,8,512]{3,2,1,0:T(8,128)(2,1)}), bf16[16,2,8,512]{3,2,1,0:T(8,128)(2,1)S(1)}, u32[]{:S(2)}, u32[]{:S(2)}) async-start(bf16[16,2,8,512]{3,2,1,0:T(8,128)(2,1)} %spatial.3), calls=%async_computation.1 | async-start | bytes 524288 | tf_op jit(solution)/shard_map/all_to_all | solution.py:371
  33.4 20.5 %all-to-all-start = ((bf16[16,2,8,1024]{3,2,1,0:T(8,128)(2,1)}), bf16[16,2,8,1024]{3,2,1,0:T(8,128)(2,1)S(1)}, u32[]{:S(2)}, u32[]{:S(2)}) async-start(bf16[16,2,8,1024]{3,2,1,0:T(8,128)(2,1)} %spatial.2), calls=%async_computation | async-start | bytes 1048576 | tf_op jit(solution)/shard_map/all_to_all | solution.py:371
  39.8 15.3 %collective-permute-start.3 = (bf16[16,2,8,512]{3,2,1,0:T(8,128)(2,1)S(1)}, bf16[16,2,8,512]{3,2,1,0:T(8,128)(2,1)S(1)}, u32[]{:S(2)}, u32[]{:S(2)}) collective-permute-start(bf16[16,2,8,512]{3,2,1,0:T(8,128)(2,1)S(1)} %all-to-all-done.1.refs_0_), channel_id=1, source_target_pairs={{0,1},{1,0},{2,3},{3,2},{4,5},{5,4},{6,7},{7,6},{8,9},{9,8},{10,11... | collective-permute-start | bytes 786440 | tf_op jit(solution)/shard_map/ppermute | solution.py:352
  53.8 13.1 %collective-permute-start.1 = (bf16[16,2,8,1024]{3,2,1,0:T(8,128)(2,1)S(1)}, bf16[16,2,8,1024]{3,2,1,0:T(8,128)(2,1)S(1)}, u32[]{:S(2)}, u32[]{:S(2)}) collective-permute-start(bf16[16,2,8,1024]{3,2,1,0:T(8,128)(2,1)S(1)} %all-to-all-done.refs_1_), channel_id=1, source_target_pairs={{0,1},{1,0},{2,3},{3,2},{4,5},{5,4},{6,7},{7,6},{8,9},{9,8},{10,11... | collective-permute-start | bytes 1572872 | tf_op jit(solution)/shard_map/ppermute | solution.py:352

commit v4 on v3

v4 whole, which is shorter than its diff:
```python
import math
from functools import partial

import jax
import jax.numpy as jnp
from jax import lax
from jax.experimental import pallas as pl
from jax.experimental.pallas import tpu as pltpu
from jax.sharding import PartitionSpec as P

D = 3072
HEADS = 24
AGENTS = 128
HEAD = D // HEADS
SCALE = HEAD ** (-0.5)
EXPONENT = SCALE * math.log2(math.e)

epsilon = 1e-06


def dot(left, right):
    return jnp.dot(left, right, preferred_element_type=jnp.float32)


def dot_nt(left, right):
    return lax.dot_general(
        left, right, (((1,), (1,)), ((), ())), preferred_element_type=jnp.float32
    )


VMEM = pl.BlockSpec(memory_space=pltpu.VMEM)


def weighted(scores):
    weights = jnp.exp2((scores - jnp.max(scores, axis=1, keepdims=True)) * EXPONENT)
    return weights, 1.0 / jnp.sum(weights, axis=1, keepdims=True)


def spatial_kernel(at, *refs, index, pool, tiled, lines):
    inputs, rest, (own, factor, sems) = refs[:3], refs[3:-3], refs[-3:]
    if lines:
        rest, outs, out, own = rest[: -lines - 1], rest[-lines - 1 : -1], rest[-1], own
        received, gain = rest[:-1], rest[-1]
        frame = at[at.shape[0] - 1]
    else:
        received, gain, out = rest[:-2], rest[-2], rest[-1]
    ways = len(received) + 1
    tokens, width = own.shape[1:]
    lanes = pl.ds(pl.multiple_of(at[index] * HEAD, HEAD), width)
    copies = [
        pltpu.make_async_copy(ref.at[0, :, lanes], own.at[i], sems.at[i])
        for i, ref in enumerate(inputs)
    ]
    copies.append(pltpu.make_async_copy(gain.at[:, lanes], factor, sems.at[3]))
    for copy in copies:
        copy.start()
    agent = lax.broadcasted_iota(jnp.int32, (tokens // pool, tokens), 0)
    token = lax.broadcasted_iota(jnp.int32, (tokens // pool, tokens), 1)
    member = ((token >= agent * pool) & (token < (agent + 1) * pool)).astype(jnp.bfloat16)
    for copy in copies:
        copy.wait()
    blocks = [own, *received]
    for start in range(0, width, TOGETHER * HEAD):
        stop = min(width, start + TOGETHER * HEAD)
        pooled = [dot(member, ref[0, :, start:stop]) for ref in blocks]
        pooled = (jnp.concatenate(pooled) * (1.0 / pool)).astype(jnp.bfloat16)
        split = [slice(n, n + HEAD) for n in range(start, stop, HEAD)]
        agents = [pooled[:, n.start - start : n.stop - start] for n in split]
        queries, keys, values = (
            [jnp.concatenate([ref[i, :, cols] for ref in blocks]) for cols in split]
            for i in range(3)
        )
        agent_scores = [dot_nt(a, b) for a, b in zip(agents, keys)]
        token_scores = [dot_nt(a, b) for a, b in zip(queries, agents)]
        agent_weights = [weighted(x) for x in agent_scores]
        token_weights = [weighted(x) for x in token_scores]
        agent_values = [
            (dot(w.astype(jnp.bfloat16), x) * r).astype(jnp.bfloat16)
            for (w, r), x in zip(agent_weights, values)
        ]
        results = [
            dot((w * r).astype(jnp.bfloat16), x) for (w, r), x in zip(token_weights, agent_values)
        ]
        for cols, result in zip(split, results):
            result = (result * factor[:, cols]).astype(jnp.bfloat16)
            for j in range(ways):
                block = result[j * tokens : (j + 1) * tokens]
                if lines:
                    slot = out.shape[2]
                    for f in range(out.shape[0]):
                        out[f ^ frame, j, :, cols] = block[f * slot : (f + 1) * slot]
                elif tiled:
                    out[:, j, :, cols] = block.reshape(out.shape[0], out.shape[2], HEAD)
                else:
                    out[j, :, cols] = block
    if lines:
        for n, target in enumerate(outs):
            size = target.shape[0]
            target[...] = out[n * size : (n + 1) * size]


TOGETHER = 4


def spatial(q, k, v, received, gain, at, index, frames, lines=0):
    tokens = q.shape[1]
    width = received[0].shape[2] if received else q.shape[2]
    ways = len(received) + 1
    slot = tokens // frames
    tiled = slot % 8 == 0
    shape = (frames, ways, slot, width) if tiled else (ways, tokens, width)
    hbm = pl.BlockSpec(memory_space=pl.ANY)
    out = pl.pallas_call(
        partial(
            spatial_kernel, index=index, pool=tokens * ways // AGENTS, tiled=tiled, lines=lines
        ),
        out_shape=(
            [jax.ShapeDtypeStruct((frames // lines, *shape[1:]), jnp.bfloat16)] * lines
            if lines
            else jax.ShapeDtypeStruct(shape, jnp.bfloat16)
        ),
        grid_spec=pltpu.PrefetchScalarGridSpec(
            num_scalar_prefetch=1,
            grid=(),
            in_specs=[hbm] * 3 + [VMEM] * len(received) + [hbm],
            out_specs=[VMEM] * lines if lines else VMEM,
            scratch_shapes=([pltpu.VMEM(shape, jnp.bfloat16)] if lines else [])
            + [
                pltpu.VMEM((3, tokens, width), jnp.bfloat16),
                pltpu.VMEM((1, width), jnp.float32),
                pltpu.SemaphoreType.DMA((4,)),
            ],
        ),
        cost_estimate=pl.CostEstimate(
            flops=10 * tokens * ways * AGENTS * width,
            bytes_accessed=10 * tokens * ways * width,
            transcendentals=2 * tokens * ways * width,
        ),
        compiler_params=pltpu.CompilerParams(vmem_limit_bytes=16 << 20),
        name="spatial",
    )(at, q, k, v, *received, gain)
    if not tiled and not lines:
        out = out.reshape(ways, frames, slot, width).transpose(1, 0, 2, 3)
    return out


def rows_of(ref, block, tokens, tiled):
    if tiled:
        return ref[:, block, :, :].reshape(tokens, -1)
    return ref[block]


def squares(x, inverse):
    y = x.astype(jnp.float32) * inverse
    y = y * y
    total = y[:, :HEAD]
    for at in range(HEAD, y.shape[1], HEAD):
        total = total + y[:, at : at + HEAD]
    return total


AHEAD = 4


def hold(held, xs, depths, shifts, tokens, ways, tiled):
    column = 0
    for x, depth, shift in zip(xs, depths, shifts):
        for j in range(ways):
            held[j * tokens : (j + 1) * tokens, column : column + depth] = rows_of(
                x, (j - shift) % ways, tokens, tiled
            )
        column += depth


def project_kernel(at, *refs, groups, shifts, depths, tokens, ways, tiled):
    xs = refs[: len(shifts)]
    weight, gain, acc, ss = refs[len(shifts) : len(shifts) + 4]
    rest = refs[len(shifts) + 4 :]
    kept = rest[: len(groups) - sum(g is not None for g in groups)]
    sems = rest[-1]
    used = [g for g in groups if g is not None]
    scratch = rest[len(kept) : -1]
    held, buffers = scratch[: len(used)], scratch[len(used) :]
    targets = [*buffers, *kept]
    copies = []
    for i, target in enumerate(targets):
        rows = pl.ds(pl.multiple_of(at[i] * HEAD, HEAD), target.shape[1])
        for c in range(3):
            copies.append(
                pltpu.make_async_copy(weight.at[c, rows, :], target.at[c], sems.at[3 * i + c])
            )
    for copy in copies[:AHEAD]:
        copy.start()
    width = weight.shape[2]
    tile = width // 3 if width % 3 == 0 else width
    total = None
    for i, members in enumerate(used):
        hold(
            held[i],
            [xs[m] for m in members],
            [depths[m] for m in members],
            [shifts[m] for m in members],
            tokens,
            ways,
            tiled,
        )
        lanes = pl.ds(pl.multiple_of(at[i] * HEAD, HEAD), held[i].shape[1])
        part = squares(held[i][...], 1.0 / gain[:, lanes])
        total = part if total is None else total + part
        for c in range(3):
            copies[3 * i + c].wait()
            if 3 * i + c + AHEAD < len(copies):
                copies[3 * i + c + AHEAD].start()
            for n in range(0, width, tile):
                cols = slice(n, n + tile)
                value = dot(held[i][...], buffers[i][c, :, cols])
                if i == 0:
                    acc[c, :, cols] = value
                else:
                    acc[c, :, cols] += value
    ss[...] = total
    for n in range(3 * len(used) + AHEAD, len(copies)):
        copies[n].start()
    for copy in copies[3 * len(used) :]:
        copy.wait()


def project(groups, arrays, shifts, at, later, weight, gain, tokens, ways, tiled):
    rows = tokens * ways
    width = weight.shape[2]
    depths = [x.shape[-1] for x in arrays]
    sums = [sum(depths[m] for m in g) for g in groups]
    return pl.pallas_call(
        partial(
            project_kernel,
            groups=(*groups, *[None] * len(later)),
            shifts=shifts,
            depths=depths,
            tokens=tokens,
            ways=ways,
            tiled=tiled,
        ),
        out_shape=(
            pltpu.VMEM((3, rows, width), jnp.float32),
            pltpu.VMEM((rows, HEAD), jnp.float32),
            *[pltpu.VMEM((3, depth, width), weight.dtype) for depth in later],
        ),
        grid_spec=pltpu.PrefetchScalarGridSpec(
            num_scalar_prefetch=1,
            grid=(),
            in_specs=[VMEM] * len(arrays) + [pl.BlockSpec(memory_space=pl.ANY), VMEM],
            out_specs=(VMEM,) * (2 + len(later)),
            scratch_shapes=[pltpu.VMEM((rows, depth), jnp.bfloat16) for depth in sums]
            + [pltpu.VMEM((3, depth, width), weight.dtype) for depth in sums]
            + [pltpu.SemaphoreType.DMA((3 * (len(sums) + len(later)),))],
        ),
        cost_estimate=pl.CostEstimate(
            flops=6 * rows * sum(sums) * width,
            bytes_accessed=6 * (sum(sums) + sum(later)) * width,
            transcendentals=0,
        ),
        compiler_params=pltpu.CompilerParams(vmem_limit_bytes=32 << 20),
        name="project",
    )(at, *arrays, weight, gain)


def temporal_kernel(at, *refs, first, shifts, heads, tokens, ways, slot, tiled):
    count = len(shifts)
    xs = refs[:count]
    gain, acc, ss = refs[count : count + 3]
    ws = refs[count + 3 : 2 * count + 3]
    out, *held, rstd = refs[2 * count + 3 :]
    step = heads * HEAD

    @pl.when(pl.program_id(0) == 0)
    def _():
        total = ss[...]
        for i in range(count):
            depth = ws[i].shape[1]
            hold(held[i], [xs[i]], [depth], [shifts[i]], tokens, ways, tiled)
            lanes = pl.ds(pl.multiple_of(at[first + i] * HEAD, HEAD), depth)
            total = total + squares(held[i][...], 1.0 / gain[:, lanes])
        mean = jnp.sum(total, axis=1, keepdims=True) * (1.0 / D)
        rstd[...] = jnp.broadcast_to(lax.rsqrt(mean + epsilon), rstd.shape)

    row = lax.broadcasted_iota(jnp.int32, (tokens, tokens), 0)
    col = lax.broadcasted_iota(jnp.int32, (tokens, tokens), 1)
    same = lax.rem(row, slot) == lax.rem(col, slot)
    part = pl.ds(pl.multiple_of(pl.program_id(0) * step, step), step)
    factor = jnp.concatenate([rstd[...]] * heads, axis=1)
    qkv = []
    for c in range(3):
        value = acc[c, :, part]
        for i in range(count):
            value = value + dot(held[i][...], ws[i][c, :, part])
        qkv.append((value * factor).astype(jnp.bfloat16))
    split = [
        (j, slice(j * tokens, (j + 1) * tokens), slice(h * HEAD, (h + 1) * HEAD))
        for h in range(heads)
        for j in range(ways)
    ]
    scores = [
        jnp.where(same, dot_nt(qkv[0][rows, cols], qkv[1][rows, cols]), -1e30)
        for _, rows, cols in split
    ]
    weights = [weighted(x) for x in scores]
    me = at[first + count]
    for (j, rows, cols), (w, r) in zip(split, weights):
        result = dot((w * r).astype(jnp.bfloat16), qkv[2][rows, cols]).astype(jnp.bfloat16)
        target = lax.rem(me + ways - j, ways)
        if tiled:
            out[:, target, :, cols] = result.reshape(out.shape[0], slot, HEAD)
        else:
            out[target, :, cols] = result


def temporal(arrays, shifts, at, first, gain, carried, tokens, ways, slot, tiled):
    rows = tokens * ways
    width = carried[0].shape[2]
    depths = [x.shape[-1] for x in arrays]
    frames = tokens // slot
    heads = math.gcd(width // HEAD, FINAL_HEADS)
    step = heads * HEAD
    if tiled:
        shape = (frames, ways, slot, width)
        out_spec = pl.BlockSpec((frames, ways, slot, step), lambda n, at: (0, 0, 0, n))
    else:
        shape = (ways, tokens, width)
        out_spec = pl.BlockSpec((ways, tokens, step), lambda n, at: (0, 0, n))
    operands = [*arrays, gain, *carried]
    out = pl.pallas_call(
        partial(
            temporal_kernel,
            first=first,
            shifts=shifts,
            heads=heads,
            tokens=tokens,
            ways=ways,
            slot=slot,
            tiled=tiled,
        ),
        out_shape=jax.ShapeDtypeStruct(shape, jnp.bfloat16),
        grid_spec=pltpu.PrefetchScalarGridSpec(
            num_scalar_prefetch=1,
            grid=(width // step,),
            in_specs=[VMEM] * len(operands),
            out_specs=out_spec,
            scratch_shapes=[pltpu.VMEM((rows, depth), jnp.bfloat16) for depth in depths]
            + [pltpu.VMEM((rows, HEAD), jnp.float32)],
        ),
        cost_estimate=pl.CostEstimate(
            flops=6 * rows * sum(depths) * width,
            bytes_accessed=2 * rows * width,
            transcendentals=rows * width,
        ),
        compiler_params=pltpu.CompilerParams(vmem_limit_bytes=16 << 20),
        name="temporal",
    )(at, *operands)
    if not tiled:
        out = out.reshape(ways, frames, slot, width).transpose(1, 0, 2, 3)
    return out


FINAL_HEADS = 6


def pack_kernel(at, q, k, v, out, sems, *, index):
    lanes = pl.ds(pl.multiple_of(at[index] * HEAD, HEAD), out.shape[2])
    copies = [
        pltpu.make_async_copy(ref.at[0, :, lanes], out.at[i], sems.at[i])
        for i, ref in enumerate((q, k, v))
    ]
    for copy in copies:
        copy.start()
    for copy in copies:
        copy.wait()


def pack(q, k, v, at, index, width):
    return pl.pallas_call(
        partial(pack_kernel, index=index),
        out_shape=pltpu.VMEM((3, q.shape[1], width), q.dtype),
        grid_spec=pltpu.PrefetchScalarGridSpec(
            num_scalar_prefetch=1,
            grid=(),
            in_specs=[pl.BlockSpec(memory_space=pl.ANY)] * 3,
            out_specs=VMEM,
            scratch_shapes=[pltpu.SemaphoreType.DMA((3,))],
        ),
        compiler_params=pltpu.CompilerParams(vmem_limit_bytes=8 << 20),
        name="pack",
    )(at, q, k, v)


def collect_kernel(*refs, picks):
    out = refs[-1]
    for n, (which, block) in enumerate(picks):
        out[n] = refs[which][block]


def collect(parts, picks):
    return pl.pallas_call(
        partial(collect_kernel, picks=tuple(picks)),
        out_shape=jax.ShapeDtypeStruct((len(picks), *parts[0].shape[1:]), parts[0].dtype),
        in_specs=[VMEM] * len(parts),
        out_specs=VMEM,
        compiler_params=pltpu.CompilerParams(vmem_limit_bytes=8 << 20),
        name="collect",
    )(*parts)


def assemble_kernel(at, *refs, places):
    out = refs[-1]
    frame = at[at.shape[0] - 1]
    for ref, keys in zip(refs[:-1], places):
        for n, key in enumerate(keys):
            if key is not None:
                out[key ^ frame] = ref[n]


def assemble(parts, places, at):
    count = sum(key is not None for keys in places for key in keys)
    return pl.pallas_call(
        partial(assemble_kernel, places=places),
        out_shape=jax.ShapeDtypeStruct((count, *parts[0].shape[1:]), parts[0].dtype),
        grid_spec=pltpu.PrefetchScalarGridSpec(
            num_scalar_prefetch=1,
            grid=(),
            in_specs=[VMEM] * len(parts),
            out_specs=VMEM,
        ),
        compiler_params=pltpu.CompilerParams(vmem_limit_bytes=8 << 20),
        name="assemble",
    )(at, *parts)


def stages(frames):
    pair = 2
    line = min(4, frames // pair)
    return line, frames // (line * pair), pair


def spread_by_permutes(outs, at, frames):
    line, side, pair = stages(frames)
    rest = side * pair

    def swap(x, key):
        return lax.ppermute(x, "frame", [(i, i ^ key) for i in range(frames)])

    lined = {0: outs[0]}
    for a in range(line - 1, 0, -1):
        lined[a] = swap(outs[a], a * rest)
    sided = {}
    for b in range(1, side):
        picks = [(a, b * pair + c) for a in range(line) for c in range(pair)]
        sided[b] = swap(collect([lined[a] for a in range(line)], picks), b * pair)
    parts = [lined[a] for a in range(line)] + [sided[b] for b in range(1, side)]
    picks = [(a, 1) for a in range(line)]
    picks += [(line + b - 1, a * pair + 1) for b in range(1, side) for a in range(line)]
    parts.append(swap(collect(parts, picks), 1))
    places = [(a * rest,) + (None,) * (rest - 1) for a in range(line)]
    places += [
        tuple(
            a * rest + b * pair if c == 0 else None for a in range(line) for c in range(pair)
        )
        for b in range(1, side)
    ]
    places.append(tuple(a * rest + b * pair + 1 for b in range(side) for a in range(line)))
    return assemble(parts, tuple(places), at)


def local(spatial_q, spatial_k, spatial_v, norm_gain, temporal_weight):
    frames = lax.axis_size("frame")
    ways = lax.axis_size("row")
    me = lax.axis_index("row").astype(jnp.int32)
    tokens = spatial_q.shape[1]
    slot = tokens // frames
    tiled = slot % 8 == 0
    width = temporal_weight.shape[2]
    group = width // HEAD
    hbm = lambda x: pltpu.with_memory_space_constraint(x, pltpu.HBM)
    weight = hbm(jnp.transpose(temporal_weight, (1, 0, 2)))
    spatial_q, spatial_k, spatial_v = (hbm(x) for x in (spatial_q, spatial_k, spatial_v))
    gain = norm_gain.reshape(1, -1)

    staged = three_chunks(group, ways, frames, slot)
    if staged:
        sizes = MIXED if group == sum(MIXED) else (group // 3, group // 3, group - 2 * (group // 3))
    else:
        first = max(1, group * 5 // 12)
        sizes = (first, group - first) if group > 1 else (1,)
    chunks = [(sum(sizes[:i]), size) for i, size in enumerate(sizes)]
    last = len(chunks) - 1
    behind = [lax.rem(me + ways - k, ways) * group + c for c, _ in chunks for k in range(ways)]
    ahead = [lax.rem(me + k, ways) * group + c for c, _ in chunks for k in range(ways)]
    table = jnp.stack(behind + ahead + [me, lax.axis_index("frame").astype(jnp.int32)])

    def shift(x, k):
        return lax.ppermute(x, "row", [(i, (i + k) % ways) for i in range(ways)])

    received = []
    for i, (_, size) in enumerate(chunks):
        parts = []
        for k in range(1, ways):
            index = len(behind) + i * ways + k
            packed = pack(spatial_q, spatial_k, spatial_v, table, index, size * HEAD)
            parts.append(shift(packed, k))
        received.append(parts)

    pieces = {}
    for i, parts in enumerate(received):
        lines = stages(frames)[0] if staged and i == 1 else 0
        out = spatial(
            spatial_q, spatial_k, spatial_v, parts, hbm(gain), table, i * ways, frames, lines
        )
        if lines:
            pieces[i, 0] = spread_by_permutes(out, table, frames)
        else:
            out = lax.all_to_all(out, "frame", split_axis=0, concat_axis=0, tiled=True)
            pieces[i, 0] = out
        for k in range(1, ways):
            pieces[i, k] = shift(pieces[i, 0], k)
    if not tiled:
        flat = lambda x: x.transpose(1, 0, 2, 3).reshape(ways, tokens, -1)
        pieces = {key: flat(x) for key, x in pieces.items()}

    early = [[(0, k)] for k in range(1, ways)] if last else []
    early.append([(i, 0) for i in range(last + 1)])
    final = [(i, k) for i in range(min(1, last), last + 1) for k in range(1, ways)]
    order = [g[0] for g in early] + final
    at = jnp.stack([behind[i * ways + k] for i, k in order] + [me])
    flat = [key for g in early for key in g]
    groups = tuple(tuple(flat.index(key) for key in g) for g in early)
    shared = dict(tokens=tokens, ways=ways, tiled=tiled)
    carried = project(
        groups,
        [pieces[key] for key in flat],
        tuple(k for _, k in flat),
        at,
        [chunks[i][1] * HEAD for i, _ in final],
        weight,
        gain,
        **shared,
    )
    arrays, shifts = [pieces[key] for key in final], tuple(k for _, k in final)
    out = temporal(arrays, shifts, at, len(early), gain, carried, slot=slot, **shared)
    out = out.reshape(frames * ways, slot, width)
    out = lax.all_to_all(out, ("frame", "row"), split_axis=0, concat_axis=0, tiled=True)
    out = out.reshape(frames, ways, slot, width).transpose(0, 2, 1, 3)
    return out.reshape(1, tokens, ways * width)


MIXED = (4, 4, 4)


def three_chunks(group, ways, frames, slot):
    return group >= 3 and ways == 2 and frames & (frames - 1) == 0 and slot % 8 == 0 and frames > 2


def solution(mesh):
    return jax.shard_map(
        local,
        mesh=mesh,
        in_specs=(
            P("frame", "row", None),
            P("frame", "row", None),
            P("frame", "row", None),
            P(),
            P(None, None, "row"),
        ),
        out_specs=P("frame", "row", None),
        check_vma=False,
    )
```

time: 99.3 us -> 112 us (1.13)
  starting transfers between devices: 19.5 us -> 29.3 us
  Pallas kernels: 25.1 us -> 29.4 us
    all_to_all x2, waiting for transfers between devices: 13.7 us -> 0.01 us  [local(): out = lax.all_to_all(out, 'frame', split_axis=0, concat_axis=0, tiled=True)]
    ppermute x0 -> x5, waiting for transfers between devices: none -> 8.63 us  [swap(): return lax.ppermute(x, 'frame', [(i, i ^ key) for i in range(frames)])]
    ppermute x0 -> x5, starting transfers between devices: none -> 8.08 us  [swap(): return lax.ppermute(x, 'frame', [(i, i ^ key) for i in range(frames)])]
    ppermute x4 -> x6, waiting for transfers between devices: 12.7 us -> 17.9 us  [shift(): return lax.ppermute(x, 'row', [(i, (i + k) % ways) for i in range(ways)])]
    pallas_call x6 -> x11, Pallas kernels: 25.2 us -> 29.4 us  [the longest x1 9.99 us: project(): pl.pallas_call(partial(project_kernel, groups=(*groups, *[None] * len(lat...]
    ppermute x4 -> x6, starting transfers between devices: 4.61 us -> 6.44 us  [shift(): return lax.ppermute(x, 'row', [(i, (i + k) % ways) for i in range(ways)])]
  transfers between devices with their start and end apart: 6 -> 13, of which waited for: 5 -> 8; matrix products, arithmetic and copies ran while one was open for 0% -> 0% of each run, Pallas kernels for 19% -> 17%
where the time goes in v4:
time: 112 us
  Pallas kernels  29.4 us (26%)
  starting transfers between devices  29.3 us (26%)
  waiting for transfers between devices  26.5 us (24%)
  blocking collectives  25.6 us (23%)
    all_to_all x1, blocking collectives, local(): lax.all_to_all(out, ('frame', 'row'), split_axis=0, concat_axis=0, tiled=...  25.6 us
    ppermute x6, waiting for transfers between devices, shift(): return lax.ppermute(x, 'row', [(i, (i + k) % ways) for i in range(ways)])  17.9 us
    all_to_all x2, starting transfers between devices, local(): out = lax.all_to_all(out, 'frame', split_axis=0, concat_axis=0, tiled=True)  14.8 us
    pallas_call x1, Pallas kernels, project(): pl.pallas_call(partial(project_kernel, groups=(*groups, *[None] * len(lat...  9.99 us
    pallas_call x3, Pallas kernels, spatial(): pl.pallas_call(partial(spatial_kernel, index=index, pool=tokens * ways //...  9.03 us
    ppermute x5, waiting for transfers between devices, swap(): return lax.ppermute(x, 'frame', [(i, i ^ key) for i in range(frames)])  8.63 us
    ppermute x5, starting transfers between devices, swap(): return lax.ppermute(x, 'frame', [(i, i ^ key) for i in range(frames)])  8.08 us
    ppermute x6, starting transfers between devices, shift(): return lax.ppermute(x, 'row', [(i, (i + k) % ways) for i in range(ways)])  6.44 us
  transfers between devices with their start and end apart: 13, of which 8 were waited for; matrix products, arithmetic and copies ran while one was open for 0% of the time, Pallas kernels for 17%

profile of v4, /device:TPU:1, one launch (start us, length us, event | category | flops | bytes accessed | tf_op | source)
XLA Modules:
  0.0 112.0 jit_solution(119786125187417267)
XLA Ops:
  0.0 0.1 stack.59.at
  0.1 1.6 %pack.5 = bf16[3,128,512]{2,1,0:T(8,128)(2,1)S(1)} custom-call(s32[14]{0:T(128)S(1)} %stack.59.at, bf16[1,128,3072]{2,1,0:T(8,128)(2,1)} %refs_0_.5, bf16[1,128,3072]{2,1,0:T(8,128)(2,1)} %refs_1_.5, bf16[1,128,3072]{2,1,0:T(8,128)(2,1)} %refs_2_.5), custom_call_target="tpu_custom_call" | custom-call | tf_op jit(solution)/shard_map/pack/pallas_call | solution.py:380
  1.7 2.1 %collective-permute-start.9 = (bf16[3,128,512]{2,1,0:T(8,128)(2,1)S(1)}, bf16[3,128,512]{2,1,0:T(8,128)(2,1)S(1)}, u32[]{:S(2)}, u32[]{:S(2)}) collective-permute-start(bf16[3,128,512]{2,1,0:T(8,128)(2,1)S(1)} %pack.5), channel_id=1, source_target_pairs={{0,1},{1,0},{2,3},{3,2},{4,5},{5,4},{6,7},{7,6},{8,9},{9,8},{10,11... | collective-permute-start | bytes 1179656 | tf_op jit(solution)/shard_map/ppermute | solution.py:499
  3.8 8.8 %collective-permute-done.9.refs_3_ = bf16[3,128,512]{2,1,0:T(8,128)(2,1)S(1)} collective-permute-done((bf16[3,128,512]{2,1,0:T(8,128)(2,1)S(1)}, bf16[3,128,512]{2,1,0:T(8,128)(2,1)S(1)}, u32[]{:S(2)}, u32[]{:S(2)}) %collective-permute-start.9) | collective-permute-done | bytes 393248 | tf_op jit(solution)/shard_map/ppermute | solution.py:499
  12.6 3.2 %spatial.5 = bf16[16,2,8,512]{3,2,1,0:T(8,128)(2,1)} custom-call(s32[14]{0:T(128)S(1)} %stack.59.at, bf16[1,128,3072]{2,1,0:T(8,128)(2,1)} %refs_0_.5, bf16[1,128,3072]{2,1,0:T(8,128)(2,1)} %refs_1_.5, bf16[1,128,3072]{2,1,0:T(8,128)(2,1)} %refs_2_.5, bf16[3,128,512]{2,1,0:T(8,128)(2,1)S(1)} %collective-permute-done.9.refs_3_, f32[1,3072]{1,0:T(1,128)} %bitcast.20), custom_call_target="tpu_custom_call" | custom-call | flops 167772160 | bytes 1310720 | tf_op jit(solution)/shard_map/spatial/pallas_call | solution.py:113
  15.9 7.4 %all-to-all-start.1 = ((bf16[16,2,8,512]{3,2,1,0:T(8,128)(2,1)}), bf16[16,2,8,512]{3,2,1,0:T(8,128)(2,1)S(1)}, u32[]{:S(2)}, u32[]{:S(2)}) async-start(bf16[16,2,8,512]{3,2,1,0:T(8,128)(2,1)} %spatial.5), calls=%async_computation.1 | async-start | bytes 524288 | tf_op jit(solution)/shard_map/all_to_all | solution.py:519
  23.2 1.6 %pack.4 = bf16[3,128,512]{2,1,0:T(8,128)(2,1)S(1)} custom-call(s32[14]{0:T(128)S(1)} %stack.59.at, bf16[1,128,3072]{2,1,0:T(8,128)(2,1)} %refs_0_.5, bf16[1,128,3072]{2,1,0:T(8,128)(2,1)} %refs_1_.5, bf16[1,128,3072]{2,1,0:T(8,128)(2,1)} %refs_2_.5), custom_call_target="tpu_custom_call" | custom-call | tf_op jit(solution)/shard_map/pack/pallas_call | solution.py:380
  24.8 0.0 copy-start
  24.8 1.3 %collective-permute-start.7 = (bf16[3,128,512]{2,1,0:T(8,128)(2,1)S(1)}, bf16[3,128,512]{2,1,0:T(8,128)(2,1)S(1)}, u32[]{:S(2)}, u32[]{:S(2)}) collective-permute-start(bf16[3,128,512]{2,1,0:T(8,128)(2,1)S(1)} %pack.4), channel_id=1, source_target_pairs={{0,1},{1,0},{2,3},{3,2},{4,5},{5,4},{6,7},{7,6},{8,9},{9,8},{10,11... | collective-permute-start | bytes 1179656 | tf_op jit(solution)/shard_map/ppermute | solution.py:499
  26.1 1.6 %pack.3 = bf16[3,128,512]{2,1,0:T(8,128)(2,1)S(1)} custom-call(s32[14]{0:T(128)S(1)} %stack.59.at, bf16[1,128,3072]{2,1,0:T(8,128)(2,1)} %refs_0_.5, bf16[1,128,3072]{2,1,0:T(8,128)(2,1)} %refs_1_.5, bf16[1,128,3072]{2,1,0:T(8,128)(2,1)} %refs_2_.5), custom_call_target="tpu_custom_call" | custom-call | tf_op jit(solution)/shard_map/pack/pallas_call | solution.py:380
  27.7 0.3 collective-permute-start
  28.0 7.4 %collective-permute-done.7.refs_3_ = bf16[3,128,512]{2,1,0:T(8,128)(2,1)S(1)} collective-permute-done((bf16[3,128,512]{2,1,0:T(8,128)(2,1)S(1)}, bf16[3,128,512]{2,1,0:T(8,128)(2,1)S(1)}, u32[]{:S(2)}, u32[]{:S(2)}) %collective-permute-start.7) | collective-permute-done | bytes 393248 | tf_op jit(solution)/shard_map/ppermute | solution.py:499
  35.5 3.2 %spatial.4 = bf16[16,2,8,512]{3,2,1,0:T(8,128)(2,1)} custom-call(s32[14]{0:T(128)S(1)} %stack.59.at, bf16[1,128,3072]{2,1,0:T(8,128)(2,1)} %refs_0_.5, bf16[1,128,3072]{2,1,0:T(8,128)(2,1)} %refs_1_.5, bf16[1,128,3072]{2,1,0:T(8,128)(2,1)} %refs_2_.5, bf16[3,128,512]{2,1,0:T(8,128)(2,1)S(1)} %collective-permute-done.7.refs_3_, f32[1,3072]{1,0:T(1,128)} %bitcast.21), custom_call_target="tpu_custom_call" | custom-call | flops 167772160 | bytes 1310720 | tf_op jit(solution)/shard_map/spatial/pallas_call | solution.py:113
  38.7 0.0 all-to-all-done.1.refs_1_
  38.7 7.4 %all-to-all-start = ((bf16[16,2,8,512]{3,2,1,0:T(8,128)(2,1)}), bf16[16,2,8,512]{3,2,1,0:T(8,128)(2,1)S(1)}, u32[]{:S(2)}, u32[]{:S(2)}) async-start(bf16[16,2,8,512]{3,2,1,0:T(8,128)(2,1)} %spatial.4), calls=%async_computation | async-start | bytes 524288 | tf_op jit(solution)/shard_map/all_to_all | solution.py:519
  46.2 0.0 collective-permute-done.refs_3_
  46.2 2.6 %spatial.3 = (bf16[4,2,8,512]{3,2,1,0:T(8,128)(2,1)S(1)}, bf16[4,2,8,512]{3,2,1,0:T(8,128)(2,1)S(1)}, bf16[4,2,8,512]{3,2,1,0:T(8,128)(2,1)S(1)}, bf16[4,2,8,512]{3,2,1,0:T(8,128)(2,1)S(1)}) custom-call(s32[14]{0:T(128)S(1)} %stack.59.at, bf16[1,128,3072]{2,1,0:T(8,128)(2,1)} %refs_0_.5, bf16[1,128,3072]{2,1,0:T(8,128)(2,1)} %refs_1_.5, ...), custom_call_target="tpu_custom_call" | custom-call | flops 167772160 | bytes 1310720 | tf_op jit(solution)/shard_map/spatial/pallas_call | solution.py:113
  48.7 1.4 %collective-permute-start.1 = (bf16[4,2,8,512]{3,2,1,0:T(8,128)(2,1)S(1)}, bf16[4,2,8,512]{3,2,1,0:T(8,128)(2,1)S(1)}, u32[]{:S(2)}, u32[]{:S(2)}) collective-permute-start(bf16[4,2,8,512]{3,2,1,0:T(8,128)(2,1)S(1)} %get-tuple-element.14), channel_id=1, source_target_pairs={{0,8},{2,10},{4,12},{6,14},{8,0},{10,2},{12,4},{14,6},{16,24},{18,... | collective-permute-start | bytes 196616 | tf_op jit(solution)/shard_map/ppermute | solution.py:448
  50.2 2.1 %collective-permute-start.2 = (bf16[4,2,8,512]{3,2,1,0:T(8,128)(2,1)S(1)}, bf16[4,2,8,512]{3,2,1,0:T(8,128)(2,1)S(1)}, u32[]{:S(2)}, u32[]{:S(2)}) collective-permute-start(bf16[4,2,8,512]{3,2,1,0:T(8,128)(2,1)S(1)} %get-tuple-element.15), channel_id=1, source_target_pairs={{0,16},{2,18},{4,20},{6,22},{8,24},{10,26},{12,28},{14,30},{16,0},... | collective-permute-start | bytes 196616 | tf_op jit(solution)/shard_map/ppermute | solution.py:448
  52.3 0.1 collective-permute-start.3
  52.4 1.9 %collective-permute-done.1.refs_1_ = bf16[4,2,8,512]{3,2,1,0:T(8,128)(2,1)S(1)} collective-permute-done((bf16[4,2,8,512]{3,2,1,0:T(8,128)(2,1)S(1)}, bf16[4,2,8,512]{3,2,1,0:T(8,128)(2,1)S(1)}, u32[]{:S(2)}, u32[]{:S(2)}) %collective-permute-start.1) | collective-permute-done | bytes 65568 | tf_op jit(solution)/shard_map/ppermute | solution.py:448
  54.2 2.6 %collective-permute-done.2.refs_2_ = bf16[4,2,8,512]{3,2,1,0:T(8,128)(2,1)S(1)} collective-permute-done((bf16[4,2,8,512]{3,2,1,0:T(8,128)(2,1)S(1)}, bf16[4,2,8,512]{3,2,1,0:T(8,128)(2,1)S(1)}, u32[]{:S(2)}, u32[]{:S(2)}) %collective-permute-start.2) | collective-permute-done | bytes 65568 | tf_op jit(solution)/shard_map/ppermute | solution.py:448
  56.8 1.9 %collective-permute-done.3.refs_3_ = bf16[4,2,8,512]{3,2,1,0:T(8,128)(2,1)S(1)} collective-permute-done((bf16[4,2,8,512]{3,2,1,0:T(8,128)(2,1)S(1)}, bf16[4,2,8,512]{3,2,1,0:T(8,128)(2,1)S(1)}, u32[]{:S(2)}, u32[]{:S(2)}) %collective-permute-start.3) | collective-permute-done | bytes 65568 | tf_op jit(solution)/shard_map/ppermute | solution.py:448
  58.7 1.2 %collective-permute-start.4 = (bf16[8,2,8,512]{3,2,1,0:T(8,128)(2,1)S(1)}, bf16[8,2,8,512]{3,2,1,0:T(8,128)(2,1)S(1)}, u32[]{:S(2)}, u32[]{:S(2)}) collective-permute-start(bf16[8,2,8,512]{3,2,1,0:T(8,128)(2,1)S(1)} %collect.2), channel_id=1, source_target_pairs={{0,4},{2,6},{4,0},{6,2},{8,12},{10,14},{12,8},{14,10},{16,20},{18,... | collective-permute-start | bytes 393224 | tf_op jit(solution)/shard_map/ppermute | solution.py:448
  59.9 1.2 %collective-permute-start.10 = (bf16[16,2,8,512]{3,2,1,0:T(8,128)(2,1)S(1)}, bf16[16,2,8,512]{3,2,1,0:T(8,128)(2,1)S(1)}, u32[]{:S(2)}, u32[]{:S(2)}) collective-permute-start(bf16[16,2,8,512]{3,2,1,0:T(8,128)(2,1)S(1)} %all-to-all-done.1.refs_1_), channel_id=1, source_target_pairs={{0,1},{1,0},{2,3},{3,2},{4,5},{5,4},{6,7},{7,6},{8,9},{9,8},{10,11... | collective-permute-start | bytes 786440 | tf_op jit(solution)/shard_map/ppermute | solution.py:499
  61.1 1.4 %collective-permute-done.4.refs_4_ = bf16[8,2,8,512]{3,2,1,0:T(8,128)(2,1)S(1)} collective-permute-done((bf16[8,2,8,512]{3,2,1,0:T(8,128)(2,1)S(1)}, bf16[8,2,8,512]{3,2,1,0:T(8,128)(2,1)S(1)}, u32[]{:S(2)}, u32[]{:S(2)}) %collective-permute-start.4) | collective-permute-done | bytes 131104 | tf_op jit(solution)/shard_map/ppermute | solution.py:448
  62.6 3.2 %collective-permute-start.5 = (bf16[8,2,8,512]{3,2,1,0:T(8,128)(2,1)S(1)}, bf16[8,2,8,512]{3,2,1,0:T(8,128)(2,1)S(1)}, u32[]{:S(2)}, u32[]{:S(2)}) collective-permute-start(bf16[8,2,8,512]{3,2,1,0:T(8,128)(2,1)S(1)} %collect.3), channel_id=1, source_target_pairs={{0,2},{2,0},{4,6},{6,4},{8,10},{10,8},{12,14},{14,12},{16,18},{18,... | collective-permute-start | bytes 393224 | tf_op jit(solution)/shard_map/ppermute | solution.py:448
  65.8 0.1 stack.52.at
  65.9 0.9 collective-permute-done.5.refs_5_
  66.8 0.6 assemble.1.refs_2_
  67.4 1.3 %collective-permute-start.6 = (bf16[16,2,8,512]{3,2,1,0:T(8,128)(2,1)S(1)}, bf16[16,2,8,512]{3,2,1,0:T(8,128)(2,1)S(1)}, u32[]{:S(2)}, u32[]{:S(2)}) collective-permute-start(bf16[16,2,8,512]{3,2,1,0:T(8,128)(2,1)S(1)} %assemble.1.refs_2_), channel_id=1, source_target_pairs={{0,1},{1,0},{2,3},{3,2},{4,5},{5,4},{6,7},{7,6},{8,9},{9,8},{10,11... | collective-permute-start | bytes 786440 | tf_op jit(solution)/shard_map/ppermute | solution.py:499
  68.6 0.0 all-to-all-done.refs_3_
  68.6 0.3 collective-permute-start.8
  68.9 0.0 collective-permute-done.10.refs_0_
  68.9 0.0 copy-done
  68.9 10.0 %project.1 = (f32[3,256,1536]{2,1,0:T(8,128)S(1)}, f32[256,128]{1,0:T(8,128)S(1)}, bf16[3,512,1536]{2,1,0:T(8,128)(2,1)S(1)}, bf16[3,512,1536]{2,1,0:T(8,128)(2,1)S(1)}) custom-call(s32[5]{0:T(128)S(1)} %stack.52.at, bf16[16,2,8,512]{3,2,1,0:T(8,128)(2,1)S(1)} %collective-permute-done.10.refs_0_, bf16[16,2,8,512]{3,2,1,0:T(8,128)(2,1)S(1)} %all-to-all-done.1.refs_1_, ...), custom_call_target="tpu_custom_call" | custom-call | flops 4831838208 | bytes 28311552 | tf_op jit(solution)/shard_map/project/pallas_call | solution.py:233
  78.9 0.0 collective-permute-done.6.refs_0_
  78.9 1.6 %collective-permute-done.8.refs_1_ = bf16[16,2,8,512]{3,2,1,0:T(8,128)(2,1)S(1)} collective-permute-done((bf16[16,2,8,512]{3,2,1,0:T(8,128)(2,1)S(1)}, bf16[16,2,8,512]{3,2,1,0:T(8,128)(2,1)S(1)}, u32[]{:S(2)}, u32[]{:S(2)}) %collective-permute-start.8) | collective-permute-done | bytes 262176 | tf_op jit(solution)/shard_map/ppermute | solution.py:499
  80.5 5.0 %temporal.1 = bf16[16,2,8,1536]{3,2,1,0:T(8,128)(2,1)S(1)} custom-call(s32[5]{0:T(128)S(1)} %stack.52.at, bf16[16,2,8,512]{3,2,1,0:T(8,128)(2,1)S(1)} %collective-permute-done.6.refs_0_, bf16[16,2,8,512]{3,2,1,0:T(8,128)(2,1)S(1)} %collective-permute-done.8.refs_1_, f32[1,3072]{1,0:T(1,128)S(1)} %bitcast.24, f32[3,256,1536]{2,1,0:T(8,128)S(1)} %get-tuple-element.17.refs_3_, ...), custom_call_target="tpu_custom_call" | custom-call | flops 2415919104 | bytes 786432 | tf_op jit(solution)/shard_map/temporal/pallas_call | solution.py:331
  85.5 25.6 %all_to_all.15 = bf16[32,8,1536]{2,1,0:T(8,128)(2,1)S(1)} all-to-all(bf16[32,8,1536]{2,1,0:T(8,128)(2,1)S(1)} %bitcast.19), channel_id=1, replica_groups=mesh['frame'=16,'row'=2] {'frame','row'}, dimensions={0} | all-to-all | bytes 1572864 | tf_op jit(solution)/shard_map/all_to_all | solution.py:548
  111.1 0.9 copy.7
  (2 shorter events, 0.0 us)
Async XLA Ops:
  1.7 10.9 %collective-permute-start.9 = (bf16[3,128,512]{2,1,0:T(8,128)(2,1)S(1)}, bf16[3,128,512]{2,1,0:T(8,128)(2,1)S(1)}, u32[]{:S(2)}, u32[]{:S(2)}) collective-permute-start(bf16[3,128,512]{2,1,0:T(8,128)(2,1)S(1)} %pack.5), channel_id=1, source_target_pairs={{0,1},{1,0},{2,3},{3,2},{4,5},{5,4},{6,7},{7,6},{8,9},{9,8},{10,11... | collective-permute-start | bytes 1179656 | tf_op jit(solution)/shard_map/ppermute | solution.py:499
  15.9 22.9 %all-to-all-start.1 = ((bf16[16,2,8,512]{3,2,1,0:T(8,128)(2,1)}), bf16[16,2,8,512]{3,2,1,0:T(8,128)(2,1)S(1)}, u32[]{:S(2)}, u32[]{:S(2)}) async-start(bf16[16,2,8,512]{3,2,1,0:T(8,128)(2,1)} %spatial.5), calls=%async_computation.1 | async-start | bytes 524288 | tf_op jit(solution)/shard_map/all_to_all | solution.py:519
  24.8 44.1 %copy-start = (f32[3072]{0:T(1024)S(1)}, f32[3072]{0:T(1024)}, u32[]{:S(2)}) copy-start(f32[3072]{0:T(1024)} %param.8) | copy-start | bytes 36868
  24.8 10.6 %collective-permute-start.7 = (bf16[3,128,512]{2,1,0:T(8,128)(2,1)S(1)}, bf16[3,128,512]{2,1,0:T(8,128)(2,1)S(1)}, u32[]{:S(2)}, u32[]{:S(2)}) collective-permute-start(bf16[3,128,512]{2,1,0:T(8,128)(2,1)S(1)} %pack.4), channel_id=1, source_target_pairs={{0,1},{1,0},{2,3},{3,2},{4,5},{5,4},{6,7},{7,6},{8,9},{9,8},{10,11... | collective-permute-start | bytes 1179656 | tf_op jit(solution)/shard_map/ppermute | solution.py:499
  27.7 18.4 %collective-permute-start = (bf16[3,128,512]{2,1,0:T(8,128)(2,1)S(1)}, bf16[3,128,512]{2,1,0:T(8,128)(2,1)S(1)}, u32[]{:S(2)}, u32[]{:S(2)}) collective-permute-start(bf16[3,128,512]{2,1,0:T(8,128)(2,1)S(1)} %pack.3), channel_id=1, source_target_pairs={{0,1},{1,0},{2,3},{3,2},{4,5},{5,4},{6,7},{7,6},{8,9},{9,8},{10,11... | collective-permute-start | bytes 1179656 | tf_op jit(solution)/shard_map/ppermute | solution.py:499
  38.7 29.9 %all-to-all-start = ((bf16[16,2,8,512]{3,2,1,0:T(8,128)(2,1)}), bf16[16,2,8,512]{3,2,1,0:T(8,128)(2,1)S(1)}, u32[]{:S(2)}, u32[]{:S(2)}) async-start(bf16[16,2,8,512]{3,2,1,0:T(8,128)(2,1)} %spatial.4), calls=%async_computation | async-start | bytes 524288 | tf_op jit(solution)/shard_map/all_to_all | solution.py:519
  48.7 5.5 %collective-permute-start.1 = (bf16[4,2,8,512]{3,2,1,0:T(8,128)(2,1)S(1)}, bf16[4,2,8,512]{3,2,1,0:T(8,128)(2,1)S(1)}, u32[]{:S(2)}, u32[]{:S(2)}) collective-permute-start(bf16[4,2,8,512]{3,2,1,0:T(8,128)(2,1)S(1)} %get-tuple-element.14), channel_id=1, source_target_pairs={{0,8},{2,10},{4,12},{6,14},{8,0},{10,2},{12,4},{14,6},{16,24},{18,... | collective-permute-start | bytes 196616 | tf_op jit(solution)/shard_map/ppermute | solution.py:448
  50.2 6.6 %collective-permute-start.2 = (bf16[4,2,8,512]{3,2,1,0:T(8,128)(2,1)S(1)}, bf16[4,2,8,512]{3,2,1,0:T(8,128)(2,1)S(1)}, u32[]{:S(2)}, u32[]{:S(2)}) collective-permute-start(bf16[4,2,8,512]{3,2,1,0:T(8,128)(2,1)S(1)} %get-tuple-element.15), channel_id=1, source_target_pairs={{0,16},{2,18},{4,20},{6,22},{8,24},{10,26},{12,28},{14,30},{16,0},... | collective-permute-start | bytes 196616 | tf_op jit(solution)/shard_map/ppermute | solution.py:448
  52.3 6.4 %collective-permute-start.3 = (bf16[4,2,8,512]{3,2,1,0:T(8,128)(2,1)S(1)}, bf16[4,2,8,512]{3,2,1,0:T(8,128)(2,1)S(1)}, u32[]{:S(2)}, u32[]{:S(2)}) collective-permute-start(bf16[4,2,8,512]{3,2,1,0:T(8,128)(2,1)S(1)} %get-tuple-element.16), channel_id=1, source_target_pairs={{0,24},{2,26},{4,28},{6,30},{8,16},{10,18},{12,20},{14,22},{16,8},... | collective-permute-start | bytes 196616 | tf_op jit(solution)/shard_map/ppermute | solution.py:448
  58.7 3.9 %collective-permute-start.4 = (bf16[8,2,8,512]{3,2,1,0:T(8,128)(2,1)S(1)}, bf16[8,2,8,512]{3,2,1,0:T(8,128)(2,1)S(1)}, u32[]{:S(2)}, u32[]{:S(2)}) collective-permute-start(bf16[8,2,8,512]{3,2,1,0:T(8,128)(2,1)S(1)} %collect.2), channel_id=1, source_target_pairs={{0,4},{2,6},{4,0},{6,2},{8,12},{10,14},{12,8},{14,10},{16,20},{18,... | collective-permute-start | bytes 393224 | tf_op jit(solution)/shard_map/ppermute | solution.py:448
  59.9 9.0 %collective-permute-start.10 = (bf16[16,2,8,512]{3,2,1,0:T(8,128)(2,1)S(1)}, bf16[16,2,8,512]{3,2,1,0:T(8,128)(2,1)S(1)}, u32[]{:S(2)}, u32[]{:S(2)}) collective-permute-start(bf16[16,2,8,512]{3,2,1,0:T(8,128)(2,1)S(1)} %all-to-all-done.1.refs_1_), channel_id=1, source_target_pairs={{0,1},{1,0},{2,3},{3,2},{4,5},{5,4},{6,7},{7,6},{8,9},{9,8},{10,11... | collective-permute-start | bytes 786440 | tf_op jit(solution)/shard_map/ppermute | solution.py:499
  62.6 4.2 %collective-permute-start.5 = (bf16[8,2,8,512]{3,2,1,0:T(8,128)(2,1)S(1)}, bf16[8,2,8,512]{3,2,1,0:T(8,128)(2,1)S(1)}, u32[]{:S(2)}, u32[]{:S(2)}) collective-permute-start(bf16[8,2,8,512]{3,2,1,0:T(8,128)(2,1)S(1)} %collect.3), channel_id=1, source_target_pairs={{0,2},{2,0},{4,6},{6,4},{8,10},{10,8},{12,14},{14,12},{16,18},{18,... | collective-permute-start | bytes 393224 | tf_op jit(solution)/shard_map/ppermute | solution.py:448
  67.4 11.5 %collective-permute-start.6 = (bf16[16,2,8,512]{3,2,1,0:T(8,128)(2,1)S(1)}, bf16[16,2,8,512]{3,2,1,0:T(8,128)(2,1)S(1)}, u32[]{:S(2)}, u32[]{:S(2)}) collective-permute-start(bf16[16,2,8,512]{3,2,1,0:T(8,128)(2,1)S(1)} %assemble.1.refs_2_), channel_id=1, source_target_pairs={{0,1},{1,0},{2,3},{3,2},{4,5},{5,4},{6,7},{7,6},{8,9},{9,8},{10,11... | collective-permute-start | bytes 786440 | tf_op jit(solution)/shard_map/ppermute | solution.py:499
  68.6 11.9 %collective-permute-start.8 = (bf16[16,2,8,512]{3,2,1,0:T(8,128)(2,1)S(1)}, bf16[16,2,8,512]{3,2,1,0:T(8,128)(2,1)S(1)}, u32[]{:S(2)}, u32[]{:S(2)}) collective-permute-start(bf16[16,2,8,512]{3,2,1,0:T(8,128)(2,1)S(1)} %all-to-all-done.refs_3_), channel_id=1, source_target_pairs={{0,1},{1,0},{2,3},{3,2},{4,5},{5,4},{6,7},{7,6},{8,9},{9,8},{10,11... | collective-permute-start | bytes 786440 | tf_op jit(solution)/shard_map/ppermute | solution.py:499

commit v5 on v4

--- a/solution.py
+++ b/solution.py
@@ -99,7 +99,7 @@
             target[...] = out[n * size : (n + 1) * size]
 
 
-TOGETHER = 4
+TOGETHER = 3
 
 
 def spatial(q, k, v, received, gain, at, index, frames, lines=0):
@@ -376,7 +376,31 @@
         copy.wait()
 
 
-def pack(q, k, v, at, index, width):
+def pack_blocks_kernel(at, q, k, v, out):
+    for i, ref in enumerate((q, k, v)):
+        out[i] = ref[0]
+
+
+def pack(q, k, v, at, index, width, aligned):
+    if aligned:
+        blocks = width // HEAD
+        return pl.pallas_call(
+            pack_blocks_kernel,
+            out_shape=jax.ShapeDtypeStruct((3, q.shape[1], width), q.dtype),
+            grid_spec=pltpu.PrefetchScalarGridSpec(
+                num_scalar_prefetch=1,
+                grid=(1,),
+                in_specs=[
+                    pl.BlockSpec(
+                        (1, q.shape[1], width), lambda i, at: (0, 0, at[index] // blocks)
+                    )
+                ]
+                * 3,
+                out_specs=pl.BlockSpec((3, q.shape[1], width), lambda i, at: (0, 0, 0)),
+            ),
+            compiler_params=pltpu.CompilerParams(vmem_limit_bytes=8 << 20),
+            name="pack",
+        )(at, q, k, v)
     return pl.pallas_call(
         partial(pack_kernel, index=index),
         out_shape=pltpu.VMEM((3, q.shape[1], width), q.dtype),
@@ -491,6 +515,7 @@
         sizes = (first, group - first) if group > 1 else (1,)
     chunks = [(sum(sizes[:i]), size) for i, size in enumerate(sizes)]
     last = len(chunks) - 1
+    aligned = lambda i: group % chunks[i][1] == 0 and chunks[i][0] % chunks[i][1] == 0
     behind = [lax.rem(me + ways - k, ways) * group + c for c, _ in chunks for k in range(ways)]
     ahead = [lax.rem(me + k, ways) * group + c for c, _ in chunks for k in range(ways)]
     table = jnp.stack(behind + ahead + [me, lax.axis_index("frame").astype(jnp.int32)])
@@ -503,7 +528,7 @@
         parts = []
         for k in range(1, ways):
             index = len(behind) + i * ways + k
-            packed = pack(spatial_q, spatial_k, spatial_v, table, index, size * HEAD)
+            packed = pack(spatial_q, spatial_k, spatial_v, table, index, size * HEAD, aligned(i))
             parts.append(shift(packed, k))
         received.append(parts)
 
@@ -550,7 +575,7 @@
     return out.reshape(1, tokens, ways * width)
 
 
-MIXED = (4, 4, 4)
+MIXED = (6, 3, 3)
 
 
 def three_chunks(group, ways, frames, slot):

time: 112 us -> 111 us (level)
  starting transfers between devices: 29.3 us -> 26.3 us
  waiting for transfers between devices: 26.5 us -> 28 us
    all_to_all x2, waiting for transfers between devices: 0.01 us -> 7.12 us  [local(): out = lax.all_to_all(out, 'frame', split_axis=0, concat_axis=0, tiled=True)]
    ppermute x6, waiting for transfers between devices: 17.9 us -> 13 us  [shift(): return lax.ppermute(x, 'row', [(i, (i + k) % ways) for i in range(ways)])]
    all_to_all x2, starting transfers between devices: 14.8 us -> 11.8 us  [local(): out = lax.all_to_all(out, 'frame', split_axis=0, concat_axis=0, tiled=True)]
  transfers between devices with their start and end apart: 13 -> 13, of which waited for: 8 -> 7; matrix products, arithmetic and copies ran while one was open for 0% -> 0% of each run, Pallas kernels for 17% -> 18%
where the time goes in v5:
time: 111 us; the launch traced here: 110 us
  Pallas kernels  29.9 us (27%)
  waiting for transfers between devices  28 us (25%)
  starting transfers between devices  26.3 us (24%)
  blocking collectives  24.8 us (22%)
    all_to_all x1, blocking collectives, local(): lax.all_to_all(out, ('frame', 'row'), split_axis=0, concat_axis=0, tiled=...  24.8 us
    ppermute x6, waiting for transfers between devices, shift(): return lax.ppermute(x, 'row', [(i, (i + k) % ways) for i in range(ways)])  13 us
    all_to_all x2, starting transfers between devices, local(): out = lax.all_to_all(out, 'frame', split_axis=0, concat_axis=0, tiled=True)  11.8 us
    pallas_call x1, Pallas kernels, project(): pl.pallas_call(partial(project_kernel, groups=(*groups, *[None] * len(lat...  10.2 us
    pallas_call x3, Pallas kernels, spatial(): pl.pallas_call(partial(spatial_kernel, index=index, pool=tokens * ways //...  9.33 us
    ppermute x5, starting transfers between devices, swap(): return lax.ppermute(x, 'frame', [(i, i ^ key) for i in range(frames)])  8.08 us
    ppermute x5, waiting for transfers between devices, swap(): return lax.ppermute(x, 'frame', [(i, i ^ key) for i in range(frames)])  7.88 us
    all_to_all x2, waiting for transfers between devices, local(): out = lax.all_to_all(out, 'frame', split_axis=0, concat_axis=0, tiled=True)  7.12 us
  transfers between devices with their start and end apart: 13, of which 7 were waited for; matrix products, arithmetic and copies ran while one was open for 0% of the time, Pallas kernels for 18%

profile of v5, /device:TPU:1, one launch (start us, length us, event | category | flops | bytes accessed | tf_op | source)
XLA Modules:
  0.0 110.2 jit_solution(14889198106445145245)
XLA Ops:
  0.0 0.1 stack.59.at
  0.1 1.7 %pack.5 = bf16[3,128,768]{2,1,0:T(8,128)(2,1)S(1)} custom-call(s32[14]{0:T(128)S(1)} %stack.59.at, bf16[1,128,3072]{2,1,0:T(8,128)(2,1)} %refs_0_.5, bf16[1,128,3072]{2,1,0:T(8,128)(2,1)} %refs_1_.5, bf16[1,128,3072]{2,1,0:T(8,128)(2,1)} %refs_2_.5), custom_call_target="tpu_custom_call" | custom-call | tf_op jit(solution)/shard_map/pack/pallas_call | solution.py:387
  1.8 2.1 %collective-permute-start.9 = (bf16[3,128,768]{2,1,0:T(8,128)(2,1)S(1)}, bf16[3,128,768]{2,1,0:T(8,128)(2,1)S(1)}, u32[]{:S(2)}, u32[]{:S(2)}) collective-permute-start(bf16[3,128,768]{2,1,0:T(8,128)(2,1)S(1)} %pack.5), channel_id=1, source_target_pairs={{0,1},{1,0},{2,3},{3,2},{4,5},{5,4},{6,7},{7,6},{8,9},{9,8},{10,11... | collective-permute-start | bytes 1769480 | tf_op jit(solution)/shard_map/ppermute | solution.py:524
  3.9 13.0 %collective-permute-done.9.refs_3_ = bf16[3,128,768]{2,1,0:T(8,128)(2,1)S(1)} collective-permute-done((bf16[3,128,768]{2,1,0:T(8,128)(2,1)S(1)}, bf16[3,128,768]{2,1,0:T(8,128)(2,1)S(1)}, u32[]{:S(2)}, u32[]{:S(2)}) %collective-permute-start.9) | collective-permute-done | bytes 589856 | tf_op jit(solution)/shard_map/ppermute | solution.py:524
  16.9 3.9 %spatial.5 = bf16[16,2,8,768]{3,2,1,0:T(8,128)(2,1)} custom-call(s32[14]{0:T(128)S(1)} %stack.59.at, bf16[1,128,3072]{2,1,0:T(8,128)(2,1)} %refs_0_.5, bf16[1,128,3072]{2,1,0:T(8,128)(2,1)} %refs_1_.5, bf16[1,128,3072]{2,1,0:T(8,128)(2,1)} %refs_2_.5, bf16[3,128,768]{2,1,0:T(8,128)(2,1)S(1)} %collective-permute-done.9.refs_3_, f32[1,3072]{1,0:T(1,128)} %bitcast.20), custom_call_target="tpu_custom_call" | custom-call | flops 251658240 | bytes 1966080 | tf_op jit(solution)/shard_map/spatial/pallas_call | solution.py:113
  20.8 7.4 %all-to-all-start.1 = ((bf16[16,2,8,768]{3,2,1,0:T(8,128)(2,1)}), bf16[16,2,8,768]{3,2,1,0:T(8,128)(2,1)S(1)}, u32[]{:S(2)}, u32[]{:S(2)}) async-start(bf16[16,2,8,768]{3,2,1,0:T(8,128)(2,1)} %spatial.5), calls=%async_computation.1 | async-start | bytes 786432 | tf_op jit(solution)/shard_map/all_to_all | solution.py:544
  28.2 1.6 %pack.4 = bf16[3,128,384]{2,1,0:T(8,128)(2,1)S(1)} custom-call(s32[14]{0:T(128)S(1)} %stack.59.at, bf16[1,128,3072]{2,1,0:T(8,128)(2,1)} %refs_0_.5, bf16[1,128,3072]{2,1,0:T(8,128)(2,1)} %refs_1_.5, bf16[1,128,3072]{2,1,0:T(8,128)(2,1)} %refs_2_.5), custom_call_target="tpu_custom_call" | custom-call | tf_op jit(solution)/shard_map/pack/pallas_call | solution.py:387
  29.8 0.0 copy-start
  29.8 1.3 %collective-permute-start.7 = (bf16[3,128,384]{2,1,0:T(8,128)(2,1)S(1)}, bf16[3,128,384]{2,1,0:T(8,128)(2,1)S(1)}, u32[]{:S(2)}, u32[]{:S(2)}) collective-permute-start(bf16[3,128,384]{2,1,0:T(8,128)(2,1)S(1)} %pack.4), channel_id=1, source_target_pairs={{0,1},{1,0},{2,3},{3,2},{4,5},{5,4},{6,7},{7,6},{8,9},{9,8},{10,11... | collective-permute-start | bytes 884744 | tf_op jit(solution)/shard_map/ppermute | solution.py:524
  31.0 1.6 %pack.3 = bf16[3,128,384]{2,1,0:T(8,128)(2,1)S(1)} custom-call(s32[14]{0:T(128)S(1)} %stack.59.at, bf16[1,128,3072]{2,1,0:T(8,128)(2,1)} %refs_0_.5, bf16[1,128,3072]{2,1,0:T(8,128)(2,1)} %refs_1_.5, bf16[1,128,3072]{2,1,0:T(8,128)(2,1)} %refs_2_.5), custom_call_target="tpu_custom_call" | custom-call | tf_op jit(solution)/shard_map/pack/pallas_call | solution.py:387
  32.6 0.3 collective-permute-start
  32.9 7.1 %all-to-all-done.1.refs_1_ = bf16[16,2,8,768]{3,2,1,0:T(8,128)(2,1)S(1)} async-done(((bf16[16,2,8,768]{3,2,1,0:T(8,128)(2,1)}), bf16[16,2,8,768]{3,2,1,0:T(8,128)(2,1)S(1)}, u32[]{:S(2)}, u32[]{:S(2)}) %all-to-all-start.1) | async-done | bytes 393248 | tf_op jit(solution)/shard_map/all_to_all | solution.py:544
  40.1 1.2 %collective-permute-start.10 = (bf16[16,2,8,768]{3,2,1,0:T(8,128)(2,1)S(1)}, bf16[16,2,8,768]{3,2,1,0:T(8,128)(2,1)S(1)}, u32[]{:S(2)}, u32[]{:S(2)}) collective-permute-start(bf16[16,2,8,768]{3,2,1,0:T(8,128)(2,1)S(1)} %all-to-all-done.1.refs_1_), channel_id=1, source_target_pairs={{0,1},{1,0},{2,3},{3,2},{4,5},{5,4},{6,7},{7,6},{8,9},{9,8},{10,11... | collective-permute-start | bytes 1179656 | tf_op jit(solution)/shard_map/ppermute | solution.py:524
  41.3 0.0 collective-permute-done.7.refs_3_
  41.3 3.0 %spatial.4 = bf16[16,2,8,384]{3,2,1,0:T(8,128)(2,1)} custom-call(s32[14]{0:T(128)S(1)} %stack.59.at, bf16[1,128,3072]{2,1,0:T(8,128)(2,1)} %refs_0_.5, bf16[1,128,3072]{2,1,0:T(8,128)(2,1)} %refs_1_.5, bf16[1,128,3072]{2,1,0:T(8,128)(2,1)} %refs_2_.5, bf16[3,128,384]{2,1,0:T(8,128)(2,1)S(1)} %collective-permute-done.7.refs_3_, f32[1,3072]{1,0:T(1,128)} %bitcast.21), custom_call_target="tpu_custom_call" | custom-call | flops 125829120 | bytes 983040 | tf_op jit(solution)/shard_map/spatial/pallas_call | solution.py:113
  44.3 4.5 %all-to-all-start = ((bf16[16,2,8,384]{3,2,1,0:T(8,128)(2,1)}), bf16[16,2,8,384]{3,2,1,0:T(8,128)(2,1)S(1)}, u32[]{:S(2)}, u32[]{:S(2)}) async-start(bf16[16,2,8,384]{3,2,1,0:T(8,128)(2,1)} %spatial.4), calls=%async_computation | async-start | bytes 393216 | tf_op jit(solution)/shard_map/all_to_all | solution.py:544
  48.8 0.0 collective-permute-done.refs_3_
  48.8 2.4 %spatial.3 = (bf16[4,2,8,384]{3,2,1,0:T(8,128)(2,1)S(1)}, bf16[4,2,8,384]{3,2,1,0:T(8,128)(2,1)S(1)}, bf16[4,2,8,384]{3,2,1,0:T(8,128)(2,1)S(1)}, bf16[4,2,8,384]{3,2,1,0:T(8,128)(2,1)S(1)}) custom-call(s32[14]{0:T(128)S(1)} %stack.59.at, bf16[1,128,3072]{2,1,0:T(8,128)(2,1)} %refs_0_.5, bf16[1,128,3072]{2,1,0:T(8,128)(2,1)} %refs_1_.5, ...), custom_call_target="tpu_custom_call" | custom-call | flops 125829120 | bytes 983040 | tf_op jit(solution)/shard_map/spatial/pallas_call | solution.py:113
  51.2 1.4 %collective-permute-start.1 = (bf16[4,2,8,384]{3,2,1,0:T(8,128)(2,1)S(1)}, bf16[4,2,8,384]{3,2,1,0:T(8,128)(2,1)S(1)}, u32[]{:S(2)}, u32[]{:S(2)}) collective-permute-start(bf16[4,2,8,384]{3,2,1,0:T(8,128)(2,1)S(1)} %get-tuple-element.14), channel_id=1, source_target_pairs={{0,8},{2,10},{4,12},{6,14},{8,0},{10,2},{12,4},{14,6},{16,24},{18,... | collective-permute-start | bytes 147464 | tf_op jit(solution)/shard_map/ppermute | solution.py:472
  52.6 2.1 %collective-permute-start.2 = (bf16[4,2,8,384]{3,2,1,0:T(8,128)(2,1)S(1)}, bf16[4,2,8,384]{3,2,1,0:T(8,128)(2,1)S(1)}, u32[]{:S(2)}, u32[]{:S(2)}) collective-permute-start(bf16[4,2,8,384]{3,2,1,0:T(8,128)(2,1)S(1)} %get-tuple-element.15), channel_id=1, source_target_pairs={{0,16},{2,18},{4,20},{6,22},{8,24},{10,26},{12,28},{14,30},{16,0},... | collective-permute-start | bytes 147464 | tf_op jit(solution)/shard_map/ppermute | solution.py:472
  54.7 0.1 collective-permute-start.3
  54.8 0.6 collective-permute-done.1.refs_1_
  55.4 2.0 %collective-permute-done.2.refs_2_ = bf16[4,2,8,384]{3,2,1,0:T(8,128)(2,1)S(1)} collective-permute-done((bf16[4,2,8,384]{3,2,1,0:T(8,128)(2,1)S(1)}, bf16[4,2,8,384]{3,2,1,0:T(8,128)(2,1)S(1)}, u32[]{:S(2)}, u32[]{:S(2)}) %collective-permute-start.2) | collective-permute-done | bytes 49184 | tf_op jit(solution)/shard_map/ppermute | solution.py:472
  57.5 2.1 %collective-permute-done.3.refs_3_ = bf16[4,2,8,384]{3,2,1,0:T(8,128)(2,1)S(1)} collective-permute-done((bf16[4,2,8,384]{3,2,1,0:T(8,128)(2,1)S(1)}, bf16[4,2,8,384]{3,2,1,0:T(8,128)(2,1)S(1)}, u32[]{:S(2)}, u32[]{:S(2)}) %collective-permute-start.3) | collective-permute-done | bytes 49184 | tf_op jit(solution)/shard_map/ppermute | solution.py:472
  59.6 1.2 %collective-permute-start.4 = (bf16[8,2,8,384]{3,2,1,0:T(8,128)(2,1)S(1)}, bf16[8,2,8,384]{3,2,1,0:T(8,128)(2,1)S(1)}, u32[]{:S(2)}, u32[]{:S(2)}) collective-permute-start(bf16[8,2,8,384]{3,2,1,0:T(8,128)(2,1)S(1)} %collect.2), channel_id=1, source_target_pairs={{0,4},{2,6},{4,0},{6,2},{8,12},{10,14},{12,8},{14,10},{16,20},{18,... | collective-permute-start | bytes 294920 | tf_op jit(solution)/shard_map/ppermute | solution.py:472
  60.8 2.3 %collective-permute-done.4.refs_4_ = bf16[8,2,8,384]{3,2,1,0:T(8,128)(2,1)S(1)} collective-permute-done((bf16[8,2,8,384]{3,2,1,0:T(8,128)(2,1)S(1)}, bf16[8,2,8,384]{3,2,1,0:T(8,128)(2,1)S(1)}, u32[]{:S(2)}, u32[]{:S(2)}) %collective-permute-start.4) | collective-permute-done | bytes 98336 | tf_op jit(solution)/shard_map/ppermute | solution.py:472
  63.1 3.2 %collective-permute-start.5 = (bf16[8,2,8,384]{3,2,1,0:T(8,128)(2,1)S(1)}, bf16[8,2,8,384]{3,2,1,0:T(8,128)(2,1)S(1)}, u32[]{:S(2)}, u32[]{:S(2)}) collective-permute-start(bf16[8,2,8,384]{3,2,1,0:T(8,128)(2,1)S(1)} %collect.3), channel_id=1, source_target_pairs={{0,2},{2,0},{4,6},{6,4},{8,10},{10,8},{12,14},{14,12},{16,18},{18,... | collective-permute-start | bytes 294920 | tf_op jit(solution)/shard_map/ppermute | solution.py:472
  66.3 0.1 stack.52.at
  66.4 0.9 collective-permute-done.5.refs_5_
  67.3 0.6 assemble.1.refs_2_
  67.8 1.3 %collective-permute-start.6 = (bf16[16,2,8,384]{3,2,1,0:T(8,128)(2,1)S(1)}, bf16[16,2,8,384]{3,2,1,0:T(8,128)(2,1)S(1)}, u32[]{:S(2)}, u32[]{:S(2)}) collective-permute-start(bf16[16,2,8,384]{3,2,1,0:T(8,128)(2,1)S(1)} %assemble.1.refs_2_), channel_id=1, source_target_pairs={{0,1},{1,0},{2,3},{3,2},{4,5},{5,4},{6,7},{7,6},{8,9},{9,8},{10,11... | collective-permute-start | bytes 589832 | tf_op jit(solution)/shard_map/ppermute | solution.py:524
  69.1 0.0 all-to-all-done.refs_3_
  69.1 0.3 collective-permute-start.8
  69.4 0.0 collective-permute-done.10.refs_0_
  69.4 0.0 copy-done
  69.4 10.2 %project.1 = (f32[3,256,1536]{2,1,0:T(8,128)S(1)}, f32[256,128]{1,0:T(8,128)S(1)}, bf16[3,384,1536]{2,1,0:T(8,128)(2,1)S(1)}, bf16[3,384,1536]{2,1,0:T(8,128)(2,1)S(1)}) custom-call(s32[5]{0:T(128)S(1)} %stack.52.at, bf16[16,2,8,768]{3,2,1,0:T(8,128)(2,1)S(1)} %collective-permute-done.10.refs_0_, bf16[16,2,8,768]{3,2,1,0:T(8,128)(2,1)S(1)} %all-to-all-done.1.refs_1_, ...), custom_call_target="tpu_custom_call" | custom-call | flops 5435817984 | bytes 28311552 | tf_op jit(solution)/shard_map/project/pallas_call | solution.py:233
  79.6 0.0 collective-permute-done.6.refs_0_
  79.6 0.0 collective-permute-done.8.refs_1_
  79.6 4.9 %temporal.1 = bf16[16,2,8,1536]{3,2,1,0:T(8,128)(2,1)S(1)} custom-call(s32[5]{0:T(128)S(1)} %stack.52.at, bf16[16,2,8,384]{3,2,1,0:T(8,128)(2,1)S(1)} %collective-permute-done.6.refs_0_, bf16[16,2,8,384]{3,2,1,0:T(8,128)(2,1)S(1)} %collective-permute-done.8.refs_1_, f32[1,3072]{1,0:T(1,128)S(1)} %bitcast.24, f32[3,256,1536]{2,1,0:T(8,128)S(1)} %get-tuple-element.17.refs_3_, ...), custom_call_target="tpu_custom_call" | custom-call | flops 1811939328 | bytes 786432 | tf_op jit(solution)/shard_map/temporal/pallas_call | solution.py:331
  84.6 24.8 %all_to_all.15 = bf16[32,8,1536]{2,1,0:T(8,128)(2,1)S(1)} all-to-all(bf16[32,8,1536]{2,1,0:T(8,128)(2,1)S(1)} %bitcast.19), channel_id=1, replica_groups=mesh['frame'=16,'row'=2] {'frame','row'}, dimensions={0} | all-to-all | bytes 1572864 | tf_op jit(solution)/shard_map/all_to_all | solution.py:573
  109.4 0.9 copy.7
  (2 shorter events, 0.0 us)
Async XLA Ops:
  1.8 15.1 %collective-permute-start.9 = (bf16[3,128,768]{2,1,0:T(8,128)(2,1)S(1)}, bf16[3,128,768]{2,1,0:T(8,128)(2,1)S(1)}, u32[]{:S(2)}, u32[]{:S(2)}) collective-permute-start(bf16[3,128,768]{2,1,0:T(8,128)(2,1)S(1)} %pack.5), channel_id=1, source_target_pairs={{0,1},{1,0},{2,3},{3,2},{4,5},{5,4},{6,7},{7,6},{8,9},{9,8},{10,11... | collective-permute-start | bytes 1769480 | tf_op jit(solution)/shard_map/ppermute | solution.py:524
  20.8 19.2 %all-to-all-start.1 = ((bf16[16,2,8,768]{3,2,1,0:T(8,128)(2,1)}), bf16[16,2,8,768]{3,2,1,0:T(8,128)(2,1)S(1)}, u32[]{:S(2)}, u32[]{:S(2)}) async-start(bf16[16,2,8,768]{3,2,1,0:T(8,128)(2,1)} %spatial.5), calls=%async_computation.1 | async-start | bytes 786432 | tf_op jit(solution)/shard_map/all_to_all | solution.py:544
  29.8 39.6 %copy-start = (f32[3072]{0:T(1024)S(1)}, f32[3072]{0:T(1024)}, u32[]{:S(2)}) copy-start(f32[3072]{0:T(1024)} %param.8) | copy-start | bytes 36868
  29.8 11.5 %collective-permute-start.7 = (bf16[3,128,384]{2,1,0:T(8,128)(2,1)S(1)}, bf16[3,128,384]{2,1,0:T(8,128)(2,1)S(1)}, u32[]{:S(2)}, u32[]{:S(2)}) collective-permute-start(bf16[3,128,384]{2,1,0:T(8,128)(2,1)S(1)} %pack.4), channel_id=1, source_target_pairs={{0,1},{1,0},{2,3},{3,2},{4,5},{5,4},{6,7},{7,6},{8,9},{9,8},{10,11... | collective-permute-start | bytes 884744 | tf_op jit(solution)/shard_map/ppermute | solution.py:524
  32.6 16.2 %collective-permute-start = (bf16[3,128,384]{2,1,0:T(8,128)(2,1)S(1)}, bf16[3,128,384]{2,1,0:T(8,128)(2,1)S(1)}, u32[]{:S(2)}, u32[]{:S(2)}) collective-permute-start(bf16[3,128,384]{2,1,0:T(8,128)(2,1)S(1)} %pack.3), channel_id=1, source_target_pairs={{0,1},{1,0},{2,3},{3,2},{4,5},{5,4},{6,7},{7,6},{8,9},{9,8},{10,11... | collective-permute-start | bytes 884744 | tf_op jit(solution)/shard_map/ppermute | solution.py:524
  40.1 29.3 %collective-permute-start.10 = (bf16[16,2,8,768]{3,2,1,0:T(8,128)(2,1)S(1)}, bf16[16,2,8,768]{3,2,1,0:T(8,128)(2,1)S(1)}, u32[]{:S(2)}, u32[]{:S(2)}) collective-permute-start(bf16[16,2,8,768]{3,2,1,0:T(8,128)(2,1)S(1)} %all-to-all-done.1.refs_1_), channel_id=1, source_target_pairs={{0,1},{1,0},{2,3},{3,2},{4,5},{5,4},{6,7},{7,6},{8,9},{9,8},{10,11... | collective-permute-start | bytes 1179656 | tf_op jit(solution)/shard_map/ppermute | solution.py:524
  44.3 24.8 %all-to-all-start = ((bf16[16,2,8,384]{3,2,1,0:T(8,128)(2,1)}), bf16[16,2,8,384]{3,2,1,0:T(8,128)(2,1)S(1)}, u32[]{:S(2)}, u32[]{:S(2)}) async-start(bf16[16,2,8,384]{3,2,1,0:T(8,128)(2,1)} %spatial.4), calls=%async_computation | async-start | bytes 393216 | tf_op jit(solution)/shard_map/all_to_all | solution.py:544
  51.2 4.2 %collective-permute-start.1 = (bf16[4,2,8,384]{3,2,1,0:T(8,128)(2,1)S(1)}, bf16[4,2,8,384]{3,2,1,0:T(8,128)(2,1)S(1)}, u32[]{:S(2)}, u32[]{:S(2)}) collective-permute-start(bf16[4,2,8,384]{3,2,1,0:T(8,128)(2,1)S(1)} %get-tuple-element.14), channel_id=1, source_target_pairs={{0,8},{2,10},{4,12},{6,14},{8,0},{10,2},{12,4},{14,6},{16,24},{18,... | collective-permute-start | bytes 147464 | tf_op jit(solution)/shard_map/ppermute | solution.py:472
  52.6 4.9 %collective-permute-start.2 = (bf16[4,2,8,384]{3,2,1,0:T(8,128)(2,1)S(1)}, bf16[4,2,8,384]{3,2,1,0:T(8,128)(2,1)S(1)}, u32[]{:S(2)}, u32[]{:S(2)}) collective-permute-start(bf16[4,2,8,384]{3,2,1,0:T(8,128)(2,1)S(1)} %get-tuple-element.15), channel_id=1, source_target_pairs={{0,16},{2,18},{4,20},{6,22},{8,24},{10,26},{12,28},{14,30},{16,0},... | collective-permute-start | bytes 147464 | tf_op jit(solution)/shard_map/ppermute | solution.py:472
  54.7 4.8 %collective-permute-start.3 = (bf16[4,2,8,384]{3,2,1,0:T(8,128)(2,1)S(1)}, bf16[4,2,8,384]{3,2,1,0:T(8,128)(2,1)S(1)}, u32[]{:S(2)}, u32[]{:S(2)}) collective-permute-start(bf16[4,2,8,384]{3,2,1,0:T(8,128)(2,1)S(1)} %get-tuple-element.16), channel_id=1, source_target_pairs={{0,24},{2,26},{4,28},{6,30},{8,16},{10,18},{12,20},{14,22},{16,8},... | collective-permute-start | bytes 147464 | tf_op jit(solution)/shard_map/ppermute | solution.py:472
  59.6 3.5 %collective-permute-start.4 = (bf16[8,2,8,384]{3,2,1,0:T(8,128)(2,1)S(1)}, bf16[8,2,8,384]{3,2,1,0:T(8,128)(2,1)S(1)}, u32[]{:S(2)}, u32[]{:S(2)}) collective-permute-start(bf16[8,2,8,384]{3,2,1,0:T(8,128)(2,1)S(1)} %collect.2), channel_id=1, source_target_pairs={{0,4},{2,6},{4,0},{6,2},{8,12},{10,14},{12,8},{14,10},{16,20},{18,... | collective-permute-start | bytes 294920 | tf_op jit(solution)/shard_map/ppermute | solution.py:472
  63.1 4.2 %collective-permute-start.5 = (bf16[8,2,8,384]{3,2,1,0:T(8,128)(2,1)S(1)}, bf16[8,2,8,384]{3,2,1,0:T(8,128)(2,1)S(1)}, u32[]{:S(2)}, u32[]{:S(2)}) collective-permute-start(bf16[8,2,8,384]{3,2,1,0:T(8,128)(2,1)S(1)} %collect.3), channel_id=1, source_target_pairs={{0,2},{2,0},{4,6},{6,4},{8,10},{10,8},{12,14},{14,12},{16,18},{18,... | collective-permute-start | bytes 294920 | tf_op jit(solution)/shard_map/ppermute | solution.py:472
  67.8 11.8 %collective-permute-start.6 = (bf16[16,2,8,384]{3,2,1,0:T(8,128)(2,1)S(1)}, bf16[16,2,8,384]{3,2,1,0:T(8,128)(2,1)S(1)}, u32[]{:S(2)}, u32[]{:S(2)}) collective-permute-start(bf16[16,2,8,384]{3,2,1,0:T(8,128)(2,1)S(1)} %assemble.1.refs_2_), channel_id=1, source_target_pairs={{0,1},{1,0},{2,3},{3,2},{4,5},{5,4},{6,7},{7,6},{8,9},{9,8},{10,11... | collective-permute-start | bytes 589832 | tf_op jit(solution)/shard_map/ppermute | solution.py:524
  69.1 10.5 %collective-permute-start.8 = (bf16[16,2,8,384]{3,2,1,0:T(8,128)(2,1)S(1)}, bf16[16,2,8,384]{3,2,1,0:T(8,128)(2,1)S(1)}, u32[]{:S(2)}, u32[]{:S(2)}) collective-permute-start(bf16[16,2,8,384]{3,2,1,0:T(8,128)(2,1)S(1)} %all-to-all-done.refs_3_), channel_id=1, source_target_pairs={{0,1},{1,0},{2,3},{3,2},{4,5},{5,4},{6,7},{7,6},{8,9},{9,8},{10,11... | collective-permute-start | bytes 589832 | tf_op jit(solution)/shard_map/ppermute | solution.py:524

commit v6 on v4

--- a/solution.py
+++ b/solution.py
@@ -172,10 +172,11 @@
         column += depth
 
 
-def project_kernel(at, *refs, groups, shifts, depths, tokens, ways, tiled):
+def project_kernel(at, *refs, groups, places, shifts, depths, carried, tokens, ways, tiled):
     xs = refs[: len(shifts)]
-    weight, gain, acc, ss = refs[len(shifts) : len(shifts) + 4]
-    rest = refs[len(shifts) + 4 :]
+    weight, gain = refs[len(shifts) : len(shifts) + 2]
+    before, refs = refs[len(shifts) + 2 :][: 2 * carried], refs[len(shifts) + 2 + 2 * carried :]
+    acc, ss, *rest = refs
     kept = rest[: len(groups) - sum(g is not None for g in groups)]
     sems = rest[-1]
     used = [g for g in groups if g is not None]
@@ -184,7 +185,7 @@
     targets = [*buffers, *kept]
     copies = []
     for i, target in enumerate(targets):
-        rows = pl.ds(pl.multiple_of(at[i] * HEAD, HEAD), target.shape[1])
+        rows = pl.ds(pl.multiple_of(at[places[i]] * HEAD, HEAD), target.shape[1])
         for c in range(3):
             copies.append(
                 pltpu.make_async_copy(weight.at[c, rows, :], target.at[c], sems.at[3 * i + c])
@@ -193,7 +194,7 @@
         copy.start()
     width = weight.shape[2]
     tile = width // 3 if width % 3 == 0 else width
-    total = None
+    total = before[1][...] if carried else None
     for i, members in enumerate(used):
         hold(
             held[i],
@@ -204,7 +205,7 @@
             ways,
             tiled,
         )
-        lanes = pl.ds(pl.multiple_of(at[i] * HEAD, HEAD), held[i].shape[1])
+        lanes = pl.ds(pl.multiple_of(at[places[i]] * HEAD, HEAD), held[i].shape[1])
         part = squares(held[i][...], 1.0 / gain[:, lanes])
         total = part if total is None else total + part
         for c in range(3):
@@ -215,7 +216,7 @@
                 cols = slice(n, n + tile)
                 value = dot(held[i][...], buffers[i][c, :, cols])
                 if i == 0:
-                    acc[c, :, cols] = value
+                    acc[c, :, cols] = before[0][c, :, cols] + value if carried else value
                 else:
                     acc[c, :, cols] += value
     ss[...] = total
@@ -225,7 +226,7 @@
         copy.wait()
 
 
-def project(groups, arrays, shifts, at, later, weight, gain, tokens, ways, tiled):
+def project(groups, places, arrays, shifts, at, later, carried, weight, gain, tokens, ways, tiled):
     rows = tokens * ways
     width = weight.shape[2]
     depths = [x.shape[-1] for x in arrays]
@@ -234,8 +235,10 @@
         partial(
             project_kernel,
             groups=(*groups, *[None] * len(later)),
+            places=places,
             shifts=shifts,
             depths=depths,
+            carried=bool(carried),
             tokens=tokens,
             ways=ways,
             tiled=tiled,
@@ -248,7 +251,9 @@
         grid_spec=pltpu.PrefetchScalarGridSpec(
             num_scalar_prefetch=1,
             grid=(),
-            in_specs=[VMEM] * len(arrays) + [pl.BlockSpec(memory_space=pl.ANY), VMEM],
+            in_specs=[VMEM] * len(arrays)
+            + [pl.BlockSpec(memory_space=pl.ANY)]
+            + [VMEM] * (1 + len(carried)),
             out_specs=(VMEM,) * (2 + len(later)),
             scratch_shapes=[pltpu.VMEM((rows, depth), jnp.bfloat16) for depth in sums]
             + [pltpu.VMEM((3, depth, width), weight.dtype) for depth in sums]
@@ -259,12 +264,15 @@
             bytes_accessed=6 * (sum(sums) + sum(later)) * width,
             transcendentals=0,
         ),
+        input_output_aliases=(
+            {len(arrays) + 3: 0, len(arrays) + 4: 1} if carried else {}
+        ),
         compiler_params=pltpu.CompilerParams(vmem_limit_bytes=32 << 20),
         name="project",
-    )(at, *arrays, weight, gain)
-
-
-def temporal_kernel(at, *refs, first, shifts, heads, tokens, ways, slot, tiled):
+    )(at, *arrays, weight, gain, *carried)
+
+
+def temporal_kernel(at, *refs, places, shifts, heads, tokens, ways, slot, tiled):
     count = len(shifts)
     xs = refs[:count]
     gain, acc, ss = refs[count : count + 3]
@@ -278,7 +286,7 @@
         for i in range(count):
             depth = ws[i].shape[1]
             hold(held[i], [xs[i]], [depth], [shifts[i]], tokens, ways, tiled)
-            lanes = pl.ds(pl.multiple_of(at[first + i] * HEAD, HEAD), depth)
+            lanes = pl.ds(pl.multiple_of(at[places[i]] * HEAD, HEAD), depth)
             total = total + squares(held[i][...], 1.0 / gain[:, lanes])
         mean = jnp.sum(total, axis=1, keepdims=True) * (1.0 / D)
         rstd[...] = jnp.broadcast_to(lax.rsqrt(mean + epsilon), rstd.shape)
@@ -304,7 +312,7 @@
         for _, rows, cols in split
     ]
     weights = [weighted(x) for x in scores]
-    me = at[first + count]
+    me = at[at.shape[0] - 2]
     for (j, rows, cols), (w, r) in zip(split, weights):
         result = dot((w * r).astype(jnp.bfloat16), qkv[2][rows, cols]).astype(jnp.bfloat16)
         target = lax.rem(me + ways - j, ways)
@@ -314,7 +322,7 @@
             out[target, :, cols] = result
 
 
-def temporal(arrays, shifts, at, first, gain, carried, tokens, ways, slot, tiled):
+def temporal(arrays, shifts, at, places, gain, carried, tokens, ways, slot, tiled):
     rows = tokens * ways
     width = carried[0].shape[2]
     depths = [x.shape[-1] for x in arrays]
@@ -331,7 +339,7 @@
     out = pl.pallas_call(
         partial(
             temporal_kernel,
-            first=first,
+            places=places,
             shifts=shifts,
             heads=heads,
             tokens=tokens,
@@ -509,7 +517,7 @@
 
     pieces = {}
     for i, parts in enumerate(received):
-        lines = stages(frames)[0] if staged and i == 1 else 0
+        lines = stages(frames)[0] if staged and i != 1 else 0
         out = spatial(
             spatial_q, spatial_k, spatial_v, parts, hbm(gain), table, i * ways, frames, lines
         )
@@ -524,26 +532,33 @@
         flat = lambda x: x.transpose(1, 0, 2, 3).reshape(ways, tokens, -1)
         pieces = {key: flat(x) for key, x in pieces.items()}
 
-    early = [[(0, k)] for k in range(1, ways)] if last else []
-    early.append([(i, 0) for i in range(last + 1)])
-    final = [(i, k) for i in range(min(1, last), last + 1) for k in range(1, ways)]
-    order = [g[0] for g in early] + final
-    at = jnp.stack([behind[i * ways + k] for i, k in order] + [me])
-    flat = [key for g in early for key in g]
-    groups = tuple(tuple(flat.index(key) for key in g) for g in early)
+    others = lambda i: [[(i, k)] for k in range(1, ways)]
+    if staged:
+        steps = [[[(0, 0), (1, 0)]], others(0), [[(2, 0)]] + others(1)]
+    else:
+        steps = [[key for i in range(last) for key in others(i)] + [[(i, 0) for i in range(last + 1)]]]
+    final = [g[0] for g in others(last)]
+    place = lambda key: key[0] * ways + key[1]
     shared = dict(tokens=tokens, ways=ways, tiled=tiled)
-    carried = project(
-        groups,
-        [pieces[key] for key in flat],
-        tuple(k for _, k in flat),
-        at,
-        [chunks[i][1] * HEAD for i, _ in final],
-        weight,
-        gain,
-        **shared,
-    )
+    carried = ()
+    for n, wanted in enumerate(steps):
+        flat = [key for g in wanted for key in g]
+        later = final if n == len(steps) - 1 else []
+        carried = project(
+            tuple(tuple(flat.index(key) for key in g) for g in wanted),
+            tuple(place(key) for key in [g[0] for g in wanted] + later),
+            [pieces[key] for key in flat],
+            tuple(k for _, k in flat),
+            table,
+            [chunks[i][1] * HEAD for i, _ in later],
+            carried,
+            weight,
+            gain,
+            **shared,
+        )
     arrays, shifts = [pieces[key] for key in final], tuple(k for _, k in final)
-    out = temporal(arrays, shifts, at, len(early), gain, carried, slot=slot, **shared)
+    places = tuple(place(key) for key in final)
+    out = temporal(arrays, shifts, table, places, gain, carried, slot=slot, **shared)
     out = out.reshape(frames * ways, slot, width)
     out = lax.all_to_all(out, ("frame", "row"), split_axis=0, concat_axis=0, tiled=True)
     out = out.reshape(frames, ways, slot, width).transpose(0, 2, 1, 3)

time: 112 us -> 106 us (0.946)
  waiting for transfers between devices: 26.5 us -> 14.7 us
  Pallas kernels: 29.4 us -> 33.5 us
  starting transfers between devices: 29.3 us -> 30.9 us
    ppermute x5 -> x10, starting transfers between devices: 8.08 us -> 16 us  [swap(): return lax.ppermute(x, 'frame', [(i, i ^ key) for i in range(frames)])]
    ppermute x6, waiting for transfers between devices: 17.9 us -> 10.5 us  [shift(): return lax.ppermute(x, 'row', [(i, (i + k) % ways) for i in range(ways)])]
    all_to_all x2 -> x1, starting transfers between devices: 14.8 us -> 8.49 us  [local(): out = lax.all_to_all(out, 'frame', split_axis=0, concat_axis=0, tiled=True)]
    pallas_call x1 -> x3, Pallas kernels: 9.99 us -> 15.4 us  [project(): pl.pallas_call(partial(project_kernel, groups=(*groups, *[None] * len(lat...]
    ppermute x5 -> x10, waiting for transfers between devices: 8.63 us -> 4.19 us  [swap(): return lax.ppermute(x, 'frame', [(i, i ^ key) for i in range(frames)])]
    pallas_call x1, Pallas kernels: 4.99 us -> 3.76 us  [temporal(): pl.pallas_call(partial(temporal_kernel, places=places, shifts=shifts, hea...]
  transfers between devices with their start and end apart: 13 -> 17, of which waited for: 8 -> 5; matrix products, arithmetic and copies ran while one was open for 0% -> 0% of each run, Pallas kernels for 17% -> 27%
where the time goes in v6:
time: 106 us; the launch traced here: 105 us
  Pallas kernels  33.5 us (32%)
  starting transfers between devices  30.9 us (29%)
  blocking collectives  25.1 us (24%)
  waiting for transfers between devices  14.7 us (14%)
    all_to_all x1, blocking collectives, local(): lax.all_to_all(out, ('frame', 'row'), split_axis=0, concat_axis=0, tiled=...  25.1 us
    ppermute x10, starting transfers between devices, swap(): return lax.ppermute(x, 'frame', [(i, i ^ key) for i in range(frames)])  16 us
    pallas_call x3, Pallas kernels, project(): pl.pallas_call(partial(project_kernel, groups=(*groups, *[None] * len(lat...  15.4 us
    ppermute x6, waiting for transfers between devices, shift(): return lax.ppermute(x, 'row', [(i, (i + k) % ways) for i in range(ways)])  10.5 us
    all_to_all x1, starting transfers between devices, local(): out = lax.all_to_all(out, 'frame', split_axis=0, concat_axis=0, tiled=True)  8.49 us
    pallas_call x3, Pallas kernels, spatial(): pl.pallas_call(partial(spatial_kernel, index=index, pool=tokens * ways //...  8.37 us
    ppermute x6, starting transfers between devices, shift(): return lax.ppermute(x, 'row', [(i, (i + k) % ways) for i in range(ways)])  6.5 us
    pallas_call x3, Pallas kernels, pack(): pl.pallas_call(partial(pack_kernel, index=index), out_shape=pltpu.VMEM((3...  4.81 us
  transfers between devices with their start and end apart: 17, of which 5 were waited for; matrix products, arithmetic and copies ran while one was open for 0% of the time, Pallas kernels for 27%

profile of v6, /device:TPU:1, one launch (start us, length us, event | category | flops | bytes accessed | tf_op | source)
XLA Modules:
  0.0 105.4 jit_solution(12116530853205599995)
XLA Ops:
  0.0 0.1 stack.50.at
  0.1 1.6 %pack.4 = bf16[3,128,512]{2,1,0:T(8,128)(2,1)S(1)} custom-call(s32[14]{0:T(128)S(1)} %stack.50.at, bf16[1,128,3072]{2,1,0:T(8,128)(2,1)} %refs_0_.5, bf16[1,128,3072]{2,1,0:T(8,128)(2,1)} %refs_1_.5, bf16[1,128,3072]{2,1,0:T(8,128)(2,1)} %refs_2_.5), custom_call_target="tpu_custom_call" | custom-call | tf_op jit(solution)/shard_map/pack/pallas_call | solution.py:388
  1.7 2.1 %collective-permute-start.7 = (bf16[3,128,512]{2,1,0:T(8,128)(2,1)S(1)}, bf16[3,128,512]{2,1,0:T(8,128)(2,1)S(1)}, u32[]{:S(2)}, u32[]{:S(2)}) collective-permute-start(bf16[3,128,512]{2,1,0:T(8,128)(2,1)S(1)} %pack.4), channel_id=1, source_target_pairs={{0,1},{1,0},{2,3},{3,2},{4,5},{5,4},{6,7},{7,6},{8,9},{9,8},{10,11... | collective-permute-start | bytes 1179656 | tf_op jit(solution)/shard_map/ppermute | solution.py:507
  3.8 1.6 %pack.5 = bf16[3,128,512]{2,1,0:T(8,128)(2,1)S(1)} custom-call(s32[14]{0:T(128)S(1)} %stack.50.at, bf16[1,128,3072]{2,1,0:T(8,128)(2,1)} %refs_0_.5, bf16[1,128,3072]{2,1,0:T(8,128)(2,1)} %refs_1_.5, bf16[1,128,3072]{2,1,0:T(8,128)(2,1)} %refs_2_.5), custom_call_target="tpu_custom_call" | custom-call | tf_op jit(solution)/shard_map/pack/pallas_call | solution.py:388
  5.4 0.1 collective-permute-start.9
  5.5 1.6 %pack.3 = bf16[3,128,512]{2,1,0:T(8,128)(2,1)S(1)} custom-call(s32[14]{0:T(128)S(1)} %stack.50.at, bf16[1,128,3072]{2,1,0:T(8,128)(2,1)} %refs_0_.5, bf16[1,128,3072]{2,1,0:T(8,128)(2,1)} %refs_1_.5, bf16[1,128,3072]{2,1,0:T(8,128)(2,1)} %refs_2_.5), custom_call_target="tpu_custom_call" | custom-call | tf_op jit(solution)/shard_map/pack/pallas_call | solution.py:388
  7.1 1.5 %collective-permute-start = (bf16[3,128,512]{2,1,0:T(8,128)(2,1)S(1)}, bf16[3,128,512]{2,1,0:T(8,128)(2,1)S(1)}, u32[]{:S(2)}, u32[]{:S(2)}) collective-permute-start(bf16[3,128,512]{2,1,0:T(8,128)(2,1)S(1)} %pack.3), channel_id=1, source_target_pairs={{0,1},{1,0},{2,3},{3,2},{4,5},{5,4},{6,7},{7,6},{8,9},{9,8},{10,11... | collective-permute-start | bytes 1179656 | tf_op jit(solution)/shard_map/ppermute | solution.py:507
  8.6 4.0 %collective-permute-done.7.refs_3_ = bf16[3,128,512]{2,1,0:T(8,128)(2,1)S(1)} collective-permute-done((bf16[3,128,512]{2,1,0:T(8,128)(2,1)S(1)}, bf16[3,128,512]{2,1,0:T(8,128)(2,1)S(1)}, u32[]{:S(2)}, u32[]{:S(2)}) %collective-permute-start.7) | collective-permute-done | bytes 393248 | tf_op jit(solution)/shard_map/ppermute | solution.py:507
  12.6 3.2 %spatial.4 = bf16[16,2,8,512]{3,2,1,0:T(8,128)(2,1)} custom-call(s32[14]{0:T(128)S(1)} %stack.50.at, bf16[1,128,3072]{2,1,0:T(8,128)(2,1)} %refs_0_.5, bf16[1,128,3072]{2,1,0:T(8,128)(2,1)} %refs_1_.5, bf16[1,128,3072]{2,1,0:T(8,128)(2,1)} %refs_2_.5, bf16[3,128,512]{2,1,0:T(8,128)(2,1)S(1)} %collective-permute-done.7.refs_3_, f32[1,3072]{1,0:T(1,128)} %bitcast.20), custom_call_target="tpu_custom_call" | custom-call | flops 167772160 | bytes 1310720 | tf_op jit(solution)/shard_map/spatial/pallas_call | solution.py:113
  15.9 0.0 copy-start
  15.9 8.5 %all-to-all-start = ((bf16[16,2,8,512]{3,2,1,0:T(8,128)(2,1)}), bf16[16,2,8,512]{3,2,1,0:T(8,128)(2,1)S(1)}, u32[]{:S(2)}, u32[]{:S(2)}) async-start(bf16[16,2,8,512]{3,2,1,0:T(8,128)(2,1)} %spatial.4), calls=%async_computation | async-start | bytes 524288 | tf_op jit(solution)/shard_map/all_to_all | solution.py:527
  24.4 0.0 collective-permute-done.9.refs_3_
  24.4 2.6 %spatial.5 = (bf16[4,2,8,512]{3,2,1,0:T(8,128)(2,1)S(1)}, bf16[4,2,8,512]{3,2,1,0:T(8,128)(2,1)S(1)}, bf16[4,2,8,512]{3,2,1,0:T(8,128)(2,1)S(1)}, bf16[4,2,8,512]{3,2,1,0:T(8,128)(2,1)S(1)}) custom-call(s32[14]{0:T(128)S(1)} %stack.50.at, bf16[1,128,3072]{2,1,0:T(8,128)(2,1)} %refs_0_.5, bf16[1,128,3072]{2,1,0:T(8,128)(2,1)} %refs_1_.5, ...), custom_call_target="tpu_custom_call" | custom-call | flops 167772160 | bytes 1310720 | tf_op jit(solution)/shard_map/spatial/pallas_call | solution.py:113
  26.9 1.4 %collective-permute-start.10 = (bf16[4,2,8,512]{3,2,1,0:T(8,128)(2,1)S(1)}, bf16[4,2,8,512]{3,2,1,0:T(8,128)(2,1)S(1)}, u32[]{:S(2)}, u32[]{:S(2)}) collective-permute-start(bf16[4,2,8,512]{3,2,1,0:T(8,128)(2,1)S(1)} %get-tuple-element.25), channel_id=1, source_target_pairs={{0,8},{2,10},{4,12},{6,14},{8,0},{10,2},{12,4},{14,6},{16,24},{18,... | collective-permute-start | bytes 196616 | tf_op jit(solution)/shard_map/ppermute | solution.py:456
  28.4 2.1 %collective-permute-start.11 = (bf16[4,2,8,512]{3,2,1,0:T(8,128)(2,1)S(1)}, bf16[4,2,8,512]{3,2,1,0:T(8,128)(2,1)S(1)}, u32[]{:S(2)}, u32[]{:S(2)}) collective-permute-start(bf16[4,2,8,512]{3,2,1,0:T(8,128)(2,1)S(1)} %get-tuple-element.26), channel_id=1, source_target_pairs={{0,16},{2,18},{4,20},{6,22},{8,24},{10,26},{12,28},{14,30},{16,0},... | collective-permute-start | bytes 196616 | tf_op jit(solution)/shard_map/ppermute | solution.py:456
  30.5 0.1 collective-permute-start.12
  30.6 0.0 collective-permute-done.refs_3_
  30.6 2.6 %spatial.3 = (bf16[4,2,8,512]{3,2,1,0:T(8,128)(2,1)S(1)}, bf16[4,2,8,512]{3,2,1,0:T(8,128)(2,1)S(1)}, bf16[4,2,8,512]{3,2,1,0:T(8,128)(2,1)S(1)}, bf16[4,2,8,512]{3,2,1,0:T(8,128)(2,1)S(1)}) custom-call(s32[14]{0:T(128)S(1)} %stack.50.at, bf16[1,128,3072]{2,1,0:T(8,128)(2,1)} %refs_0_.5, bf16[1,128,3072]{2,1,0:T(8,128)(2,1)} %refs_1_.5, ...), custom_call_target="tpu_custom_call" | custom-call | flops 167772160 | bytes 1310720 | tf_op jit(solution)/shard_map/spatial/pallas_call | solution.py:113
  33.1 0.5 collective-permute-start.1
  33.6 3.0 %collective-permute-start.2 = (bf16[4,2,8,512]{3,2,1,0:T(8,128)(2,1)S(1)}, bf16[4,2,8,512]{3,2,1,0:T(8,128)(2,1)S(1)}, u32[]{:S(2)}, u32[]{:S(2)}) collective-permute-start(bf16[4,2,8,512]{3,2,1,0:T(8,128)(2,1)S(1)} %get-tuple-element.22), channel_id=1, source_target_pairs={{0,16},{2,18},{4,20},{6,22},{8,24},{10,26},{12,28},{14,30},{16,0},... | collective-permute-start | bytes 196616 | tf_op jit(solution)/shard_map/ppermute | solution.py:456
  36.6 0.0 collective-permute-done.10.refs_1_
  36.6 0.1 collective-permute-start.3
  36.7 0.0 collective-permute-done.11.refs_2_
  36.7 0.1 collective-permute-done.12.refs_3_
  36.9 1.3 %collective-permute-start.13 = (bf16[8,2,8,512]{3,2,1,0:T(8,128)(2,1)S(1)}, bf16[8,2,8,512]{3,2,1,0:T(8,128)(2,1)S(1)}, u32[]{:S(2)}, u32[]{:S(2)}) collective-permute-start(bf16[8,2,8,512]{3,2,1,0:T(8,128)(2,1)S(1)} %collect.6), channel_id=1, source_target_pairs={{0,4},{2,6},{4,0},{6,2},{8,12},{10,14},{12,8},{14,10},{16,20},{18,... | collective-permute-start | bytes 393224 | tf_op jit(solution)/shard_map/ppermute | solution.py:456
  38.2 0.4 collective-permute-done.1.refs_1_
  38.6 3.6 %collective-permute-done.2.refs_2_ = bf16[4,2,8,512]{3,2,1,0:T(8,128)(2,1)S(1)} collective-permute-done((bf16[4,2,8,512]{3,2,1,0:T(8,128)(2,1)S(1)}, bf16[4,2,8,512]{3,2,1,0:T(8,128)(2,1)S(1)}, u32[]{:S(2)}, u32[]{:S(2)}) %collective-permute-start.2) | collective-permute-done | bytes 65568 | tf_op jit(solution)/shard_map/ppermute | solution.py:456
  42.2 0.0 collective-permute-done.3.refs_3_
  42.3 1.2 %collective-permute-start.4 = (bf16[8,2,8,512]{3,2,1,0:T(8,128)(2,1)S(1)}, bf16[8,2,8,512]{3,2,1,0:T(8,128)(2,1)S(1)}, u32[]{:S(2)}, u32[]{:S(2)}) collective-permute-start(bf16[8,2,8,512]{3,2,1,0:T(8,128)(2,1)S(1)} %collect.4), channel_id=1, source_target_pairs={{0,4},{2,6},{4,0},{6,2},{8,12},{10,14},{12,8},{14,10},{16,20},{18,... | collective-permute-start | bytes 393224 | tf_op jit(solution)/shard_map/ppermute | solution.py:456
  43.5 0.0 collective-permute-done.13.refs_4_
  43.5 2.7 %collective-permute-start.14 = (bf16[8,2,8,512]{3,2,1,0:T(8,128)(2,1)S(1)}, bf16[8,2,8,512]{3,2,1,0:T(8,128)(2,1)S(1)}, u32[]{:S(2)}, u32[]{:S(2)}) collective-permute-start(bf16[8,2,8,512]{3,2,1,0:T(8,128)(2,1)S(1)} %collect.7), channel_id=1, source_target_pairs={{0,2},{2,0},{4,6},{6,4},{8,10},{10,8},{12,14},{14,12},{16,18},{18,... | collective-permute-start | bytes 393224 | tf_op jit(solution)/shard_map/ppermute | solution.py:456
  46.2 0.0 collective-permute-done.4.refs_4_
  46.3 3.5 %collective-permute-start.5 = (bf16[8,2,8,512]{3,2,1,0:T(8,128)(2,1)S(1)}, bf16[8,2,8,512]{3,2,1,0:T(8,128)(2,1)S(1)}, u32[]{:S(2)}, u32[]{:S(2)}) collective-permute-start(bf16[8,2,8,512]{3,2,1,0:T(8,128)(2,1)S(1)} %collect.5), channel_id=1, source_target_pairs={{0,2},{2,0},{4,6},{6,4},{8,10},{10,8},{12,14},{14,12},{16,18},{18,... | collective-permute-start | bytes 393224 | tf_op jit(solution)/shard_map/ppermute | solution.py:456
  49.7 0.0 collective-permute-done.14.refs_5_
  49.7 0.6 assemble.3.refs_0_
  50.3 1.3 %collective-permute-start.15 = (bf16[16,2,8,512]{3,2,1,0:T(8,128)(2,1)S(1)}, bf16[16,2,8,512]{3,2,1,0:T(8,128)(2,1)S(1)}, u32[]{:S(2)}, u32[]{:S(2)}) collective-permute-start(bf16[16,2,8,512]{3,2,1,0:T(8,128)(2,1)S(1)} %assemble.3.refs_0_), channel_id=1, source_target_pairs={{0,1},{1,0},{2,3},{3,2},{4,5},{5,4},{6,7},{7,6},{8,9},{9,8},{10,11... | collective-permute-start | bytes 786440 | tf_op jit(solution)/shard_map/ppermute | solution.py:507
  51.6 0.0 collective-permute-done.5.refs_5_
  51.6 0.6 assemble.2.refs_0_
  52.1 0.4 collective-permute-start.6
  52.6 0.0 all-to-all-done.refs_1_
  52.6 1.1 %collective-permute-start.8 = (bf16[16,2,8,512]{3,2,1,0:T(8,128)(2,1)S(1)}, bf16[16,2,8,512]{3,2,1,0:T(8,128)(2,1)S(1)}, u32[]{:S(2)}, u32[]{:S(2)}) collective-permute-start(bf16[16,2,8,512]{3,2,1,0:T(8,128)(2,1)S(1)} %all-to-all-done.refs_1_), channel_id=1, source_target_pairs={{0,1},{1,0},{2,3},{3,2},{4,5},{5,4},{6,7},{7,6},{8,9},{9,8},{10,11... | collective-permute-start | bytes 786440 | tf_op jit(solution)/shard_map/ppermute | solution.py:507
  53.7 5.4 %project.3 = (f32[3,256,1536]{2,1,0:T(8,128)S(1)}, f32[256,128]{1,0:T(8,128)S(1)}) custom-call(s32[14]{0:T(128)S(1)} %stack.50.at, bf16[16,2,8,512]{3,2,1,0:T(8,128)(2,1)S(1)} %assemble.3.refs_0_, bf16[16,2,8,512]{3,2,1,0:T(8,128)(2,1)S(1)} %all-to-all-done.refs_1_, bf16[3,3072,1536]{2,1,0:T(8,128)(2,1)} %bitcast.27, f32[1,3072]{1,0:T(1,128)S(1)} %bitcast.23), custom_call_target="tpu_custom_call" | custom-call | flops 2415919104 | bytes 9437184 | tf_op jit(solution)/shard_map/project/pallas_call | solution.py:234
  59.1 3.8 %project.4 = (f32[3,256,1536]{2,1,0:T(8,128)S(1)}, f32[256,128]{1,0:T(8,128)S(1)}) custom-call(s32[14]{0:T(128)S(1)} %stack.50.at, bf16[16,2,8,512]{3,2,1,0:T(8,128)(2,1)S(1)} %collective-permute-done.15.refs_0_, bf16[3,3072,1536]{2,1,0:T(8,128)(2,1)} %bitcast.28, f32[1,3072]{1,0:T(1,128)S(1)} %bitcast.24, ...), custom_call_target="tpu_custom_call", output_to_operand_aliasing={{0}: (4, {}), {1}: (5, {})} | custom-call | flops 1207959552 | bytes 4718592 | tf_op jit(solution)/shard_map/project/pallas_call | solution.py:234
  62.9 6.5 %collective-permute-done.8.refs_1_ = bf16[16,2,8,512]{3,2,1,0:T(8,128)(2,1)S(1)} collective-permute-done((bf16[16,2,8,512]{3,2,1,0:T(8,128)(2,1)S(1)}, bf16[16,2,8,512]{3,2,1,0:T(8,128)(2,1)S(1)}, u32[]{:S(2)}, u32[]{:S(2)}) %collective-permute-start.8) | collective-permute-done | bytes 262176 | tf_op jit(solution)/shard_map/ppermute | solution.py:507
  69.4 6.2 %project.5 = (f32[3,256,1536]{2,1,0:T(8,128)S(1)}, f32[256,128]{1,0:T(8,128)S(1)}, bf16[3,512,1536]{2,1,0:T(8,128)(2,1)S(1)}) custom-call(s32[14]{0:T(128)S(1)} %stack.50.at, bf16[16,2,8,512]{3,2,1,0:T(8,128)(2,1)S(1)} %assemble.2.refs_0_, bf16[16,2,8,512]{3,2,1,0:T(8,128)(2,1)S(1)} %collective-permute-done.8.refs_1_, ...), custom_call_target="tpu_custom_call", output_to_operand_aliasing={{0}: (5, {}), {1}: (6, {})} | custom-call | flops 2415919104 | bytes 14155776 | tf_op jit(solution)/shard_map/project/pallas_call | solution.py:234
  75.7 3.8 %temporal.1 = bf16[16,2,8,1536]{3,2,1,0:T(8,128)(2,1)S(1)} custom-call(s32[14]{0:T(128)S(1)} %stack.50.at, bf16[16,2,8,512]{3,2,1,0:T(8,128)(2,1)S(1)} %collective-permute-done.6.refs_0_, f32[1,3072]{1,0:T(1,128)S(1)} %bitcast.26, f32[3,256,1536]{2,1,0:T(8,128)S(1)} %get-tuple-element.32.refs_2_, f32[256,128]{1,0:T(8,128)S(1)} %get-tuple-element.33.refs_3_, ...), custom_call_target="tpu_custom_call" | custom-call | flops 1207959552 | bytes 786432 | tf_op jit(solution)/shard_map/temporal/pallas_call | solution.py:339
  79.4 25.1 %all_to_all.10 = bf16[32,8,1536]{2,1,0:T(8,128)(2,1)S(1)} all-to-all(bf16[32,8,1536]{2,1,0:T(8,128)(2,1)S(1)} %bitcast.19), channel_id=1, replica_groups=mesh['frame'=16,'row'=2] {'frame','row'}, dimensions={0} | all-to-all | bytes 1572864 | tf_op jit(solution)/shard_map/all_to_all | solution.py:563
  104.5 0.9 copy.15
  (7 shorter events, 0.0 us)
Async XLA Ops:
  1.7 10.9 %collective-permute-start.7 = (bf16[3,128,512]{2,1,0:T(8,128)(2,1)S(1)}, bf16[3,128,512]{2,1,0:T(8,128)(2,1)S(1)}, u32[]{:S(2)}, u32[]{:S(2)}) collective-permute-start(bf16[3,128,512]{2,1,0:T(8,128)(2,1)S(1)} %pack.4), channel_id=1, source_target_pairs={{0,1},{1,0},{2,3},{3,2},{4,5},{5,4},{6,7},{7,6},{8,9},{9,8},{10,11... | collective-permute-start | bytes 1179656 | tf_op jit(solution)/shard_map/ppermute | solution.py:507
  5.4 19.0 %collective-permute-start.9 = (bf16[3,128,512]{2,1,0:T(8,128)(2,1)S(1)}, bf16[3,128,512]{2,1,0:T(8,128)(2,1)S(1)}, u32[]{:S(2)}, u32[]{:S(2)}) collective-permute-start(bf16[3,128,512]{2,1,0:T(8,128)(2,1)S(1)} %pack.5), channel_id=1, source_target_pairs={{0,1},{1,0},{2,3},{3,2},{4,5},{5,4},{6,7},{7,6},{8,9},{9,8},{10,11... | collective-permute-start | bytes 1179656 | tf_op jit(solution)/shard_map/ppermute | solution.py:507
  7.1 23.5 %collective-permute-start = (bf16[3,128,512]{2,1,0:T(8,128)(2,1)S(1)}, bf16[3,128,512]{2,1,0:T(8,128)(2,1)S(1)}, u32[]{:S(2)}, u32[]{:S(2)}) collective-permute-start(bf16[3,128,512]{2,1,0:T(8,128)(2,1)S(1)} %pack.3), channel_id=1, source_target_pairs={{0,1},{1,0},{2,3},{3,2},{4,5},{5,4},{6,7},{7,6},{8,9},{9,8},{10,11... | collective-permute-start | bytes 1179656 | tf_op jit(solution)/shard_map/ppermute | solution.py:507
  15.9 37.8 %copy-start = (f32[3072]{0:T(1024)S(1)}, f32[3072]{0:T(1024)}, u32[]{:S(2)}) copy-start(f32[3072]{0:T(1024)} %param.8) | copy-start | bytes 36868
  15.9 36.7 %all-to-all-start = ((bf16[16,2,8,512]{3,2,1,0:T(8,128)(2,1)}), bf16[16,2,8,512]{3,2,1,0:T(8,128)(2,1)S(1)}, u32[]{:S(2)}, u32[]{:S(2)}) async-start(bf16[16,2,8,512]{3,2,1,0:T(8,128)(2,1)} %spatial.4), calls=%async_computation | async-start | bytes 524288 | tf_op jit(solution)/shard_map/all_to_all | solution.py:527
  26.9 9.7 %collective-permute-start.10 = (bf16[4,2,8,512]{3,2,1,0:T(8,128)(2,1)S(1)}, bf16[4,2,8,512]{3,2,1,0:T(8,128)(2,1)S(1)}, u32[]{:S(2)}, u32[]{:S(2)}) collective-permute-start(bf16[4,2,8,512]{3,2,1,0:T(8,128)(2,1)S(1)} %get-tuple-element.25), channel_id=1, source_target_pairs={{0,8},{2,10},{4,12},{6,14},{8,0},{10,2},{12,4},{14,6},{16,24},{18,... | collective-permute-start | bytes 196616 | tf_op jit(solution)/shard_map/ppermute | solution.py:456
  28.4 8.4 %collective-permute-start.11 = (bf16[4,2,8,512]{3,2,1,0:T(8,128)(2,1)S(1)}, bf16[4,2,8,512]{3,2,1,0:T(8,128)(2,1)S(1)}, u32[]{:S(2)}, u32[]{:S(2)}) collective-permute-start(bf16[4,2,8,512]{3,2,1,0:T(8,128)(2,1)S(1)} %get-tuple-element.26), channel_id=1, source_target_pairs={{0,16},{2,18},{4,20},{6,22},{8,24},{10,26},{12,28},{14,30},{16,0},... | collective-permute-start | bytes 196616 | tf_op jit(solution)/shard_map/ppermute | solution.py:456
  30.5 6.4 %collective-permute-start.12 = (bf16[4,2,8,512]{3,2,1,0:T(8,128)(2,1)S(1)}, bf16[4,2,8,512]{3,2,1,0:T(8,128)(2,1)S(1)}, u32[]{:S(2)}, u32[]{:S(2)}) collective-permute-start(bf16[4,2,8,512]{3,2,1,0:T(8,128)(2,1)S(1)} %get-tuple-element.27), channel_id=1, source_target_pairs={{0,24},{2,26},{4,28},{6,30},{8,16},{10,18},{12,20},{14,22},{16,8},... | collective-permute-start | bytes 196616 | tf_op jit(solution)/shard_map/ppermute | solution.py:456
  33.1 5.5 %collective-permute-start.1 = (bf16[4,2,8,512]{3,2,1,0:T(8,128)(2,1)S(1)}, bf16[4,2,8,512]{3,2,1,0:T(8,128)(2,1)S(1)}, u32[]{:S(2)}, u32[]{:S(2)}) collective-permute-start(bf16[4,2,8,512]{3,2,1,0:T(8,128)(2,1)S(1)} %get-tuple-element.21), channel_id=1, source_target_pairs={{0,8},{2,10},{4,12},{6,14},{8,0},{10,2},{12,4},{14,6},{16,24},{18,... | collective-permute-start | bytes 196616 | tf_op jit(solution)/shard_map/ppermute | solution.py:456
  33.6 8.6 %collective-permute-start.2 = (bf16[4,2,8,512]{3,2,1,0:T(8,128)(2,1)S(1)}, bf16[4,2,8,512]{3,2,1,0:T(8,128)(2,1)S(1)}, u32[]{:S(2)}, u32[]{:S(2)}) collective-permute-start(bf16[4,2,8,512]{3,2,1,0:T(8,128)(2,1)S(1)} %get-tuple-element.22), channel_id=1, source_target_pairs={{0,16},{2,18},{4,20},{6,22},{8,24},{10,26},{12,28},{14,30},{16,0},... | collective-permute-start | bytes 196616 | tf_op jit(solution)/shard_map/ppermute | solution.py:456
  36.6 5.6 %collective-permute-start.3 = (bf16[4,2,8,512]{3,2,1,0:T(8,128)(2,1)S(1)}, bf16[4,2,8,512]{3,2,1,0:T(8,128)(2,1)S(1)}, u32[]{:S(2)}, u32[]{:S(2)}) collective-permute-start(bf16[4,2,8,512]{3,2,1,0:T(8,128)(2,1)S(1)} %get-tuple-element.23), channel_id=1, source_target_pairs={{0,24},{2,26},{4,28},{6,30},{8,16},{10,18},{12,20},{14,22},{16,8},... | collective-permute-start | bytes 196616 | tf_op jit(solution)/shard_map/ppermute | solution.py:456
  36.9 6.6 %collective-permute-start.13 = (bf16[8,2,8,512]{3,2,1,0:T(8,128)(2,1)S(1)}, bf16[8,2,8,512]{3,2,1,0:T(8,128)(2,1)S(1)}, u32[]{:S(2)}, u32[]{:S(2)}) collective-permute-start(bf16[8,2,8,512]{3,2,1,0:T(8,128)(2,1)S(1)} %collect.6), channel_id=1, source_target_pairs={{0,4},{2,6},{4,0},{6,2},{8,12},{10,14},{12,8},{14,10},{16,20},{18,... | collective-permute-start | bytes 393224 | tf_op jit(solution)/shard_map/ppermute | solution.py:456
  42.3 4.0 %collective-permute-start.4 = (bf16[8,2,8,512]{3,2,1,0:T(8,128)(2,1)S(1)}, bf16[8,2,8,512]{3,2,1,0:T(8,128)(2,1)S(1)}, u32[]{:S(2)}, u32[]{:S(2)}) collective-permute-start(bf16[8,2,8,512]{3,2,1,0:T(8,128)(2,1)S(1)} %collect.4), channel_id=1, source_target_pairs={{0,4},{2,6},{4,0},{6,2},{8,12},{10,14},{12,8},{14,10},{16,20},{18,... | collective-permute-start | bytes 393224 | tf_op jit(solution)/shard_map/ppermute | solution.py:456
  43.5 6.2 %collective-permute-start.14 = (bf16[8,2,8,512]{3,2,1,0:T(8,128)(2,1)S(1)}, bf16[8,2,8,512]{3,2,1,0:T(8,128)(2,1)S(1)}, u32[]{:S(2)}, u32[]{:S(2)}) collective-permute-start(bf16[8,2,8,512]{3,2,1,0:T(8,128)(2,1)S(1)} %collect.7), channel_id=1, source_target_pairs={{0,2},{2,0},{4,6},{6,4},{8,10},{10,8},{12,14},{14,12},{16,18},{18,... | collective-permute-start | bytes 393224 | tf_op jit(solution)/shard_map/ppermute | solution.py:456
  46.3 5.3 %collective-permute-start.5 = (bf16[8,2,8,512]{3,2,1,0:T(8,128)(2,1)S(1)}, bf16[8,2,8,512]{3,2,1,0:T(8,128)(2,1)S(1)}, u32[]{:S(2)}, u32[]{:S(2)}) collective-permute-start(bf16[8,2,8,512]{3,2,1,0:T(8,128)(2,1)S(1)} %collect.5), channel_id=1, source_target_pairs={{0,2},{2,0},{4,6},{6,4},{8,10},{10,8},{12,14},{14,12},{16,18},{18,... | collective-permute-start | bytes 393224 | tf_op jit(solution)/shard_map/ppermute | solution.py:456
  50.3 8.8 %collective-permute-start.15 = (bf16[16,2,8,512]{3,2,1,0:T(8,128)(2,1)S(1)}, bf16[16,2,8,512]{3,2,1,0:T(8,128)(2,1)S(1)}, u32[]{:S(2)}, u32[]{:S(2)}) collective-permute-start(bf16[16,2,8,512]{3,2,1,0:T(8,128)(2,1)S(1)} %assemble.3.refs_0_), channel_id=1, source_target_pairs={{0,1},{1,0},{2,3},{3,2},{4,5},{5,4},{6,7},{7,6},{8,9},{9,8},{10,11... | collective-permute-start | bytes 786440 | tf_op jit(solution)/shard_map/ppermute | solution.py:507
  52.1 23.5 %collective-permute-start.6 = (bf16[16,2,8,512]{3,2,1,0:T(8,128)(2,1)S(1)}, bf16[16,2,8,512]{3,2,1,0:T(8,128)(2,1)S(1)}, u32[]{:S(2)}, u32[]{:S(2)}) collective-permute-start(bf16[16,2,8,512]{3,2,1,0:T(8,128)(2,1)S(1)} %assemble.2.refs_0_), channel_id=1, source_target_pairs={{0,1},{1,0},{2,3},{3,2},{4,5},{5,4},{6,7},{7,6},{8,9},{9,8},{10,11... | collective-permute-start | bytes 786440 | tf_op jit(solution)/shard_map/ppermute | solution.py:507
  52.6 16.9 %collective-permute-start.8 = (bf16[16,2,8,512]{3,2,1,0:T(8,128)(2,1)S(1)}, bf16[16,2,8,512]{3,2,1,0:T(8,128)(2,1)S(1)}, u32[]{:S(2)}, u32[]{:S(2)}) collective-permute-start(bf16[16,2,8,512]{3,2,1,0:T(8,128)(2,1)S(1)} %all-to-all-done.refs_1_), channel_id=1, source_target_pairs={{0,1},{1,0},{2,3},{3,2},{4,5},{5,4},{6,7},{7,6},{8,9},{9,8},{10,11... | collective-permute-start | bytes 786440 | tf_op jit(solution)/shard_map/ppermute | solution.py:507

commit v7 on v6

--- a/solution.py
+++ b/solution.py
@@ -172,19 +172,25 @@
         column += depth
 
 
-def project_kernel(at, *refs, groups, places, shifts, depths, carried, tokens, ways, tiled):
+def project_kernel(
+    at, *refs, groups, places, shifts, depths, carried, given, tokens, ways, tiled
+):
     xs = refs[: len(shifts)]
     weight, gain = refs[len(shifts) : len(shifts) + 2]
-    before, refs = refs[len(shifts) + 2 :][: 2 * carried], refs[len(shifts) + 2 + 2 * carried :]
+    refs = refs[len(shifts) + 2 :]
+    before, there = refs[: 2 * carried], refs[2 * carried : 2 * carried + given]
+    refs = refs[2 * carried + given :]
     acc, ss, *rest = refs
     kept = rest[: len(groups) - sum(g is not None for g in groups)]
     sems = rest[-1]
     used = [g for g in groups if g is not None]
     scratch = rest[len(kept) : -1]
-    held, buffers = scratch[: len(used)], scratch[len(used) :]
+    held, buffers = scratch[: len(used)], [*there, *scratch[len(used) :]]
     targets = [*buffers, *kept]
     copies = []
     for i, target in enumerate(targets):
+        if i < given:
+            continue
         rows = pl.ds(pl.multiple_of(at[places[i]] * HEAD, HEAD), target.shape[1])
         for c in range(3):
             copies.append(
@@ -209,9 +215,11 @@
         part = squares(held[i][...], 1.0 / gain[:, lanes])
         total = part if total is None else total + part
         for c in range(3):
-            copies[3 * i + c].wait()
-            if 3 * i + c + AHEAD < len(copies):
-                copies[3 * i + c + AHEAD].start()
+            now = 3 * (i - given) + c
+            if now >= 0:
+                copies[now].wait()
+                if now + AHEAD < len(copies):
+                    copies[now + AHEAD].start()
             for n in range(0, width, tile):
                 cols = slice(n, n + tile)
                 value = dot(held[i][...], buffers[i][c, :, cols])
@@ -220,13 +228,16 @@
                 else:
                     acc[c, :, cols] += value
     ss[...] = total
-    for n in range(3 * len(used) + AHEAD, len(copies)):
+    done = 3 * (len(used) - given)
+    for n in range(done + AHEAD, len(copies)):
         copies[n].start()
-    for copy in copies[3 * len(used) :]:
+    for copy in copies[done:]:
         copy.wait()
 
 
-def project(groups, places, arrays, shifts, at, later, carried, weight, gain, tokens, ways, tiled):
+def project(
+    groups, places, arrays, shifts, at, later, carried, given, weight, gain, tokens, ways, tiled
+):
     rows = tokens * ways
     width = weight.shape[2]
     depths = [x.shape[-1] for x in arrays]
@@ -239,6 +250,7 @@
             shifts=shifts,
             depths=depths,
             carried=bool(carried),
+            given=len(given),
             tokens=tokens,
             ways=ways,
             tiled=tiled,
@@ -253,10 +265,10 @@
             grid=(),
             in_specs=[VMEM] * len(arrays)
             + [pl.BlockSpec(memory_space=pl.ANY)]
-            + [VMEM] * (1 + len(carried)),
+            + [VMEM] * (1 + len(carried) + len(given)),
             out_specs=(VMEM,) * (2 + len(later)),
             scratch_shapes=[pltpu.VMEM((rows, depth), jnp.bfloat16) for depth in sums]
-            + [pltpu.VMEM((3, depth, width), weight.dtype) for depth in sums]
+            + [pltpu.VMEM((3, depth, width), weight.dtype) for depth in sums[len(given) :]]
             + [pltpu.SemaphoreType.DMA((3 * (len(sums) + len(later)),))],
         ),
         cost_estimate=pl.CostEstimate(
@@ -269,7 +281,7 @@
         ),
         compiler_params=pltpu.CompilerParams(vmem_limit_bytes=32 << 20),
         name="project",
-    )(at, *arrays, weight, gain, *carried)
+    )(at, *arrays, weight, gain, *carried, *given)
 
 
 def temporal_kernel(at, *refs, places, shifts, heads, tokens, ways, slot, tiled):
@@ -384,7 +396,31 @@
         copy.wait()
 
 
-def pack(q, k, v, at, index, width):
+def pack_blocks_kernel(at, q, k, v, out):
+    for i, ref in enumerate((q, k, v)):
+        out[i] = ref[0]
+
+
+def pack(q, k, v, at, index, width, aligned):
+    if aligned:
+        blocks = width // HEAD
+        return pl.pallas_call(
+            pack_blocks_kernel,
+            out_shape=jax.ShapeDtypeStruct((3, q.shape[1], width), q.dtype),
+            grid_spec=pltpu.PrefetchScalarGridSpec(
+                num_scalar_prefetch=1,
+                grid=(1,),
+                in_specs=[
+                    pl.BlockSpec(
+                        (1, q.shape[1], width), lambda i, at: (0, 0, at[index] // blocks)
+                    )
+                ]
+                * 3,
+                out_specs=pl.BlockSpec((3, q.shape[1], width), lambda i, at: (0, 0, 0)),
+            ),
+            compiler_params=pltpu.CompilerParams(vmem_limit_bytes=8 << 20),
+            name="pack",
+        )(at, q, k, v)
     return pl.pallas_call(
         partial(pack_kernel, index=index),
         out_shape=pltpu.VMEM((3, q.shape[1], width), q.dtype),
@@ -499,6 +535,7 @@
         sizes = (first, group - first) if group > 1 else (1,)
     chunks = [(sum(sizes[:i]), size) for i, size in enumerate(sizes)]
     last = len(chunks) - 1
+    aligned = lambda i: group % chunks[i][1] == 0 and chunks[i][0] % chunks[i][1] == 0
     behind = [lax.rem(me + ways - k, ways) * group + c for c, _ in chunks for k in range(ways)]
     ahead = [lax.rem(me + k, ways) * group + c for c, _ in chunks for k in range(ways)]
     table = jnp.stack(behind + ahead + [me, lax.axis_index("frame").astype(jnp.int32)])
@@ -511,7 +548,7 @@
         parts = []
         for k in range(1, ways):
             index = len(behind) + i * ways + k
-            packed = pack(spatial_q, spatial_k, spatial_v, table, index, size * HEAD)
+            packed = pack(spatial_q, spatial_k, spatial_v, table, index, size * HEAD, aligned(i))
             parts.append(shift(packed, k))
         received.append(parts)
 
@@ -534,17 +571,17 @@
 
     others = lambda i: [[(i, k)] for k in range(1, ways)]
     if staged:
-        steps = [[[(0, 0), (1, 0)]], others(0), [[(2, 0)]] + others(1)]
+        steps = [[[(0, 0)]], [[(1, 0)]], [[(2, 0)]] + others(0) + others(1)]
     else:
         steps = [[key for i in range(last) for key in others(i)] + [[(i, 0) for i in range(last + 1)]]]
     final = [g[0] for g in others(last)]
     place = lambda key: key[0] * ways + key[1]
     shared = dict(tokens=tokens, ways=ways, tiled=tiled)
-    carried = ()
+    carried, given = (), ()
     for n, wanted in enumerate(steps):
         flat = [key for g in wanted for key in g]
-        later = final if n == len(steps) - 1 else []
-        carried = project(
+        later = final if n == len(steps) - 1 else steps[n + 1][0] if n == len(steps) - 2 else []
+        acc, ss, *brought = project(
             tuple(tuple(flat.index(key) for key in g) for g in wanted),
             tuple(place(key) for key in [g[0] for g in wanted] + later),
             [pieces[key] for key in flat],
@@ -552,10 +589,13 @@
             table,
             [chunks[i][1] * HEAD for i, _ in later],
             carried,
+            given,
             weight,
             gain,
             **shared,
         )
+        carried, given = (acc, ss), brought
+    carried = (*carried, *given)
     arrays, shifts = [pieces[key] for key in final], tuple(k for _, k in final)
     places = tuple(place(key) for key in final)
     out = temporal(arrays, shifts, table, places, gain, carried, slot=slot, **shared)

time: 106 us -> 101 us (0.953)
  waiting for transfers between devices: 14.7 us -> 10.3 us
    ppermute x6, waiting for transfers between devices: 10.5 us -> 5.9 us  [shift(): return lax.ppermute(x, 'row', [(i, (i + k) % ways) for i in range(ways)])]
where the time goes in v7:
time: 101 us; the launch traced here: 100 us
  Pallas kernels  32.6 us (32%)
  starting transfers between devices  30.8 us (30%)
  blocking collectives  25.6 us (25%)
  waiting for transfers between devices  10.3 us (10%)
    all_to_all x1, blocking collectives, local(): lax.all_to_all(out, ('frame', 'row'), split_axis=0, concat_axis=0, tiled=...  25.6 us
    ppermute x10, starting transfers between devices, swap(): return lax.ppermute(x, 'frame', [(i, i ^ key) for i in range(frames)])  15.8 us
    pallas_call x3, Pallas kernels, project(): pl.pallas_call(partial(project_kernel, groups=(*groups, *[None] * len(lat...  14.5 us
    all_to_all x1, starting transfers between devices, local(): out = lax.all_to_all(out, 'frame', split_axis=0, concat_axis=0, tiled=True)  8.49 us
    pallas_call x3, Pallas kernels, spatial(): pl.pallas_call(partial(spatial_kernel, index=index, pool=tokens * ways //...  8.38 us
    ppermute x6, starting transfers between devices, shift(): return lax.ppermute(x, 'row', [(i, (i + k) % ways) for i in range(ways)])  6.48 us
    ppermute x6, waiting for transfers between devices, shift(): return lax.ppermute(x, 'row', [(i, (i + k) % ways) for i in range(ways)])  5.9 us
    pallas_call x3, Pallas kernels, pack(): pl.pallas_call(pack_blocks_kernel, out_shape=jax.ShapeDtypeStruct((3, q.s...  4.82 us
  transfers between devices with their start and end apart: 17, of which 5 were waited for; matrix products, arithmetic and copies ran while one was open for 0% of the time, Pallas kernels for 27%

profile of v7, /device:TPU:1, one launch (start us, length us, event | category | flops | bytes accessed | tf_op | source)
XLA Modules:
  0.0 100.3 jit_solution(8153948901089718181)
XLA Ops:
  0.0 0.1 stack.50.at
  0.1 1.6 %pack.5 = bf16[3,128,512]{2,1,0:T(8,128)(2,1)S(1)} custom-call(s32[14]{0:T(128)S(1)} %stack.50.at, bf16[1,128,3072]{2,1,0:T(8,128)(2,1)} %refs_0_.5, bf16[1,128,3072]{2,1,0:T(8,128)(2,1)} %refs_1_.5, bf16[1,128,3072]{2,1,0:T(8,128)(2,1)} %refs_2_.5), custom_call_target="tpu_custom_call" | custom-call | tf_op jit(solution)/shard_map/pack/pallas_call | solution.py:407
  1.7 2.1 %collective-permute-start.14 = (bf16[3,128,512]{2,1,0:T(8,128)(2,1)S(1)}, bf16[3,128,512]{2,1,0:T(8,128)(2,1)S(1)}, u32[]{:S(2)}, u32[]{:S(2)}) collective-permute-start(bf16[3,128,512]{2,1,0:T(8,128)(2,1)S(1)} %pack.5), channel_id=1, source_target_pairs={{0,1},{1,0},{2,3},{3,2},{4,5},{5,4},{6,7},{7,6},{8,9},{9,8},{10,11... | collective-permute-start | bytes 1179656 | tf_op jit(solution)/shard_map/ppermute | solution.py:544
  3.8 1.6 %pack.4 = bf16[3,128,512]{2,1,0:T(8,128)(2,1)S(1)} custom-call(s32[14]{0:T(128)S(1)} %stack.50.at, bf16[1,128,3072]{2,1,0:T(8,128)(2,1)} %refs_0_.5, bf16[1,128,3072]{2,1,0:T(8,128)(2,1)} %refs_1_.5, bf16[1,128,3072]{2,1,0:T(8,128)(2,1)} %refs_2_.5), custom_call_target="tpu_custom_call" | custom-call | tf_op jit(solution)/shard_map/pack/pallas_call | solution.py:407
  5.4 0.1 collective-permute-start.7
  5.5 1.6 %pack.3 = bf16[3,128,512]{2,1,0:T(8,128)(2,1)S(1)} custom-call(s32[14]{0:T(128)S(1)} %stack.50.at, bf16[1,128,3072]{2,1,0:T(8,128)(2,1)} %refs_0_.5, bf16[1,128,3072]{2,1,0:T(8,128)(2,1)} %refs_1_.5, bf16[1,128,3072]{2,1,0:T(8,128)(2,1)} %refs_2_.5), custom_call_target="tpu_custom_call" | custom-call | tf_op jit(solution)/shard_map/pack/pallas_call | solution.py:407
  7.1 1.5 %collective-permute-start = (bf16[3,128,512]{2,1,0:T(8,128)(2,1)S(1)}, bf16[3,128,512]{2,1,0:T(8,128)(2,1)S(1)}, u32[]{:S(2)}, u32[]{:S(2)}) collective-permute-start(bf16[3,128,512]{2,1,0:T(8,128)(2,1)S(1)} %pack.3), channel_id=1, source_target_pairs={{0,1},{1,0},{2,3},{3,2},{4,5},{5,4},{6,7},{7,6},{8,9},{9,8},{10,11... | collective-permute-start | bytes 1179656 | tf_op jit(solution)/shard_map/ppermute | solution.py:544
  8.6 4.0 %collective-permute-done.14.refs_3_ = bf16[3,128,512]{2,1,0:T(8,128)(2,1)S(1)} collective-permute-done((bf16[3,128,512]{2,1,0:T(8,128)(2,1)S(1)}, bf16[3,128,512]{2,1,0:T(8,128)(2,1)S(1)}, u32[]{:S(2)}, u32[]{:S(2)}) %collective-permute-start.14) | collective-permute-done | bytes 393248 | tf_op jit(solution)/shard_map/ppermute | solution.py:544
  12.6 3.2 %spatial.5 = bf16[16,2,8,512]{3,2,1,0:T(8,128)(2,1)} custom-call(s32[14]{0:T(128)S(1)} %stack.50.at, bf16[1,128,3072]{2,1,0:T(8,128)(2,1)} %refs_0_.5, bf16[1,128,3072]{2,1,0:T(8,128)(2,1)} %refs_1_.5, bf16[1,128,3072]{2,1,0:T(8,128)(2,1)} %refs_2_.5, bf16[3,128,512]{2,1,0:T(8,128)(2,1)S(1)} %collective-permute-done.14.refs_3_, f32[1,3072]{1,0:T(1,128)} %bitcast.20), custom_call_target="tpu_custom_call" | custom-call | flops 167772160 | bytes 1310720 | tf_op jit(solution)/shard_map/spatial/pallas_call | solution.py:113
  15.9 0.0 copy-start
  15.9 8.5 %all-to-all-start = ((bf16[16,2,8,512]{3,2,1,0:T(8,128)(2,1)}), bf16[16,2,8,512]{3,2,1,0:T(8,128)(2,1)S(1)}, u32[]{:S(2)}, u32[]{:S(2)}) async-start(bf16[16,2,8,512]{3,2,1,0:T(8,128)(2,1)} %spatial.5), calls=%async_computation | async-start | bytes 524288 | tf_op jit(solution)/shard_map/all_to_all | solution.py:564
  24.4 0.0 collective-permute-done.7.refs_3_
  24.4 2.6 %spatial.4 = (bf16[4,2,8,512]{3,2,1,0:T(8,128)(2,1)S(1)}, bf16[4,2,8,512]{3,2,1,0:T(8,128)(2,1)S(1)}, bf16[4,2,8,512]{3,2,1,0:T(8,128)(2,1)S(1)}, bf16[4,2,8,512]{3,2,1,0:T(8,128)(2,1)S(1)}) custom-call(s32[14]{0:T(128)S(1)} %stack.50.at, bf16[1,128,3072]{2,1,0:T(8,128)(2,1)} %refs_0_.5, bf16[1,128,3072]{2,1,0:T(8,128)(2,1)} %refs_1_.5, ...), custom_call_target="tpu_custom_call" | custom-call | flops 167772160 | bytes 1310720 | tf_op jit(solution)/shard_map/spatial/pallas_call | solution.py:113
  27.0 3.2 %collective-permute-start.10 = (bf16[4,2,8,512]{3,2,1,0:T(8,128)(2,1)S(1)}, bf16[4,2,8,512]{3,2,1,0:T(8,128)(2,1)S(1)}, u32[]{:S(2)}, u32[]{:S(2)}) collective-permute-start(bf16[4,2,8,512]{3,2,1,0:T(8,128)(2,1)S(1)} %get-tuple-element.28), channel_id=1, source_target_pairs={{0,24},{2,26},{4,28},{6,30},{8,16},{10,18},{12,20},{14,22},{16,8},... | collective-permute-start | bytes 196616 | tf_op jit(solution)/shard_map/ppermute | solution.py:492
  30.2 0.0 collective-permute-start.8
  30.2 0.4 collective-permute-start.9
  30.6 0.0 collective-permute-done.refs_3_
  30.6 2.6 %spatial.3 = (bf16[4,2,8,512]{3,2,1,0:T(8,128)(2,1)S(1)}, bf16[4,2,8,512]{3,2,1,0:T(8,128)(2,1)S(1)}, bf16[4,2,8,512]{3,2,1,0:T(8,128)(2,1)S(1)}, bf16[4,2,8,512]{3,2,1,0:T(8,128)(2,1)S(1)}) custom-call(s32[14]{0:T(128)S(1)} %stack.50.at, bf16[1,128,3072]{2,1,0:T(8,128)(2,1)} %refs_0_.5, bf16[1,128,3072]{2,1,0:T(8,128)(2,1)} %refs_1_.5, ...), custom_call_target="tpu_custom_call" | custom-call | flops 167772160 | bytes 1310720 | tf_op jit(solution)/shard_map/spatial/pallas_call | solution.py:113
  33.1 1.1 %collective-permute-start.1 = (bf16[4,2,8,512]{3,2,1,0:T(8,128)(2,1)S(1)}, bf16[4,2,8,512]{3,2,1,0:T(8,128)(2,1)S(1)}, u32[]{:S(2)}, u32[]{:S(2)}) collective-permute-start(bf16[4,2,8,512]{3,2,1,0:T(8,128)(2,1)S(1)} %get-tuple-element.22), channel_id=1, source_target_pairs={{0,8},{2,10},{4,12},{6,14},{8,0},{10,2},{12,4},{14,6},{16,24},{18,... | collective-permute-start | bytes 196616 | tf_op jit(solution)/shard_map/ppermute | solution.py:492
  34.3 2.4 %collective-permute-start.2 = (bf16[4,2,8,512]{3,2,1,0:T(8,128)(2,1)S(1)}, bf16[4,2,8,512]{3,2,1,0:T(8,128)(2,1)S(1)}, u32[]{:S(2)}, u32[]{:S(2)}) collective-permute-start(bf16[4,2,8,512]{3,2,1,0:T(8,128)(2,1)S(1)} %get-tuple-element.23), channel_id=1, source_target_pairs={{0,16},{2,18},{4,20},{6,22},{8,24},{10,26},{12,28},{14,30},{16,0},... | collective-permute-start | bytes 196616 | tf_op jit(solution)/shard_map/ppermute | solution.py:492
  36.7 0.0 collective-permute-done.10.refs_3_
  36.7 0.1 collective-permute-start.3
  36.8 0.0 collective-permute-done.8.refs_1_
  36.8 2.7 %collective-permute-done.9.refs_2_ = bf16[4,2,8,512]{3,2,1,0:T(8,128)(2,1)S(1)} collective-permute-done((bf16[4,2,8,512]{3,2,1,0:T(8,128)(2,1)S(1)}, bf16[4,2,8,512]{3,2,1,0:T(8,128)(2,1)S(1)}, u32[]{:S(2)}, u32[]{:S(2)}) %collective-permute-start.9) | collective-permute-done | bytes 65568 | tf_op jit(solution)/shard_map/ppermute | solution.py:492
  39.5 1.2 %collective-permute-start.11 = (bf16[8,2,8,512]{3,2,1,0:T(8,128)(2,1)S(1)}, bf16[8,2,8,512]{3,2,1,0:T(8,128)(2,1)S(1)}, u32[]{:S(2)}, u32[]{:S(2)}) collective-permute-start(bf16[8,2,8,512]{3,2,1,0:T(8,128)(2,1)S(1)} %collect.6), channel_id=1, source_target_pairs={{0,4},{2,6},{4,0},{6,2},{8,12},{10,14},{12,8},{14,10},{16,20},{18,... | collective-permute-start | bytes 393224 | tf_op jit(solution)/shard_map/ppermute | solution.py:492
  40.7 0.0 collective-permute-done.1.refs_1_
  40.7 1.5 %collective-permute-done.2.refs_2_ = bf16[4,2,8,512]{3,2,1,0:T(8,128)(2,1)S(1)} collective-permute-done((bf16[4,2,8,512]{3,2,1,0:T(8,128)(2,1)S(1)}, bf16[4,2,8,512]{3,2,1,0:T(8,128)(2,1)S(1)}, u32[]{:S(2)}, u32[]{:S(2)}) %collective-permute-start.2) | collective-permute-done | bytes 65568 | tf_op jit(solution)/shard_map/ppermute | solution.py:492
  42.3 1.2 %collective-permute-start.4 = (bf16[8,2,8,512]{3,2,1,0:T(8,128)(2,1)S(1)}, bf16[8,2,8,512]{3,2,1,0:T(8,128)(2,1)S(1)}, u32[]{:S(2)}, u32[]{:S(2)}) collective-permute-start(bf16[8,2,8,512]{3,2,1,0:T(8,128)(2,1)S(1)} %collect.4), channel_id=1, source_target_pairs={{0,4},{2,6},{4,0},{6,2},{8,12},{10,14},{12,8},{14,10},{16,20},{18,... | collective-permute-start | bytes 393224 | tf_op jit(solution)/shard_map/ppermute | solution.py:492
  43.5 0.1 collective-permute-done.11.refs_4_
  43.6 4.7 %collective-permute-start.12 = (bf16[8,2,8,512]{3,2,1,0:T(8,128)(2,1)S(1)}, bf16[8,2,8,512]{3,2,1,0:T(8,128)(2,1)S(1)}, u32[]{:S(2)}, u32[]{:S(2)}) collective-permute-start(bf16[8,2,8,512]{3,2,1,0:T(8,128)(2,1)S(1)} %collect.7), channel_id=1, source_target_pairs={{0,2},{2,0},{4,6},{6,4},{8,10},{10,8},{12,14},{14,12},{16,18},{18,... | collective-permute-start | bytes 393224 | tf_op jit(solution)/shard_map/ppermute | solution.py:492
  48.3 0.0 collective-permute-done.4.refs_4_
  48.3 1.4 %collective-permute-start.5 = (bf16[8,2,8,512]{3,2,1,0:T(8,128)(2,1)S(1)}, bf16[8,2,8,512]{3,2,1,0:T(8,128)(2,1)S(1)}, u32[]{:S(2)}, u32[]{:S(2)}) collective-permute-start(bf16[8,2,8,512]{3,2,1,0:T(8,128)(2,1)S(1)} %collect.5), channel_id=1, source_target_pairs={{0,2},{2,0},{4,6},{6,4},{8,10},{10,8},{12,14},{14,12},{16,18},{18,... | collective-permute-start | bytes 393224 | tf_op jit(solution)/shard_map/ppermute | solution.py:492
  49.7 0.0 collective-permute-done.12.refs_5_
  49.8 0.6 assemble.3.refs_0_
  50.3 1.3 %collective-permute-start.13 = (bf16[16,2,8,512]{3,2,1,0:T(8,128)(2,1)S(1)}, bf16[16,2,8,512]{3,2,1,0:T(8,128)(2,1)S(1)}, u32[]{:S(2)}, u32[]{:S(2)}) collective-permute-start(bf16[16,2,8,512]{3,2,1,0:T(8,128)(2,1)S(1)} %assemble.3.refs_0_), channel_id=1, source_target_pairs={{0,1},{1,0},{2,3},{3,2},{4,5},{5,4},{6,7},{7,6},{8,9},{9,8},{10,11... | collective-permute-start | bytes 786440 | tf_op jit(solution)/shard_map/ppermute | solution.py:544
  51.6 0.0 all-to-all-done.refs_0_
  51.6 0.3 collective-permute-start.15
  51.9 0.0 collective-permute-done.5.refs_5_
  51.9 0.6 assemble.2.refs_0_
  52.4 1.3 %collective-permute-start.6 = (bf16[16,2,8,512]{3,2,1,0:T(8,128)(2,1)S(1)}, bf16[16,2,8,512]{3,2,1,0:T(8,128)(2,1)S(1)}, u32[]{:S(2)}, u32[]{:S(2)}) collective-permute-start(bf16[16,2,8,512]{3,2,1,0:T(8,128)(2,1)S(1)} %assemble.2.refs_0_), channel_id=1, source_target_pairs={{0,1},{1,0},{2,3},{3,2},{4,5},{5,4},{6,7},{7,6},{8,9},{9,8},{10,11... | collective-permute-start | bytes 786440 | tf_op jit(solution)/shard_map/ppermute | solution.py:544
  53.7 3.7 %project.3 = (f32[3,256,1536]{2,1,0:T(8,128)S(1)}, f32[256,128]{1,0:T(8,128)S(1)}) custom-call(s32[14]{0:T(128)S(1)} %stack.50.at, bf16[16,2,8,512]{3,2,1,0:T(8,128)(2,1)S(1)} %assemble.3.refs_0_, bf16[3,3072,1536]{2,1,0:T(8,128)(2,1)} %bitcast.27, f32[1,3072]{1,0:T(1,128)S(1)} %bitcast.23), custom_call_target="tpu_custom_call" | custom-call | flops 1207959552 | bytes 4718592 | tf_op jit(solution)/shard_map/project/pallas_call | solution.py:245
  57.4 4.5 %project.4 = (f32[3,256,1536]{2,1,0:T(8,128)S(1)}, f32[256,128]{1,0:T(8,128)S(1)}, bf16[3,512,1536]{2,1,0:T(8,128)(2,1)S(1)}) custom-call(s32[14]{0:T(128)S(1)} %stack.50.at, bf16[16,2,8,512]{3,2,1,0:T(8,128)(2,1)S(1)} %all-to-all-done.refs_0_, bf16[3,3072,1536]{2,1,0:T(8,128)(2,1)} %bitcast.28, ...), custom_call_target="tpu_custom_call", output_to_operand_aliasing={{0}: (4, {}), {1}: (5, {})} | custom-call | flops 1207959552 | bytes 9437184 | tf_op jit(solution)/shard_map/project/pallas_call | solution.py:245
  61.9 0.0 collective-permute-done.13.refs_1_
  62.0 1.9 %collective-permute-done.15.refs_2_ = bf16[16,2,8,512]{3,2,1,0:T(8,128)(2,1)S(1)} collective-permute-done((bf16[16,2,8,512]{3,2,1,0:T(8,128)(2,1)S(1)}, bf16[16,2,8,512]{3,2,1,0:T(8,128)(2,1)S(1)}, u32[]{:S(2)}, u32[]{:S(2)}) %collective-permute-start.15) | collective-permute-done | bytes 262176 | tf_op jit(solution)/shard_map/ppermute | solution.py:544
  63.8 6.3 %project.5 = (f32[3,256,1536]{2,1,0:T(8,128)S(1)}, f32[256,128]{1,0:T(8,128)S(1)}, bf16[3,512,1536]{2,1,0:T(8,128)(2,1)S(1)}) custom-call(s32[14]{0:T(128)S(1)} %stack.50.at, bf16[16,2,8,512]{3,2,1,0:T(8,128)(2,1)S(1)} %assemble.2.refs_0_, bf16[16,2,8,512]{3,2,1,0:T(8,128)(2,1)S(1)} %collective-permute-done.13.refs_1_, ...), custom_call_target="tpu_custom_call", output_to_operand_aliasing={{0}: (6, {}), {1}: (7, {})} | custom-call | flops 3623878656 | bytes 18874368 | tf_op jit(solution)/shard_map/project/pallas_call | solution.py:245
  70.1 3.8 %temporal.1 = bf16[16,2,8,1536]{3,2,1,0:T(8,128)(2,1)S(1)} custom-call(s32[14]{0:T(128)S(1)} %stack.50.at, bf16[16,2,8,512]{3,2,1,0:T(8,128)(2,1)S(1)} %collective-permute-done.6.refs_0_, f32[1,3072]{1,0:T(1,128)S(1)} %bitcast.26, f32[3,256,1536]{2,1,0:T(8,128)S(1)} %get-tuple-element.34.refs_2_, f32[256,128]{1,0:T(8,128)S(1)} %get-tuple-element.35.refs_3_, ...), custom_call_target="tpu_custom_call" | custom-call | flops 1207959552 | bytes 786432 | tf_op jit(solution)/shard_map/temporal/pallas_call | solution.py:351
  73.9 25.6 %all_to_all.10 = bf16[32,8,1536]{2,1,0:T(8,128)(2,1)S(1)} all-to-all(bf16[32,8,1536]{2,1,0:T(8,128)(2,1)S(1)} %bitcast.19), channel_id=1, replica_groups=mesh['frame'=16,'row'=2] {'frame','row'}, dimensions={0} | all-to-all | bytes 1572864 | tf_op jit(solution)/shard_map/all_to_all | solution.py:603
  99.5 0.9 copy.15
  (7 shorter events, 0.0 us)
Async XLA Ops:
  1.7 10.9 %collective-permute-start.14 = (bf16[3,128,512]{2,1,0:T(8,128)(2,1)S(1)}, bf16[3,128,512]{2,1,0:T(8,128)(2,1)S(1)}, u32[]{:S(2)}, u32[]{:S(2)}) collective-permute-start(bf16[3,128,512]{2,1,0:T(8,128)(2,1)S(1)} %pack.5), channel_id=1, source_target_pairs={{0,1},{1,0},{2,3},{3,2},{4,5},{5,4},{6,7},{7,6},{8,9},{9,8},{10,11... | collective-permute-start | bytes 1179656 | tf_op jit(solution)/shard_map/ppermute | solution.py:544
  5.4 19.0 %collective-permute-start.7 = (bf16[3,128,512]{2,1,0:T(8,128)(2,1)S(1)}, bf16[3,128,512]{2,1,0:T(8,128)(2,1)S(1)}, u32[]{:S(2)}, u32[]{:S(2)}) collective-permute-start(bf16[3,128,512]{2,1,0:T(8,128)(2,1)S(1)} %pack.4), channel_id=1, source_target_pairs={{0,1},{1,0},{2,3},{3,2},{4,5},{5,4},{6,7},{7,6},{8,9},{9,8},{10,11... | collective-permute-start | bytes 1179656 | tf_op jit(solution)/shard_map/ppermute | solution.py:544
  7.1 23.5 %collective-permute-start = (bf16[3,128,512]{2,1,0:T(8,128)(2,1)S(1)}, bf16[3,128,512]{2,1,0:T(8,128)(2,1)S(1)}, u32[]{:S(2)}, u32[]{:S(2)}) collective-permute-start(bf16[3,128,512]{2,1,0:T(8,128)(2,1)S(1)} %pack.3), channel_id=1, source_target_pairs={{0,1},{1,0},{2,3},{3,2},{4,5},{5,4},{6,7},{7,6},{8,9},{9,8},{10,11... | collective-permute-start | bytes 1179656 | tf_op jit(solution)/shard_map/ppermute | solution.py:544
  15.9 37.8 %copy-start = (f32[3072]{0:T(1024)S(1)}, f32[3072]{0:T(1024)}, u32[]{:S(2)}) copy-start(f32[3072]{0:T(1024)} %param.8) | copy-start | bytes 36868
  15.9 35.7 %all-to-all-start = ((bf16[16,2,8,512]{3,2,1,0:T(8,128)(2,1)}), bf16[16,2,8,512]{3,2,1,0:T(8,128)(2,1)S(1)}, u32[]{:S(2)}, u32[]{:S(2)}) async-start(bf16[16,2,8,512]{3,2,1,0:T(8,128)(2,1)} %spatial.5), calls=%async_computation | async-start | bytes 524288 | tf_op jit(solution)/shard_map/all_to_all | solution.py:564
  27.0 9.7 %collective-permute-start.10 = (bf16[4,2,8,512]{3,2,1,0:T(8,128)(2,1)S(1)}, bf16[4,2,8,512]{3,2,1,0:T(8,128)(2,1)S(1)}, u32[]{:S(2)}, u32[]{:S(2)}) collective-permute-start(bf16[4,2,8,512]{3,2,1,0:T(8,128)(2,1)S(1)} %get-tuple-element.28), channel_id=1, source_target_pairs={{0,24},{2,26},{4,28},{6,30},{8,16},{10,18},{12,20},{14,22},{16,8},... | collective-permute-start | bytes 196616 | tf_op jit(solution)/shard_map/ppermute | solution.py:492
  30.2 6.6 %collective-permute-start.8 = (bf16[4,2,8,512]{3,2,1,0:T(8,128)(2,1)S(1)}, bf16[4,2,8,512]{3,2,1,0:T(8,128)(2,1)S(1)}, u32[]{:S(2)}, u32[]{:S(2)}) collective-permute-start(bf16[4,2,8,512]{3,2,1,0:T(8,128)(2,1)S(1)} %get-tuple-element.26), channel_id=1, source_target_pairs={{0,8},{2,10},{4,12},{6,14},{8,0},{10,2},{12,4},{14,6},{16,24},{18,... | collective-permute-start | bytes 196616 | tf_op jit(solution)/shard_map/ppermute | solution.py:492
  30.2 9.3 %collective-permute-start.9 = (bf16[4,2,8,512]{3,2,1,0:T(8,128)(2,1)S(1)}, bf16[4,2,8,512]{3,2,1,0:T(8,128)(2,1)S(1)}, u32[]{:S(2)}, u32[]{:S(2)}) collective-permute-start(bf16[4,2,8,512]{3,2,1,0:T(8,128)(2,1)S(1)} %get-tuple-element.27), channel_id=1, source_target_pairs={{0,16},{2,18},{4,20},{6,22},{8,24},{10,26},{12,28},{14,30},{16,0},... | collective-permute-start | bytes 196616 | tf_op jit(solution)/shard_map/ppermute | solution.py:492
  33.1 7.6 %collective-permute-start.1 = (bf16[4,2,8,512]{3,2,1,0:T(8,128)(2,1)S(1)}, bf16[4,2,8,512]{3,2,1,0:T(8,128)(2,1)S(1)}, u32[]{:S(2)}, u32[]{:S(2)}) collective-permute-start(bf16[4,2,8,512]{3,2,1,0:T(8,128)(2,1)S(1)} %get-tuple-element.22), channel_id=1, source_target_pairs={{0,8},{2,10},{4,12},{6,14},{8,0},{10,2},{12,4},{14,6},{16,24},{18,... | collective-permute-start | bytes 196616 | tf_op jit(solution)/shard_map/ppermute | solution.py:492
  34.3 8.0 %collective-permute-start.2 = (bf16[4,2,8,512]{3,2,1,0:T(8,128)(2,1)S(1)}, bf16[4,2,8,512]{3,2,1,0:T(8,128)(2,1)S(1)}, u32[]{:S(2)}, u32[]{:S(2)}) collective-permute-start(bf16[4,2,8,512]{3,2,1,0:T(8,128)(2,1)S(1)} %get-tuple-element.23), channel_id=1, source_target_pairs={{0,16},{2,18},{4,20},{6,22},{8,24},{10,26},{12,28},{14,30},{16,0},... | collective-permute-start | bytes 196616 | tf_op jit(solution)/shard_map/ppermute | solution.py:492
  36.7 5.6 %collective-permute-start.3 = (bf16[4,2,8,512]{3,2,1,0:T(8,128)(2,1)S(1)}, bf16[4,2,8,512]{3,2,1,0:T(8,128)(2,1)S(1)}, u32[]{:S(2)}, u32[]{:S(2)}) collective-permute-start(bf16[4,2,8,512]{3,2,1,0:T(8,128)(2,1)S(1)} %get-tuple-element.24), channel_id=1, source_target_pairs={{0,24},{2,26},{4,28},{6,30},{8,16},{10,18},{12,20},{14,22},{16,8},... | collective-permute-start | bytes 196616 | tf_op jit(solution)/shard_map/ppermute | solution.py:492
  39.5 4.2 %collective-permute-start.11 = (bf16[8,2,8,512]{3,2,1,0:T(8,128)(2,1)S(1)}, bf16[8,2,8,512]{3,2,1,0:T(8,128)(2,1)S(1)}, u32[]{:S(2)}, u32[]{:S(2)}) collective-permute-start(bf16[8,2,8,512]{3,2,1,0:T(8,128)(2,1)S(1)} %collect.6), channel_id=1, source_target_pairs={{0,4},{2,6},{4,0},{6,2},{8,12},{10,14},{12,8},{14,10},{16,20},{18,... | collective-permute-start | bytes 393224 | tf_op jit(solution)/shard_map/ppermute | solution.py:492
  42.3 6.1 %collective-permute-start.4 = (bf16[8,2,8,512]{3,2,1,0:T(8,128)(2,1)S(1)}, bf16[8,2,8,512]{3,2,1,0:T(8,128)(2,1)S(1)}, u32[]{:S(2)}, u32[]{:S(2)}) collective-permute-start(bf16[8,2,8,512]{3,2,1,0:T(8,128)(2,1)S(1)} %collect.4), channel_id=1, source_target_pairs={{0,4},{2,6},{4,0},{6,2},{8,12},{10,14},{12,8},{14,10},{16,20},{18,... | collective-permute-start | bytes 393224 | tf_op jit(solution)/shard_map/ppermute | solution.py:492
  43.6 6.1 %collective-permute-start.12 = (bf16[8,2,8,512]{3,2,1,0:T(8,128)(2,1)S(1)}, bf16[8,2,8,512]{3,2,1,0:T(8,128)(2,1)S(1)}, u32[]{:S(2)}, u32[]{:S(2)}) collective-permute-start(bf16[8,2,8,512]{3,2,1,0:T(8,128)(2,1)S(1)} %collect.7), channel_id=1, source_target_pairs={{0,2},{2,0},{4,6},{6,4},{8,10},{10,8},{12,14},{14,12},{16,18},{18,... | collective-permute-start | bytes 393224 | tf_op jit(solution)/shard_map/ppermute | solution.py:492
  48.3 3.5 %collective-permute-start.5 = (bf16[8,2,8,512]{3,2,1,0:T(8,128)(2,1)S(1)}, bf16[8,2,8,512]{3,2,1,0:T(8,128)(2,1)S(1)}, u32[]{:S(2)}, u32[]{:S(2)}) collective-permute-start(bf16[8,2,8,512]{3,2,1,0:T(8,128)(2,1)S(1)} %collect.5), channel_id=1, source_target_pairs={{0,2},{2,0},{4,6},{6,4},{8,10},{10,8},{12,14},{14,12},{16,18},{18,... | collective-permute-start | bytes 393224 | tf_op jit(solution)/shard_map/ppermute | solution.py:492
  50.3 11.6 %collective-permute-start.13 = (bf16[16,2,8,512]{3,2,1,0:T(8,128)(2,1)S(1)}, bf16[16,2,8,512]{3,2,1,0:T(8,128)(2,1)S(1)}, u32[]{:S(2)}, u32[]{:S(2)}) collective-permute-start(bf16[16,2,8,512]{3,2,1,0:T(8,128)(2,1)S(1)} %assemble.3.refs_0_), channel_id=1, source_target_pairs={{0,1},{1,0},{2,3},{3,2},{4,5},{5,4},{6,7},{7,6},{8,9},{9,8},{10,11... | collective-permute-start | bytes 786440 | tf_op jit(solution)/shard_map/ppermute | solution.py:544
  51.6 12.3 %collective-permute-start.15 = (bf16[16,2,8,512]{3,2,1,0:T(8,128)(2,1)S(1)}, bf16[16,2,8,512]{3,2,1,0:T(8,128)(2,1)S(1)}, u32[]{:S(2)}, u32[]{:S(2)}) collective-permute-start(bf16[16,2,8,512]{3,2,1,0:T(8,128)(2,1)S(1)} %all-to-all-done.refs_0_), channel_id=1, source_target_pairs={{0,1},{1,0},{2,3},{3,2},{4,5},{5,4},{6,7},{7,6},{8,9},{9,8},{10,11... | collective-permute-start | bytes 786440 | tf_op jit(solution)/shard_map/ppermute | solution.py:544
  52.4 17.7 %collective-permute-start.6 = (bf16[16,2,8,512]{3,2,1,0:T(8,128)(2,1)S(1)}, bf16[16,2,8,512]{3,2,1,0:T(8,128)(2,1)S(1)}, u32[]{:S(2)}, u32[]{:S(2)}) collective-permute-start(bf16[16,2,8,512]{3,2,1,0:T(8,128)(2,1)S(1)} %assemble.2.refs_0_), channel_id=1, source_target_pairs={{0,1},{1,0},{2,3},{3,2},{4,5},{5,4},{6,7},{7,6},{8,9},{9,8},{10,11... | collective-permute-start | bytes 786440 | tf_op jit(solution)/shard_map/ppermute | solution.py:544

commit v8 on v7

--- a/solution.py
+++ b/solution.py
@@ -381,7 +381,7 @@
     return out
 
 
-FINAL_HEADS = 6
+FINAL_HEADS = 12
 
 
 def pack_kernel(at, q, k, v, out, sems, *, index):
@@ -538,7 +538,7 @@
     aligned = lambda i: group % chunks[i][1] == 0 and chunks[i][0] % chunks[i][1] == 0
     behind = [lax.rem(me + ways - k, ways) * group + c for c, _ in chunks for k in range(ways)]
     ahead = [lax.rem(me + k, ways) * group + c for c, _ in chunks for k in range(ways)]
-    table = jnp.stack(behind + ahead + [me, lax.axis_index("frame").astype(jnp.int32)])
+    table = jnp.stack(behind + [me, lax.axis_index("frame").astype(jnp.int32)])
 
     def shift(x, k):
         return lax.ppermute(x, "row", [(i, (i + k) % ways) for i in range(ways)])
@@ -547,8 +547,8 @@
     for i, (_, size) in enumerate(chunks):
         parts = []
         for k in range(1, ways):
-            index = len(behind) + i * ways + k
-            packed = pack(spatial_q, spatial_k, spatial_v, table, index, size * HEAD, aligned(i))
+            at = ahead[i * ways + k].reshape(1)
+            packed = pack(spatial_q, spatial_k, spatial_v, at, 0, size * HEAD, aligned(i))
             parts.append(shift(packed, k))
         received.append(parts)
 

time: 101 us -> 99.5 us (0.985)
  Pallas kernels: 32.6 us -> 30.4 us
    pallas_call x3, Pallas kernels: 4.82 us -> 3.17 us  [pack(): pl.pallas_call(pack_blocks_kernel, out_shape=jax.ShapeDtypeStruct((3, q.s...]
  transfers between devices with their start and end apart: 17 -> 17, of which waited for: 5 -> 5; matrix products, arithmetic and copies ran while one was open for 0% -> 0% of each run, Pallas kernels for 27% -> 26%
where the time goes in v8:
time: 99.5 us; the launch traced here: 99.1 us
  starting transfers between devices  30.8 us (31%)
  Pallas kernels  30.4 us (31%)
  blocking collectives  25.6 us (26%)
  waiting for transfers between devices  11.2 us (11%)
    all_to_all x1, blocking collectives, local(): lax.all_to_all(out, ('frame', 'row'), split_axis=0, concat_axis=0, tiled=...  25.6 us
    ppermute x10, starting transfers between devices, swap(): return lax.ppermute(x, 'frame', [(i, i ^ key) for i in range(frames)])  15.8 us
    pallas_call x3, Pallas kernels, project(): pl.pallas_call(partial(project_kernel, groups=(*groups, *[None] * len(lat...  14.5 us
    all_to_all x1, starting transfers between devices, local(): out = lax.all_to_all(out, 'frame', split_axis=0, concat_axis=0, tiled=True)  8.49 us
    pallas_call x3, Pallas kernels, spatial(): pl.pallas_call(partial(spatial_kernel, index=index, pool=tokens * ways //...  8.36 us
    ppermute x6, waiting for transfers between devices, shift(): return lax.ppermute(x, 'row', [(i, (i + k) % ways) for i in range(ways)])  6.89 us
    ppermute x6, starting transfers between devices, shift(): return lax.ppermute(x, 'row', [(i, (i + k) % ways) for i in range(ways)])  6.51 us
    ppermute x10, waiting for transfers between devices, swap(): return lax.ppermute(x, 'frame', [(i, i ^ key) for i in range(frames)])  4.35 us
  transfers between devices with their start and end apart: 17, of which 5 were waited for; matrix products, arithmetic and copies ran while one was open for 0% of the time, Pallas kernels for 26%

profile of v8, /device:TPU:1, one launch (start us, length us, event | category | flops | bytes accessed | tf_op | source)
XLA Modules:
  0.0 99.1 jit_solution(743995770157227407)
XLA Ops:
  0.0 1.1 %pack.5 = bf16[3,128,512]{2,1,0:T(8,128)(2,1)S(1)} custom-call(s32[1]{0:T(128)} %bitcast.3.at, bf16[1,128,3072]{2,1,0:T(8,128)(2,1)} %refs_0_.5, bf16[1,128,3072]{2,1,0:T(8,128)(2,1)} %refs_1_.5, bf16[1,128,3072]{2,1,0:T(8,128)(2,1)} %refs_2_.5), custom_call_target="tpu_custom_call" | custom-call | tf_op jit(solution)/shard_map/pack/pallas_call | solution.py:407
  1.1 2.1 %collective-permute-start.14 = (bf16[3,128,512]{2,1,0:T(8,128)(2,1)S(1)}, bf16[3,128,512]{2,1,0:T(8,128)(2,1)S(1)}, u32[]{:S(2)}, u32[]{:S(2)}) collective-permute-start(bf16[3,128,512]{2,1,0:T(8,128)(2,1)S(1)} %pack.5), channel_id=1, source_target_pairs={{0,1},{1,0},{2,3},{3,2},{4,5},{5,4},{6,7},{7,6},{8,9},{9,8},{10,11... | collective-permute-start | bytes 1179656 | tf_op jit(solution)/shard_map/ppermute | solution.py:544
  3.2 1.1 %pack.4 = bf16[3,128,512]{2,1,0:T(8,128)(2,1)S(1)} custom-call(s32[1]{0:T(128)} %bitcast.1.at, bf16[1,128,3072]{2,1,0:T(8,128)(2,1)} %refs_0_.5, bf16[1,128,3072]{2,1,0:T(8,128)(2,1)} %refs_1_.5, bf16[1,128,3072]{2,1,0:T(8,128)(2,1)} %refs_2_.5), custom_call_target="tpu_custom_call" | custom-call | tf_op jit(solution)/shard_map/pack/pallas_call | solution.py:407
  4.2 0.1 collective-permute-start.7
  4.3 1.1 %pack.3 = bf16[3,128,512]{2,1,0:T(8,128)(2,1)S(1)} custom-call(s32[1]{0:T(128)} %bitcast.5.at, bf16[1,128,3072]{2,1,0:T(8,128)(2,1)} %refs_0_.5, bf16[1,128,3072]{2,1,0:T(8,128)(2,1)} %refs_1_.5, bf16[1,128,3072]{2,1,0:T(8,128)(2,1)} %refs_2_.5), custom_call_target="tpu_custom_call" | custom-call | tf_op jit(solution)/shard_map/pack/pallas_call | solution.py:407
  5.4 1.5 %collective-permute-start = (bf16[3,128,512]{2,1,0:T(8,128)(2,1)S(1)}, bf16[3,128,512]{2,1,0:T(8,128)(2,1)S(1)}, u32[]{:S(2)}, u32[]{:S(2)}) collective-permute-start(bf16[3,128,512]{2,1,0:T(8,128)(2,1)S(1)} %pack.3), channel_id=1, source_target_pairs={{0,1},{1,0},{2,3},{3,2},{4,5},{5,4},{6,7},{7,6},{8,9},{9,8},{10,11... | collective-permute-start | bytes 1179656 | tf_op jit(solution)/shard_map/ppermute | solution.py:544
  6.9 0.1 stack.35.at
  7.0 5.0 %collective-permute-done.14.refs_3_ = bf16[3,128,512]{2,1,0:T(8,128)(2,1)S(1)} collective-permute-done((bf16[3,128,512]{2,1,0:T(8,128)(2,1)S(1)}, bf16[3,128,512]{2,1,0:T(8,128)(2,1)S(1)}, u32[]{:S(2)}, u32[]{:S(2)}) %collective-permute-start.14) | collective-permute-done | bytes 393248 | tf_op jit(solution)/shard_map/ppermute | solution.py:544
  12.0 3.2 %spatial.5 = bf16[16,2,8,512]{3,2,1,0:T(8,128)(2,1)} custom-call(s32[8]{0:T(128)S(1)} %stack.35.at, bf16[1,128,3072]{2,1,0:T(8,128)(2,1)} %refs_0_.5, bf16[1,128,3072]{2,1,0:T(8,128)(2,1)} %refs_1_.5, bf16[1,128,3072]{2,1,0:T(8,128)(2,1)} %refs_2_.5, bf16[3,128,512]{2,1,0:T(8,128)(2,1)S(1)} %collective-permute-done.14.refs_3_, f32[1,3072]{1,0:T(1,128)} %bitcast.17), custom_call_target="tpu_custom_call" | custom-call | flops 167772160 | bytes 1310720 | tf_op jit(solution)/shard_map/spatial/pallas_call | solution.py:113
  15.2 0.0 copy-start
  15.2 8.5 %all-to-all-start = ((bf16[16,2,8,512]{3,2,1,0:T(8,128)(2,1)}), bf16[16,2,8,512]{3,2,1,0:T(8,128)(2,1)S(1)}, u32[]{:S(2)}, u32[]{:S(2)}) async-start(bf16[16,2,8,512]{3,2,1,0:T(8,128)(2,1)} %spatial.5), calls=%async_computation | async-start | bytes 524288 | tf_op jit(solution)/shard_map/all_to_all | solution.py:564
  23.7 0.0 collective-permute-done.7.refs_3_
  23.7 2.6 %spatial.4 = (bf16[4,2,8,512]{3,2,1,0:T(8,128)(2,1)S(1)}, bf16[4,2,8,512]{3,2,1,0:T(8,128)(2,1)S(1)}, bf16[4,2,8,512]{3,2,1,0:T(8,128)(2,1)S(1)}, bf16[4,2,8,512]{3,2,1,0:T(8,128)(2,1)S(1)}) custom-call(s32[8]{0:T(128)S(1)} %stack.35.at, bf16[1,128,3072]{2,1,0:T(8,128)(2,1)} %refs_0_.5, bf16[1,128,3072]{2,1,0:T(8,128)(2,1)} %refs_1_.5, ...), custom_call_target="tpu_custom_call" | custom-call | flops 167772160 | bytes 1310720 | tf_op jit(solution)/shard_map/spatial/pallas_call | solution.py:113
  26.3 3.2 %collective-permute-start.10 = (bf16[4,2,8,512]{3,2,1,0:T(8,128)(2,1)S(1)}, bf16[4,2,8,512]{3,2,1,0:T(8,128)(2,1)S(1)}, u32[]{:S(2)}, u32[]{:S(2)}) collective-permute-start(bf16[4,2,8,512]{3,2,1,0:T(8,128)(2,1)S(1)} %get-tuple-element.28), channel_id=1, source_target_pairs={{0,24},{2,26},{4,28},{6,30},{8,16},{10,18},{12,20},{14,22},{16,8},... | collective-permute-start | bytes 196616 | tf_op jit(solution)/shard_map/ppermute | solution.py:492
  29.5 0.0 collective-permute-start.8
  29.5 0.4 collective-permute-start.9
  29.9 0.0 collective-permute-done.refs_3_
  29.9 2.6 %spatial.3 = (bf16[4,2,8,512]{3,2,1,0:T(8,128)(2,1)S(1)}, bf16[4,2,8,512]{3,2,1,0:T(8,128)(2,1)S(1)}, bf16[4,2,8,512]{3,2,1,0:T(8,128)(2,1)S(1)}, bf16[4,2,8,512]{3,2,1,0:T(8,128)(2,1)S(1)}) custom-call(s32[8]{0:T(128)S(1)} %stack.35.at, bf16[1,128,3072]{2,1,0:T(8,128)(2,1)} %refs_0_.5, bf16[1,128,3072]{2,1,0:T(8,128)(2,1)} %refs_1_.5, ...), custom_call_target="tpu_custom_call" | custom-call | flops 167772160 | bytes 1310720 | tf_op jit(solution)/shard_map/spatial/pallas_call | solution.py:113
  32.5 1.1 %collective-permute-start.1 = (bf16[4,2,8,512]{3,2,1,0:T(8,128)(2,1)S(1)}, bf16[4,2,8,512]{3,2,1,0:T(8,128)(2,1)S(1)}, u32[]{:S(2)}, u32[]{:S(2)}) collective-permute-start(bf16[4,2,8,512]{3,2,1,0:T(8,128)(2,1)S(1)} %get-tuple-element.22), channel_id=1, source_target_pairs={{0,8},{2,10},{4,12},{6,14},{8,0},{10,2},{12,4},{14,6},{16,24},{18,... | collective-permute-start | bytes 196616 | tf_op jit(solution)/shard_map/ppermute | solution.py:492
  33.6 2.4 %collective-permute-start.2 = (bf16[4,2,8,512]{3,2,1,0:T(8,128)(2,1)S(1)}, bf16[4,2,8,512]{3,2,1,0:T(8,128)(2,1)S(1)}, u32[]{:S(2)}, u32[]{:S(2)}) collective-permute-start(bf16[4,2,8,512]{3,2,1,0:T(8,128)(2,1)S(1)} %get-tuple-element.23), channel_id=1, source_target_pairs={{0,16},{2,18},{4,20},{6,22},{8,24},{10,26},{12,28},{14,30},{16,0},... | collective-permute-start | bytes 196616 | tf_op jit(solution)/shard_map/ppermute | solution.py:492
  36.0 0.0 collective-permute-done.10.refs_3_
  36.0 0.1 collective-permute-start.3
  36.1 0.0 collective-permute-done.8.refs_1_
  36.1 2.7 %collective-permute-done.9.refs_2_ = bf16[4,2,8,512]{3,2,1,0:T(8,128)(2,1)S(1)} collective-permute-done((bf16[4,2,8,512]{3,2,1,0:T(8,128)(2,1)S(1)}, bf16[4,2,8,512]{3,2,1,0:T(8,128)(2,1)S(1)}, u32[]{:S(2)}, u32[]{:S(2)}) %collective-permute-start.9) | collective-permute-done | bytes 65568 | tf_op jit(solution)/shard_map/ppermute | solution.py:492
  38.8 1.2 %collective-permute-start.11 = (bf16[8,2,8,512]{3,2,1,0:T(8,128)(2,1)S(1)}, bf16[8,2,8,512]{3,2,1,0:T(8,128)(2,1)S(1)}, u32[]{:S(2)}, u32[]{:S(2)}) collective-permute-start(bf16[8,2,8,512]{3,2,1,0:T(8,128)(2,1)S(1)} %collect.6), channel_id=1, source_target_pairs={{0,4},{2,6},{4,0},{6,2},{8,12},{10,14},{12,8},{14,10},{16,20},{18,... | collective-permute-start | bytes 393224 | tf_op jit(solution)/shard_map/ppermute | solution.py:492
  40.0 0.0 collective-permute-done.1.refs_1_
  40.0 1.5 %collective-permute-done.2.refs_2_ = bf16[4,2,8,512]{3,2,1,0:T(8,128)(2,1)S(1)} collective-permute-done((bf16[4,2,8,512]{3,2,1,0:T(8,128)(2,1)S(1)}, bf16[4,2,8,512]{3,2,1,0:T(8,128)(2,1)S(1)}, u32[]{:S(2)}, u32[]{:S(2)}) %collective-permute-start.2) | collective-permute-done | bytes 65568 | tf_op jit(solution)/shard_map/ppermute | solution.py:492
  41.6 0.0 collective-permute-done.3.refs_3_
  41.6 1.2 %collective-permute-start.4 = (bf16[8,2,8,512]{3,2,1,0:T(8,128)(2,1)S(1)}, bf16[8,2,8,512]{3,2,1,0:T(8,128)(2,1)S(1)}, u32[]{:S(2)}, u32[]{:S(2)}) collective-permute-start(bf16[8,2,8,512]{3,2,1,0:T(8,128)(2,1)S(1)} %collect.4), channel_id=1, source_target_pairs={{0,4},{2,6},{4,0},{6,2},{8,12},{10,14},{12,8},{14,10},{16,20},{18,... | collective-permute-start | bytes 393224 | tf_op jit(solution)/shard_map/ppermute | solution.py:492
  42.9 0.1 collective-permute-done.11.refs_4_
  43.0 4.7 %collective-permute-start.12 = (bf16[8,2,8,512]{3,2,1,0:T(8,128)(2,1)S(1)}, bf16[8,2,8,512]{3,2,1,0:T(8,128)(2,1)S(1)}, u32[]{:S(2)}, u32[]{:S(2)}) collective-permute-start(bf16[8,2,8,512]{3,2,1,0:T(8,128)(2,1)S(1)} %collect.7), channel_id=1, source_target_pairs={{0,2},{2,0},{4,6},{6,4},{8,10},{10,8},{12,14},{14,12},{16,18},{18,... | collective-permute-start | bytes 393224 | tf_op jit(solution)/shard_map/ppermute | solution.py:492
  47.7 0.0 collective-permute-done.4.refs_4_
  47.7 1.4 %collective-permute-start.5 = (bf16[8,2,8,512]{3,2,1,0:T(8,128)(2,1)S(1)}, bf16[8,2,8,512]{3,2,1,0:T(8,128)(2,1)S(1)}, u32[]{:S(2)}, u32[]{:S(2)}) collective-permute-start(bf16[8,2,8,512]{3,2,1,0:T(8,128)(2,1)S(1)} %collect.5), channel_id=1, source_target_pairs={{0,2},{2,0},{4,6},{6,4},{8,10},{10,8},{12,14},{14,12},{16,18},{18,... | collective-permute-start | bytes 393224 | tf_op jit(solution)/shard_map/ppermute | solution.py:492
  49.1 0.0 collective-permute-done.12.refs_5_
  49.1 0.6 assemble.3.refs_0_
  49.7 1.3 %collective-permute-start.13 = (bf16[16,2,8,512]{3,2,1,0:T(8,128)(2,1)S(1)}, bf16[16,2,8,512]{3,2,1,0:T(8,128)(2,1)S(1)}, u32[]{:S(2)}, u32[]{:S(2)}) collective-permute-start(bf16[16,2,8,512]{3,2,1,0:T(8,128)(2,1)S(1)} %assemble.3.refs_0_), channel_id=1, source_target_pairs={{0,1},{1,0},{2,3},{3,2},{4,5},{5,4},{6,7},{7,6},{8,9},{9,8},{10,11... | collective-permute-start | bytes 786440 | tf_op jit(solution)/shard_map/ppermute | solution.py:544
  50.9 0.2 collective-permute-start.15
  51.2 0.0 collective-permute-done.5.refs_5_
  51.2 0.6 assemble.2.refs_0_
  51.8 1.3 %collective-permute-start.6 = (bf16[16,2,8,512]{3,2,1,0:T(8,128)(2,1)S(1)}, bf16[16,2,8,512]{3,2,1,0:T(8,128)(2,1)S(1)}, u32[]{:S(2)}, u32[]{:S(2)}) collective-permute-start(bf16[16,2,8,512]{3,2,1,0:T(8,128)(2,1)S(1)} %assemble.2.refs_0_), channel_id=1, source_target_pairs={{0,1},{1,0},{2,3},{3,2},{4,5},{5,4},{6,7},{7,6},{8,9},{9,8},{10,11... | collective-permute-start | bytes 786440 | tf_op jit(solution)/shard_map/ppermute | solution.py:544
  53.0 3.7 %project.3 = (f32[3,256,1536]{2,1,0:T(8,128)S(1)}, f32[256,128]{1,0:T(8,128)S(1)}) custom-call(s32[8]{0:T(128)S(1)} %stack.35.at, bf16[16,2,8,512]{3,2,1,0:T(8,128)(2,1)S(1)} %assemble.3.refs_0_, bf16[3,3072,1536]{2,1,0:T(8,128)(2,1)} %bitcast.24, f32[1,3072]{1,0:T(1,128)S(1)} %bitcast.20), custom_call_target="tpu_custom_call" | custom-call | flops 1207959552 | bytes 4718592 | tf_op jit(solution)/shard_map/project/pallas_call | solution.py:245
  56.8 4.5 %project.4 = (f32[3,256,1536]{2,1,0:T(8,128)S(1)}, f32[256,128]{1,0:T(8,128)S(1)}, bf16[3,512,1536]{2,1,0:T(8,128)(2,1)S(1)}) custom-call(s32[8]{0:T(128)S(1)} %stack.35.at, bf16[16,2,8,512]{3,2,1,0:T(8,128)(2,1)S(1)} %all-to-all-done.refs_0_, bf16[3,3072,1536]{2,1,0:T(8,128)(2,1)} %bitcast.25, ...), custom_call_target="tpu_custom_call", output_to_operand_aliasing={{0}: (4, {}), {1}: (5, {})} | custom-call | flops 1207959552 | bytes 9437184 | tf_op jit(solution)/shard_map/project/pallas_call | solution.py:245
  61.3 1.9 %collective-permute-done.15.refs_2_ = bf16[16,2,8,512]{3,2,1,0:T(8,128)(2,1)S(1)} collective-permute-done((bf16[16,2,8,512]{3,2,1,0:T(8,128)(2,1)S(1)}, bf16[16,2,8,512]{3,2,1,0:T(8,128)(2,1)S(1)}, u32[]{:S(2)}, u32[]{:S(2)}) %collective-permute-start.15) | collective-permute-done | bytes 262176 | tf_op jit(solution)/shard_map/ppermute | solution.py:544
  63.2 6.2 %project.5 = (f32[3,256,1536]{2,1,0:T(8,128)S(1)}, f32[256,128]{1,0:T(8,128)S(1)}, bf16[3,512,1536]{2,1,0:T(8,128)(2,1)S(1)}) custom-call(s32[8]{0:T(128)S(1)} %stack.35.at, bf16[16,2,8,512]{3,2,1,0:T(8,128)(2,1)S(1)} %assemble.2.refs_0_, bf16[16,2,8,512]{3,2,1,0:T(8,128)(2,1)S(1)} %collective-permute-done.13.refs_1_, ...), custom_call_target="tpu_custom_call", output_to_operand_aliasing={{0}: (6, {}), {1}: (7, {})} | custom-call | flops 3623878656 | bytes 18874368 | tf_op jit(solution)/shard_map/project/pallas_call | solution.py:245
  69.4 0.0 collective-permute-done.6.refs_0_
  69.4 3.2 %temporal.1 = bf16[16,2,8,1536]{3,2,1,0:T(8,128)(2,1)S(1)} custom-call(s32[8]{0:T(128)S(1)} %stack.35.at, bf16[16,2,8,512]{3,2,1,0:T(8,128)(2,1)S(1)} %collective-permute-done.6.refs_0_, f32[1,3072]{1,0:T(1,128)S(1)} %bitcast.23, f32[3,256,1536]{2,1,0:T(8,128)S(1)} %get-tuple-element.34.refs_2_, f32[256,128]{1,0:T(8,128)S(1)} %get-tuple-element.35.refs_3_, ...), custom_call_target="tpu_custom_call" | custom-call | flops 1207959552 | bytes 786432 | tf_op jit(solution)/shard_map/temporal/pallas_call | solution.py:351
  72.6 25.6 %all_to_all.10 = bf16[32,8,1536]{2,1,0:T(8,128)(2,1)S(1)} all-to-all(bf16[32,8,1536]{2,1,0:T(8,128)(2,1)S(1)} %bitcast.16), channel_id=1, replica_groups=mesh['frame'=16,'row'=2] {'frame','row'}, dimensions={0} | all-to-all | bytes 1572864 | tf_op jit(solution)/shard_map/all_to_all | solution.py:603
  98.2 0.9 copy.15
  (7 shorter events, 0.0 us)
Async XLA Ops:
  1.1 10.9 %collective-permute-start.14 = (bf16[3,128,512]{2,1,0:T(8,128)(2,1)S(1)}, bf16[3,128,512]{2,1,0:T(8,128)(2,1)S(1)}, u32[]{:S(2)}, u32[]{:S(2)}) collective-permute-start(bf16[3,128,512]{2,1,0:T(8,128)(2,1)S(1)} %pack.5), channel_id=1, source_target_pairs={{0,1},{1,0},{2,3},{3,2},{4,5},{5,4},{6,7},{7,6},{8,9},{9,8},{10,11... | collective-permute-start | bytes 1179656 | tf_op jit(solution)/shard_map/ppermute | solution.py:544
  4.2 19.5 %collective-permute-start.7 = (bf16[3,128,512]{2,1,0:T(8,128)(2,1)S(1)}, bf16[3,128,512]{2,1,0:T(8,128)(2,1)S(1)}, u32[]{:S(2)}, u32[]{:S(2)}) collective-permute-start(bf16[3,128,512]{2,1,0:T(8,128)(2,1)S(1)} %pack.4), channel_id=1, source_target_pairs={{0,1},{1,0},{2,3},{3,2},{4,5},{5,4},{6,7},{7,6},{8,9},{9,8},{10,11... | collective-permute-start | bytes 1179656 | tf_op jit(solution)/shard_map/ppermute | solution.py:544
  5.4 24.5 %collective-permute-start = (bf16[3,128,512]{2,1,0:T(8,128)(2,1)S(1)}, bf16[3,128,512]{2,1,0:T(8,128)(2,1)S(1)}, u32[]{:S(2)}, u32[]{:S(2)}) collective-permute-start(bf16[3,128,512]{2,1,0:T(8,128)(2,1)S(1)} %pack.3), channel_id=1, source_target_pairs={{0,1},{1,0},{2,3},{3,2},{4,5},{5,4},{6,7},{7,6},{8,9},{9,8},{10,11... | collective-permute-start | bytes 1179656 | tf_op jit(solution)/shard_map/ppermute | solution.py:544
  15.2 37.8 %copy-start = (f32[3072]{0:T(1024)S(1)}, f32[3072]{0:T(1024)}, u32[]{:S(2)}) copy-start(f32[3072]{0:T(1024)} %param.8) | copy-start | bytes 36868
  15.2 35.7 %all-to-all-start = ((bf16[16,2,8,512]{3,2,1,0:T(8,128)(2,1)}), bf16[16,2,8,512]{3,2,1,0:T(8,128)(2,1)S(1)}, u32[]{:S(2)}, u32[]{:S(2)}) async-start(bf16[16,2,8,512]{3,2,1,0:T(8,128)(2,1)} %spatial.5), calls=%async_computation | async-start | bytes 524288 | tf_op jit(solution)/shard_map/all_to_all | solution.py:564
  26.3 9.7 %collective-permute-start.10 = (bf16[4,2,8,512]{3,2,1,0:T(8,128)(2,1)S(1)}, bf16[4,2,8,512]{3,2,1,0:T(8,128)(2,1)S(1)}, u32[]{:S(2)}, u32[]{:S(2)}) collective-permute-start(bf16[4,2,8,512]{3,2,1,0:T(8,128)(2,1)S(1)} %get-tuple-element.28), channel_id=1, source_target_pairs={{0,24},{2,26},{4,28},{6,30},{8,16},{10,18},{12,20},{14,22},{16,8},... | collective-permute-start | bytes 196616 | tf_op jit(solution)/shard_map/ppermute | solution.py:492
  29.5 6.6 %collective-permute-start.8 = (bf16[4,2,8,512]{3,2,1,0:T(8,128)(2,1)S(1)}, bf16[4,2,8,512]{3,2,1,0:T(8,128)(2,1)S(1)}, u32[]{:S(2)}, u32[]{:S(2)}) collective-permute-start(bf16[4,2,8,512]{3,2,1,0:T(8,128)(2,1)S(1)} %get-tuple-element.26), channel_id=1, source_target_pairs={{0,8},{2,10},{4,12},{6,14},{8,0},{10,2},{12,4},{14,6},{16,24},{18,... | collective-permute-start | bytes 196616 | tf_op jit(solution)/shard_map/ppermute | solution.py:492
  29.5 9.3 %collective-permute-start.9 = (bf16[4,2,8,512]{3,2,1,0:T(8,128)(2,1)S(1)}, bf16[4,2,8,512]{3,2,1,0:T(8,128)(2,1)S(1)}, u32[]{:S(2)}, u32[]{:S(2)}) collective-permute-start(bf16[4,2,8,512]{3,2,1,0:T(8,128)(2,1)S(1)} %get-tuple-element.27), channel_id=1, source_target_pairs={{0,16},{2,18},{4,20},{6,22},{8,24},{10,26},{12,28},{14,30},{16,0},... | collective-permute-start | bytes 196616 | tf_op jit(solution)/shard_map/ppermute | solution.py:492
  32.5 7.6 %collective-permute-start.1 = (bf16[4,2,8,512]{3,2,1,0:T(8,128)(2,1)S(1)}, bf16[4,2,8,512]{3,2,1,0:T(8,128)(2,1)S(1)}, u32[]{:S(2)}, u32[]{:S(2)}) collective-permute-start(bf16[4,2,8,512]{3,2,1,0:T(8,128)(2,1)S(1)} %get-tuple-element.22), channel_id=1, source_target_pairs={{0,8},{2,10},{4,12},{6,14},{8,0},{10,2},{12,4},{14,6},{16,24},{18,... | collective-permute-start | bytes 196616 | tf_op jit(solution)/shard_map/ppermute | solution.py:492
  33.6 8.0 %collective-permute-start.2 = (bf16[4,2,8,512]{3,2,1,0:T(8,128)(2,1)S(1)}, bf16[4,2,8,512]{3,2,1,0:T(8,128)(2,1)S(1)}, u32[]{:S(2)}, u32[]{:S(2)}) collective-permute-start(bf16[4,2,8,512]{3,2,1,0:T(8,128)(2,1)S(1)} %get-tuple-element.23), channel_id=1, source_target_pairs={{0,16},{2,18},{4,20},{6,22},{8,24},{10,26},{12,28},{14,30},{16,0},... | collective-permute-start | bytes 196616 | tf_op jit(solution)/shard_map/ppermute | solution.py:492
  36.0 5.6 %collective-permute-start.3 = (bf16[4,2,8,512]{3,2,1,0:T(8,128)(2,1)S(1)}, bf16[4,2,8,512]{3,2,1,0:T(8,128)(2,1)S(1)}, u32[]{:S(2)}, u32[]{:S(2)}) collective-permute-start(bf16[4,2,8,512]{3,2,1,0:T(8,128)(2,1)S(1)} %get-tuple-element.24), channel_id=1, source_target_pairs={{0,24},{2,26},{4,28},{6,30},{8,16},{10,18},{12,20},{14,22},{16,8},... | collective-permute-start | bytes 196616 | tf_op jit(solution)/shard_map/ppermute | solution.py:492
  38.8 4.2 %collective-permute-start.11 = (bf16[8,2,8,512]{3,2,1,0:T(8,128)(2,1)S(1)}, bf16[8,2,8,512]{3,2,1,0:T(8,128)(2,1)S(1)}, u32[]{:S(2)}, u32[]{:S(2)}) collective-permute-start(bf16[8,2,8,512]{3,2,1,0:T(8,128)(2,1)S(1)} %collect.6), channel_id=1, source_target_pairs={{0,4},{2,6},{4,0},{6,2},{8,12},{10,14},{12,8},{14,10},{16,20},{18,... | collective-permute-start | bytes 393224 | tf_op jit(solution)/shard_map/ppermute | solution.py:492
  41.6 6.1 %collective-permute-start.4 = (bf16[8,2,8,512]{3,2,1,0:T(8,128)(2,1)S(1)}, bf16[8,2,8,512]{3,2,1,0:T(8,128)(2,1)S(1)}, u32[]{:S(2)}, u32[]{:S(2)}) collective-permute-start(bf16[8,2,8,512]{3,2,1,0:T(8,128)(2,1)S(1)} %collect.4), channel_id=1, source_target_pairs={{0,4},{2,6},{4,0},{6,2},{8,12},{10,14},{12,8},{14,10},{16,20},{18,... | collective-permute-start | bytes 393224 | tf_op jit(solution)/shard_map/ppermute | solution.py:492
  43.0 6.1 %collective-permute-start.12 = (bf16[8,2,8,512]{3,2,1,0:T(8,128)(2,1)S(1)}, bf16[8,2,8,512]{3,2,1,0:T(8,128)(2,1)S(1)}, u32[]{:S(2)}, u32[]{:S(2)}) collective-permute-start(bf16[8,2,8,512]{3,2,1,0:T(8,128)(2,1)S(1)} %collect.7), channel_id=1, source_target_pairs={{0,2},{2,0},{4,6},{6,4},{8,10},{10,8},{12,14},{14,12},{16,18},{18,... | collective-permute-start | bytes 393224 | tf_op jit(solution)/shard_map/ppermute | solution.py:492
  47.7 3.5 %collective-permute-start.5 = (bf16[8,2,8,512]{3,2,1,0:T(8,128)(2,1)S(1)}, bf16[8,2,8,512]{3,2,1,0:T(8,128)(2,1)S(1)}, u32[]{:S(2)}, u32[]{:S(2)}) collective-permute-start(bf16[8,2,8,512]{3,2,1,0:T(8,128)(2,1)S(1)} %collect.5), channel_id=1, source_target_pairs={{0,2},{2,0},{4,6},{6,4},{8,10},{10,8},{12,14},{14,12},{16,18},{18,... | collective-permute-start | bytes 393224 | tf_op jit(solution)/shard_map/ppermute | solution.py:492
  49.7 11.7 %collective-permute-start.13 = (bf16[16,2,8,512]{3,2,1,0:T(8,128)(2,1)S(1)}, bf16[16,2,8,512]{3,2,1,0:T(8,128)(2,1)S(1)}, u32[]{:S(2)}, u32[]{:S(2)}) collective-permute-start(bf16[16,2,8,512]{3,2,1,0:T(8,128)(2,1)S(1)} %assemble.3.refs_0_), channel_id=1, source_target_pairs={{0,1},{1,0},{2,3},{3,2},{4,5},{5,4},{6,7},{7,6},{8,9},{9,8},{10,11... | collective-permute-start | bytes 786440 | tf_op jit(solution)/shard_map/ppermute | solution.py:544
  50.9 12.2 %collective-permute-start.15 = (bf16[16,2,8,512]{3,2,1,0:T(8,128)(2,1)S(1)}, bf16[16,2,8,512]{3,2,1,0:T(8,128)(2,1)S(1)}, u32[]{:S(2)}, u32[]{:S(2)}) collective-permute-start(bf16[16,2,8,512]{3,2,1,0:T(8,128)(2,1)S(1)} %all-to-all-done.refs_0_), channel_id=1, source_target_pairs={{0,1},{1,0},{2,3},{3,2},{4,5},{5,4},{6,7},{7,6},{8,9},{9,8},{10,11... | collective-permute-start | bytes 786440 | tf_op jit(solution)/shard_map/ppermute | solution.py:544
  51.8 17.7 %collective-permute-start.6 = (bf16[16,2,8,512]{3,2,1,0:T(8,128)(2,1)S(1)}, bf16[16,2,8,512]{3,2,1,0:T(8,128)(2,1)S(1)}, u32[]{:S(2)}, u32[]{:S(2)}) collective-permute-start(bf16[16,2,8,512]{3,2,1,0:T(8,128)(2,1)S(1)} %assemble.2.refs_0_), channel_id=1, source_target_pairs={{0,1},{1,0},{2,3},{3,2},{4,5},{5,4},{6,7},{7,6},{8,9},{9,8},{10,11... | collective-permute-start | bytes 786440 | tf_op jit(solution)/shard_map/ppermute | solution.py:544

commit v9 on v8

--- a/solution.py
+++ b/solution.py
@@ -31,22 +31,26 @@
 VMEM = pl.BlockSpec(memory_space=pltpu.VMEM)
 
 
+def with_scalars(kernel, count):
+    return lambda *refs: kernel([ref[0] for ref in refs[:count]], *refs[count:])
+
+
 def weighted(scores):
     weights = jnp.exp2((scores - jnp.max(scores, axis=1, keepdims=True)) * EXPONENT)
     return weights, 1.0 / jnp.sum(weights, axis=1, keepdims=True)
 
 
-def spatial_kernel(at, *refs, index, pool, tiled, lines):
+def spatial_kernel(at, *refs, pool, tiled, lines):
     inputs, rest, (own, factor, sems) = refs[:3], refs[3:-3], refs[-3:]
     if lines:
         rest, outs, out, own = rest[: -lines - 1], rest[-lines - 1 : -1], rest[-1], own
         received, gain = rest[:-1], rest[-1]
-        frame = at[at.shape[0] - 1]
+        frame = at[1]
     else:
         received, gain, out = rest[:-2], rest[-2], rest[-1]
     ways = len(received) + 1
     tokens, width = own.shape[1:]
-    lanes = pl.ds(pl.multiple_of(at[index] * HEAD, HEAD), width)
+    lanes = pl.ds(pl.multiple_of(at[0] * HEAD, HEAD), width)
     copies = [
         pltpu.make_async_copy(ref.at[0, :, lanes], own.at[i], sems.at[i])
         for i, ref in enumerate(inputs)
@@ -102,7 +106,7 @@
 TOGETHER = 4
 
 
-def spatial(q, k, v, received, gain, at, index, frames, lines=0):
+def spatial(q, k, v, received, gain, at, frames, lines=0):
     tokens = q.shape[1]
     width = received[0].shape[2] if received else q.shape[2]
     ways = len(received) + 1
@@ -111,8 +115,8 @@
     shape = (frames, ways, slot, width) if tiled else (ways, tokens, width)
     hbm = pl.BlockSpec(memory_space=pl.ANY)
     out = pl.pallas_call(
-        partial(
-            spatial_kernel, index=index, pool=tokens * ways // AGENTS, tiled=tiled, lines=lines
+        with_scalars(
+            partial(spatial_kernel, pool=tokens * ways // AGENTS, tiled=tiled, lines=lines), len(at)
         ),
         out_shape=(
             [jax.ShapeDtypeStruct((frames // lines, *shape[1:]), jnp.bfloat16)] * lines
@@ -120,7 +124,7 @@
             else jax.ShapeDtypeStruct(shape, jnp.bfloat16)
         ),
         grid_spec=pltpu.PrefetchScalarGridSpec(
-            num_scalar_prefetch=1,
+            num_scalar_prefetch=len(at),
             grid=(),
             in_specs=[hbm] * 3 + [VMEM] * len(received) + [hbm],
             out_specs=[VMEM] * lines if lines else VMEM,
@@ -138,7 +142,7 @@
         ),
         compiler_params=pltpu.CompilerParams(vmem_limit_bytes=16 << 20),
         name="spatial",
-    )(at, q, k, v, *received, gain)
+    )(*at, q, k, v, *received, gain)
     if not tiled and not lines:
         out = out.reshape(ways, frames, slot, width).transpose(1, 0, 2, 3)
     return out
@@ -159,7 +163,7 @@
     return total
 
 
-AHEAD = 4
+AHEAD = 9
 
 
 def hold(held, xs, depths, shifts, tokens, ways, tiled):
@@ -173,7 +177,7 @@
 
 
 def project_kernel(
-    at, *refs, groups, places, shifts, depths, carried, given, tokens, ways, tiled
+    at, *refs, groups, shifts, depths, carried, given, tokens, ways, tiled
 ):
     xs = refs[: len(shifts)]
     weight, gain = refs[len(shifts) : len(shifts) + 2]
@@ -191,7 +195,7 @@
     for i, target in enumerate(targets):
         if i < given:
             continue
-        rows = pl.ds(pl.multiple_of(at[places[i]] * HEAD, HEAD), target.shape[1])
+        rows = pl.ds(pl.multiple_of(at[i] * HEAD, HEAD), target.shape[1])
         for c in range(3):
             copies.append(
                 pltpu.make_async_copy(weight.at[c, rows, :], target.at[c], sems.at[3 * i + c])
@@ -211,7 +215,7 @@
             ways,
             tiled,
         )
-        lanes = pl.ds(pl.multiple_of(at[places[i]] * HEAD, HEAD), held[i].shape[1])
+        lanes = pl.ds(pl.multiple_of(at[i] * HEAD, HEAD), held[i].shape[1])
         part = squares(held[i][...], 1.0 / gain[:, lanes])
         total = part if total is None else total + part
         for c in range(3):
@@ -236,17 +240,17 @@
 
 
 def project(
-    groups, places, arrays, shifts, at, later, carried, given, weight, gain, tokens, ways, tiled
+    groups, arrays, shifts, at, later, carried, given, weight, gain, tokens, ways, tiled
 ):
     rows = tokens * ways
     width = weight.shape[2]
     depths = [x.shape[-1] for x in arrays]
     sums = [sum(depths[m] for m in g) for g in groups]
     return pl.pallas_call(
-        partial(
+        with_scalars(
+            partial(
             project_kernel,
             groups=(*groups, *[None] * len(later)),
-            places=places,
             shifts=shifts,
             depths=depths,
             carried=bool(carried),
@@ -254,6 +258,8 @@
             tokens=tokens,
             ways=ways,
             tiled=tiled,
+            ),
+            len(at),
         ),
         out_shape=(
             pltpu.VMEM((3, rows, width), jnp.float32),
@@ -261,7 +267,7 @@
             *[pltpu.VMEM((3, depth, width), weight.dtype) for depth in later],
         ),
         grid_spec=pltpu.PrefetchScalarGridSpec(
-            num_scalar_prefetch=1,
+            num_scalar_prefetch=len(at),
             grid=(),
             in_specs=[VMEM] * len(arrays)
             + [pl.BlockSpec(memory_space=pl.ANY)]
@@ -277,14 +283,14 @@
             transcendentals=0,
         ),
         input_output_aliases=(
-            {len(arrays) + 3: 0, len(arrays) + 4: 1} if carried else {}
+            {len(at) + len(arrays) + 2: 0, len(at) + len(arrays) + 3: 1} if carried else {}
         ),
         compiler_params=pltpu.CompilerParams(vmem_limit_bytes=32 << 20),
         name="project",
-    )(at, *arrays, weight, gain, *carried, *given)
-
-
-def temporal_kernel(at, *refs, places, shifts, heads, tokens, ways, slot, tiled):
+    )(*at, *arrays, weight, gain, *carried, *given)
+
+
+def temporal_kernel(at, *refs, shifts, heads, tokens, ways, slot, tiled):
     count = len(shifts)
     xs = refs[:count]
     gain, acc, ss = refs[count : count + 3]
@@ -298,7 +304,7 @@
         for i in range(count):
             depth = ws[i].shape[1]
             hold(held[i], [xs[i]], [depth], [shifts[i]], tokens, ways, tiled)
-            lanes = pl.ds(pl.multiple_of(at[places[i]] * HEAD, HEAD), depth)
+            lanes = pl.ds(pl.multiple_of(at[i] * HEAD, HEAD), depth)
             total = total + squares(held[i][...], 1.0 / gain[:, lanes])
         mean = jnp.sum(total, axis=1, keepdims=True) * (1.0 / D)
         rstd[...] = jnp.broadcast_to(lax.rsqrt(mean + epsilon), rstd.shape)
@@ -324,7 +330,7 @@
         for _, rows, cols in split
     ]
     weights = [weighted(x) for x in scores]
-    me = at[at.shape[0] - 2]
+    me = at[count]
     for (j, rows, cols), (w, r) in zip(split, weights):
         result = dot((w * r).astype(jnp.bfloat16), qkv[2][rows, cols]).astype(jnp.bfloat16)
         target = lax.rem(me + ways - j, ways)
@@ -334,7 +340,7 @@
             out[target, :, cols] = result
 
 
-def temporal(arrays, shifts, at, places, gain, carried, tokens, ways, slot, tiled):
+def temporal(arrays, shifts, at, gain, carried, tokens, ways, slot, tiled):
     rows = tokens * ways
     width = carried[0].shape[2]
     depths = [x.shape[-1] for x in arrays]
@@ -343,25 +349,27 @@
     step = heads * HEAD
     if tiled:
         shape = (frames, ways, slot, width)
-        out_spec = pl.BlockSpec((frames, ways, slot, step), lambda n, at: (0, 0, 0, n))
+        out_spec = pl.BlockSpec((frames, ways, slot, step), lambda n, *at: (0, 0, 0, n))
     else:
         shape = (ways, tokens, width)
-        out_spec = pl.BlockSpec((ways, tokens, step), lambda n, at: (0, 0, n))
+        out_spec = pl.BlockSpec((ways, tokens, step), lambda n, *at: (0, 0, n))
     operands = [*arrays, gain, *carried]
     out = pl.pallas_call(
-        partial(
+        with_scalars(
+            partial(
             temporal_kernel,
-            places=places,
             shifts=shifts,
             heads=heads,
             tokens=tokens,
             ways=ways,
             slot=slot,
             tiled=tiled,
+            ),
+            len(at),
         ),
         out_shape=jax.ShapeDtypeStruct(shape, jnp.bfloat16),
         grid_spec=pltpu.PrefetchScalarGridSpec(
-            num_scalar_prefetch=1,
+            num_scalar_prefetch=len(at),
             grid=(width // step,),
             in_specs=[VMEM] * len(operands),
             out_specs=out_spec,
@@ -375,7 +383,7 @@
         ),
         compiler_params=pltpu.CompilerParams(vmem_limit_bytes=16 << 20),
         name="temporal",
-    )(at, *operands)
+    )(*at, *operands)
     if not tiled:
         out = out.reshape(ways, frames, slot, width).transpose(1, 0, 2, 3)
     return out
@@ -455,7 +463,7 @@
 
 def assemble_kernel(at, *refs, places):
     out = refs[-1]
-    frame = at[at.shape[0] - 1]
+    frame = at[0]
     for ref, keys in zip(refs[:-1], places):
         for n, key in enumerate(keys):
             if key is not None:
@@ -538,7 +546,8 @@
     aligned = lambda i: group % chunks[i][1] == 0 and chunks[i][0] % chunks[i][1] == 0
     behind = [lax.rem(me + ways - k, ways) * group + c for c, _ in chunks for k in range(ways)]
     ahead = [lax.rem(me + k, ways) * group + c for c, _ in chunks for k in range(ways)]
-    table = jnp.stack(behind + [me, lax.axis_index("frame").astype(jnp.int32)])
+    frame = lax.axis_index("frame").astype(jnp.int32).reshape(1)
+    scalar = lambda key: behind[key[0] * ways + key[1]].reshape(1)
 
     def shift(x, k):
         return lax.ppermute(x, "row", [(i, (i + k) % ways) for i in range(ways)])
@@ -556,10 +565,17 @@
     for i, parts in enumerate(received):
         lines = stages(frames)[0] if staged and i != 1 else 0
         out = spatial(
-            spatial_q, spatial_k, spatial_v, parts, hbm(gain), table, i * ways, frames, lines
+            spatial_q,
+            spatial_k,
+            spatial_v,
+            parts,
+            hbm(gain),
+            (scalar((i, 0)), frame),
+            frames,
+            lines,
         )
         if lines:
-            pieces[i, 0] = spread_by_permutes(out, table, frames)
+            pieces[i, 0] = spread_by_permutes(out, frame, frames)
         else:
             out = lax.all_to_all(out, "frame", split_axis=0, concat_axis=0, tiled=True)
             pieces[i, 0] = out
@@ -575,7 +591,6 @@
     else:
         steps = [[key for i in range(last) for key in others(i)] + [[(i, 0) for i in range(last + 1)]]]
     final = [g[0] for g in others(last)]
-    place = lambda key: key[0] * ways + key[1]
     shared = dict(tokens=tokens, ways=ways, tiled=tiled)
     carried, given = (), ()
     for n, wanted in enumerate(steps):
@@ -583,10 +598,9 @@
         later = final if n == len(steps) - 1 else steps[n + 1][0] if n == len(steps) - 2 else []
         acc, ss, *brought = project(
             tuple(tuple(flat.index(key) for key in g) for g in wanted),
-            tuple(place(key) for key in [g[0] for g in wanted] + later),
             [pieces[key] for key in flat],
             tuple(k for _, k in flat),
-            table,
+            tuple(scalar(key) for key in [g[0] for g in wanted] + later),
             [chunks[i][1] * HEAD for i, _ in later],
             carried,
             given,
@@ -597,8 +611,8 @@
         carried, given = (acc, ss), brought
     carried = (*carried, *given)
     arrays, shifts = [pieces[key] for key in final], tuple(k for _, k in final)
-    places = tuple(place(key) for key in final)
-    out = temporal(arrays, shifts, table, places, gain, carried, slot=slot, **shared)
+    at = (*[scalar(key) for key in final], me.reshape(1))
+    out = temporal(arrays, shifts, at, gain, carried, slot=slot, **shared)
     out = out.reshape(frames * ways, slot, width)
     out = lax.all_to_all(out, ("frame", "row"), split_axis=0, concat_axis=0, tiled=True)
     out = out.reshape(frames, ways, slot, width).transpose(0, 2, 1, 3)

time: 99.5 us -> 98.4 us (0.989)
  Pallas kernels: 30.4 us -> 26.4 us
  waiting for transfers between devices: 11.2 us -> 14.2 us
    pallas_call x7, Pallas kernels: 26 us -> 23.1 us  [the longest x3 13.7 us: project(): pl.pallas_call(with_scalars(partial(project_kernel, groups=(*groups, *[No...]
    ppermute x6, waiting for transfers between devices: 6.89 us -> 8.79 us  [shift(): return lax.ppermute(x, 'row', [(i, (i + k) % ways) for i in range(ways)])]
    pallas_call x2, Pallas kernels: 1.12 us -> 0.04 us  [assemble(): pl.pallas_call(partial(assemble_kernel, places=places), out_shape=jax.Sha...]
    ppermute x10, waiting for transfers between devices: 4.35 us -> 5.4 us  [swap(): return lax.ppermute(x, 'frame', [(i, i ^ key) for i in range(frames)])]
  transfers between devices with their start and end apart: 17 -> 17, of which waited for: 5 -> 5; matrix products, arithmetic and copies ran while one was open for 0% -> 0% of each run, Pallas kernels for 26% -> 23%
where the time goes in v9:
time: 98.4 us; the launch traced here: 98.1 us
  starting transfers between devices  30.8 us (31%)
  Pallas kernels  26.4 us (27%)
  blocking collectives  25.7 us (26%)
  waiting for transfers between devices  14.2 us (14%)
    all_to_all x1, blocking collectives, local(): lax.all_to_all(out, ('frame', 'row'), split_axis=0, concat_axis=0, tiled=...  25.7 us
    ppermute x10, starting transfers between devices, swap(): return lax.ppermute(x, 'frame', [(i, i ^ key) for i in range(frames)])  15.8 us
    pallas_call x3, Pallas kernels, project(): pl.pallas_call(with_scalars(partial(project_kernel, groups=(*groups, *[No...  13.7 us
    ppermute x6, waiting for transfers between devices, shift(): return lax.ppermute(x, 'row', [(i, (i + k) % ways) for i in range(ways)])  8.79 us
    all_to_all x1, starting transfers between devices, local(): out = lax.all_to_all(out, 'frame', split_axis=0, concat_axis=0, tiled=True)  8.49 us
    pallas_call x3, Pallas kernels, spatial(): pl.pallas_call(with_scalars(partial(spatial_kernel, pool=tokens * ways //...  6.74 us
    ppermute x6, starting transfers between devices, shift(): return lax.ppermute(x, 'row', [(i, (i + k) % ways) for i in range(ways)])  6.5 us
    ppermute x10, waiting for transfers between devices, swap(): return lax.ppermute(x, 'frame', [(i, i ^ key) for i in range(frames)])  5.4 us
  transfers between devices with their start and end apart: 17, of which 5 were waited for; matrix products, arithmetic and copies ran while one was open for 0% of the time, Pallas kernels for 23%

profile of v9, /device:TPU:1, one launch (start us, length us, event | category | flops | bytes accessed | tf_op | source)
XLA Modules:
  0.0 98.1 jit_solution(15587345307763837117)
XLA Ops:
  0.0 1.1 %pack.5 = bf16[3,128,512]{2,1,0:T(8,128)(2,1)S(1)} custom-call(s32[1]{0:T(128)} %bitcast.6.at.refs_2_, bf16[1,128,3072]{2,1,0:T(8,128)(2,1)} %refs_2_.5, bf16[1,128,3072]{2,1,0:T(8,128)(2,1)} %refs_3_.5, bf16[1,128,3072]{2,1,0:T(8,128)(2,1)} %refs_4_.5), custom_call_target="tpu_custom_call" | custom-call | tf_op jit(solution)/shard_map/pack/pallas_call | solution.py:415
  1.1 2.1 %collective-permute-start.14 = (bf16[3,128,512]{2,1,0:T(8,128)(2,1)S(1)}, bf16[3,128,512]{2,1,0:T(8,128)(2,1)S(1)}, u32[]{:S(2)}, u32[]{:S(2)}) collective-permute-start(bf16[3,128,512]{2,1,0:T(8,128)(2,1)S(1)} %pack.5), channel_id=1, source_target_pairs={{0,1},{1,0},{2,3},{3,2},{4,5},{5,4},{6,7},{7,6},{8,9},{9,8},{10,11... | collective-permute-start | bytes 1179656 | tf_op jit(solution)/shard_map/ppermute | solution.py:553
  3.2 1.1 %pack.4 = bf16[3,128,512]{2,1,0:T(8,128)(2,1)S(1)} custom-call(s32[1]{0:T(128)} %bitcast.5.at.refs_1_, bf16[1,128,3072]{2,1,0:T(8,128)(2,1)} %refs_2_.5, bf16[1,128,3072]{2,1,0:T(8,128)(2,1)} %refs_3_.5, bf16[1,128,3072]{2,1,0:T(8,128)(2,1)} %refs_4_.5), custom_call_target="tpu_custom_call" | custom-call | tf_op jit(solution)/shard_map/pack/pallas_call | solution.py:415
  4.2 0.1 collective-permute-start.7
  4.3 1.1 %pack.3 = bf16[3,128,512]{2,1,0:T(8,128)(2,1)S(1)} custom-call(s32[1]{0:T(128)} %bitcast.at.refs_3_.refs_0_, bf16[1,128,3072]{2,1,0:T(8,128)(2,1)} %refs_2_.5, bf16[1,128,3072]{2,1,0:T(8,128)(2,1)} %refs_3_.5, bf16[1,128,3072]{2,1,0:T(8,128)(2,1)} %refs_4_.5), custom_call_target="tpu_custom_call" | custom-call | tf_op jit(solution)/shard_map/pack/pallas_call | solution.py:415
  5.4 1.5 %collective-permute-start = (bf16[3,128,512]{2,1,0:T(8,128)(2,1)S(1)}, bf16[3,128,512]{2,1,0:T(8,128)(2,1)S(1)}, u32[]{:S(2)}, u32[]{:S(2)}) collective-permute-start(bf16[3,128,512]{2,1,0:T(8,128)(2,1)S(1)} %pack.3), channel_id=1, source_target_pairs={{0,1},{1,0},{2,3},{3,2},{4,5},{5,4},{6,7},{7,6},{8,9},{9,8},{10,11... | collective-permute-start | bytes 1179656 | tf_op jit(solution)/shard_map/ppermute | solution.py:553
  6.9 5.1 %collective-permute-done.14.refs_5_ = bf16[3,128,512]{2,1,0:T(8,128)(2,1)S(1)} collective-permute-done((bf16[3,128,512]{2,1,0:T(8,128)(2,1)S(1)}, bf16[3,128,512]{2,1,0:T(8,128)(2,1)S(1)}, u32[]{:S(2)}, u32[]{:S(2)}) %collective-permute-start.14) | collective-permute-done | bytes 393248 | tf_op jit(solution)/shard_map/ppermute | solution.py:553
  12.0 2.7 %spatial.5 = bf16[16,2,8,512]{3,2,1,0:T(8,128)(2,1)} custom-call(s32[1]{0:T(128)} %bitcast.8.refs_0_, s32[1]{0:T(128)} %bitcast.2.refs_1_.at, bf16[1,128,3072]{2,1,0:T(8,128)(2,1)} %refs_2_.5, bf16[1,128,3072]{2,1,0:T(8,128)(2,1)} %refs_3_.5, bf16[1,128,3072]{2,1,0:T(8,128)(2,1)} %refs_4_.5, bf16[3,128,512]{2,1,0:T(8,128)(2,1)S(1)} %collective-permute-done.14.refs_5_, ...), custom_call_target="tpu_custom_call" | custom-call | flops 167772160 | bytes 1310720 | tf_op jit(solution)/shard_map/spatial/pallas_call | solution.py:117
  14.7 0.0 copy-start
  14.7 8.5 %all-to-all-start = ((bf16[16,2,8,512]{3,2,1,0:T(8,128)(2,1)}), bf16[16,2,8,512]{3,2,1,0:T(8,128)(2,1)S(1)}, u32[]{:S(2)}, u32[]{:S(2)}) async-start(bf16[16,2,8,512]{3,2,1,0:T(8,128)(2,1)} %spatial.5), calls=%async_computation | async-start | bytes 524288 | tf_op jit(solution)/shard_map/all_to_all | solution.py:580
  23.2 0.0 collective-permute-done.7.refs_5_
  23.2 2.0 %spatial.4 = (bf16[4,2,8,512]{3,2,1,0:T(8,128)(2,1)S(1)}, bf16[4,2,8,512]{3,2,1,0:T(8,128)(2,1)S(1)}, bf16[4,2,8,512]{3,2,1,0:T(8,128)(2,1)S(1)}, bf16[4,2,8,512]{3,2,1,0:T(8,128)(2,1)S(1)}) custom-call(s32[1]{0:T(128)} %bitcast.7.refs_0_, s32[1]{0:T(128)} %bitcast.2.refs_1_.at, bf16[1,128,3072]{2,1,0:T(8,128)(2,1)} %refs_2_.5, ...), custom_call_target="tpu_custom_call" | custom-call | flops 167772160 | bytes 1310720 | tf_op jit(solution)/shard_map/spatial/pallas_call | solution.py:117
  25.2 3.2 %collective-permute-start.10 = (bf16[4,2,8,512]{3,2,1,0:T(8,128)(2,1)S(1)}, bf16[4,2,8,512]{3,2,1,0:T(8,128)(2,1)S(1)}, u32[]{:S(2)}, u32[]{:S(2)}) collective-permute-start(bf16[4,2,8,512]{3,2,1,0:T(8,128)(2,1)S(1)} %get-tuple-element.28), channel_id=1, source_target_pairs={{0,24},{2,26},{4,28},{6,30},{8,16},{10,18},{12,20},{14,22},{16,8},... | collective-permute-start | bytes 196616 | tf_op jit(solution)/shard_map/ppermute | solution.py:500
  28.4 0.0 collective-permute-start.8
  28.4 0.4 collective-permute-start.9
  28.8 0.0 collective-permute-done.refs_5_
  28.8 2.0 %spatial.3 = (bf16[4,2,8,512]{3,2,1,0:T(8,128)(2,1)S(1)}, bf16[4,2,8,512]{3,2,1,0:T(8,128)(2,1)S(1)}, bf16[4,2,8,512]{3,2,1,0:T(8,128)(2,1)S(1)}, bf16[4,2,8,512]{3,2,1,0:T(8,128)(2,1)S(1)}) custom-call(s32[1]{0:T(128)} %bitcast.3.refs_0_.refs_1_, s32[1]{0:T(128)} %bitcast.2.refs_1_.at, bf16[1,128,3072]{2,1,0:T(8,128)(2,1)} %refs_2_.5, ...), custom_call_target="tpu_custom_call" | custom-call | flops 167772160 | bytes 1310720 | tf_op jit(solution)/shard_map/spatial/pallas_call | solution.py:117
  30.9 1.3 %collective-permute-start.1 = (bf16[4,2,8,512]{3,2,1,0:T(8,128)(2,1)S(1)}, bf16[4,2,8,512]{3,2,1,0:T(8,128)(2,1)S(1)}, u32[]{:S(2)}, u32[]{:S(2)}) collective-permute-start(bf16[4,2,8,512]{3,2,1,0:T(8,128)(2,1)S(1)} %get-tuple-element.22), channel_id=1, source_target_pairs={{0,8},{2,10},{4,12},{6,14},{8,0},{10,2},{12,4},{14,6},{16,24},{18,... | collective-permute-start | bytes 196616 | tf_op jit(solution)/shard_map/ppermute | solution.py:500
  32.2 2.3 %collective-permute-start.2 = (bf16[4,2,8,512]{3,2,1,0:T(8,128)(2,1)S(1)}, bf16[4,2,8,512]{3,2,1,0:T(8,128)(2,1)S(1)}, u32[]{:S(2)}, u32[]{:S(2)}) collective-permute-start(bf16[4,2,8,512]{3,2,1,0:T(8,128)(2,1)S(1)} %get-tuple-element.23), channel_id=1, source_target_pairs={{0,16},{2,18},{4,20},{6,22},{8,24},{10,26},{12,28},{14,30},{16,0},... | collective-permute-start | bytes 196616 | tf_op jit(solution)/shard_map/ppermute | solution.py:500
  34.5 0.0 collective-permute-done.10.refs_3_
  34.5 0.0 collective-permute-start.3
  34.5 0.0 collective-permute-done.8.refs_1_
  34.5 3.7 %collective-permute-done.9.refs_2_ = bf16[4,2,8,512]{3,2,1,0:T(8,128)(2,1)S(1)} collective-permute-done((bf16[4,2,8,512]{3,2,1,0:T(8,128)(2,1)S(1)}, bf16[4,2,8,512]{3,2,1,0:T(8,128)(2,1)S(1)}, u32[]{:S(2)}, u32[]{:S(2)}) %collective-permute-start.9) | collective-permute-done | bytes 65568 | tf_op jit(solution)/shard_map/ppermute | solution.py:500
  38.3 1.2 %collective-permute-start.11 = (bf16[8,2,8,512]{3,2,1,0:T(8,128)(2,1)S(1)}, bf16[8,2,8,512]{3,2,1,0:T(8,128)(2,1)S(1)}, u32[]{:S(2)}, u32[]{:S(2)}) collective-permute-start(bf16[8,2,8,512]{3,2,1,0:T(8,128)(2,1)S(1)} %collect.6), channel_id=1, source_target_pairs={{0,4},{2,6},{4,0},{6,2},{8,12},{10,14},{12,8},{14,10},{16,20},{18,... | collective-permute-start | bytes 393224 | tf_op jit(solution)/shard_map/ppermute | solution.py:500
  39.5 0.0 collective-permute-done.1.refs_1_
  39.5 1.5 %collective-permute-done.2.refs_2_ = bf16[4,2,8,512]{3,2,1,0:T(8,128)(2,1)S(1)} collective-permute-done((bf16[4,2,8,512]{3,2,1,0:T(8,128)(2,1)S(1)}, bf16[4,2,8,512]{3,2,1,0:T(8,128)(2,1)S(1)}, u32[]{:S(2)}, u32[]{:S(2)}) %collective-permute-start.2) | collective-permute-done | bytes 65568 | tf_op jit(solution)/shard_map/ppermute | solution.py:500
  41.0 0.0 collective-permute-done.3.refs_3_
  41.1 1.2 %collective-permute-start.4 = (bf16[8,2,8,512]{3,2,1,0:T(8,128)(2,1)S(1)}, bf16[8,2,8,512]{3,2,1,0:T(8,128)(2,1)S(1)}, u32[]{:S(2)}, u32[]{:S(2)}) collective-permute-start(bf16[8,2,8,512]{3,2,1,0:T(8,128)(2,1)S(1)} %collect.4), channel_id=1, source_target_pairs={{0,4},{2,6},{4,0},{6,2},{8,12},{10,14},{12,8},{14,10},{16,20},{18,... | collective-permute-start | bytes 393224 | tf_op jit(solution)/shard_map/ppermute | solution.py:500
  42.3 0.1 collective-permute-done.11.refs_4_
  42.4 4.7 %collective-permute-start.12 = (bf16[8,2,8,512]{3,2,1,0:T(8,128)(2,1)S(1)}, bf16[8,2,8,512]{3,2,1,0:T(8,128)(2,1)S(1)}, u32[]{:S(2)}, u32[]{:S(2)}) collective-permute-start(bf16[8,2,8,512]{3,2,1,0:T(8,128)(2,1)S(1)} %collect.7), channel_id=1, source_target_pairs={{0,2},{2,0},{4,6},{6,4},{8,10},{10,8},{12,14},{14,12},{16,18},{18,... | collective-permute-start | bytes 393224 | tf_op jit(solution)/shard_map/ppermute | solution.py:500
  47.1 0.0 collective-permute-done.4.refs_4_
  47.1 1.4 %collective-permute-start.5 = (bf16[8,2,8,512]{3,2,1,0:T(8,128)(2,1)S(1)}, bf16[8,2,8,512]{3,2,1,0:T(8,128)(2,1)S(1)}, u32[]{:S(2)}, u32[]{:S(2)}) collective-permute-start(bf16[8,2,8,512]{3,2,1,0:T(8,128)(2,1)S(1)} %collect.5), channel_id=1, source_target_pairs={{0,2},{2,0},{4,6},{6,4},{8,10},{10,8},{12,14},{14,12},{16,18},{18,... | collective-permute-start | bytes 393224 | tf_op jit(solution)/shard_map/ppermute | solution.py:500
  48.5 0.0 collective-permute-done.12.refs_5_
  48.6 1.3 %collective-permute-start.13 = (bf16[16,2,8,512]{3,2,1,0:T(8,128)(2,1)S(1)}, bf16[16,2,8,512]{3,2,1,0:T(8,128)(2,1)S(1)}, u32[]{:S(2)}, u32[]{:S(2)}) collective-permute-start(bf16[16,2,8,512]{3,2,1,0:T(8,128)(2,1)S(1)} %assemble.3.refs_1_), channel_id=1, source_target_pairs={{0,1},{1,0},{2,3},{3,2},{4,5},{5,4},{6,7},{7,6},{8,9},{9,8},{10,11... | collective-permute-start | bytes 786440 | tf_op jit(solution)/shard_map/ppermute | solution.py:553
  49.8 0.0 all-to-all-done.refs_2_
  49.8 0.3 collective-permute-start.15
  50.1 0.0 collective-permute-done.5.refs_5_
  50.1 1.3 %collective-permute-start.6 = (bf16[16,2,8,512]{3,2,1,0:T(8,128)(2,1)S(1)}, bf16[16,2,8,512]{3,2,1,0:T(8,128)(2,1)S(1)}, u32[]{:S(2)}, u32[]{:S(2)}) collective-permute-start(bf16[16,2,8,512]{3,2,1,0:T(8,128)(2,1)S(1)} %assemble.2.refs_4_), channel_id=1, source_target_pairs={{0,1},{1,0},{2,3},{3,2},{4,5},{5,4},{6,7},{7,6},{8,9},{9,8},{10,11... | collective-permute-start | bytes 786440 | tf_op jit(solution)/shard_map/ppermute | solution.py:553
  51.4 0.0 copy-done
  51.4 3.2 %project.3 = (f32[3,256,1536]{2,1,0:T(8,128)S(1)}, f32[256,128]{1,0:T(8,128)S(1)}) custom-call(s32[1]{0:T(128)} %bitcast.7.refs_0_, bf16[16,2,8,512]{3,2,1,0:T(8,128)(2,1)S(1)} %assemble.3.refs_1_, bf16[3,3072,1536]{2,1,0:T(8,128)(2,1)} %bitcast.24, f32[1,3072]{1,0:T(1,128)S(1)} %bitcast.20), custom_call_target="tpu_custom_call" | custom-call | flops 1207959552 | bytes 4718592 | tf_op jit(solution)/shard_map/project/pallas_call | solution.py:249
  54.6 3.8 %project.4 = (f32[3,256,1536]{2,1,0:T(8,128)S(1)}, f32[256,128]{1,0:T(8,128)S(1)}, bf16[3,512,1536]{2,1,0:T(8,128)(2,1)S(1)}) custom-call(s32[1]{0:T(128)} %bitcast.8.refs_0_, s32[1]{0:T(128)} %bitcast.3.refs_0_.refs_1_, bf16[16,2,8,512]{3,2,1,0:T(8,128)(2,1)S(1)} %all-to-all-done.refs_2_, ...), custom_call_target="tpu_custom_call", output_to_operand_aliasing={{0}: (5, {}), {1}: (6, {})} | custom-call | flops 1207959552 | bytes 9437184 | tf_op jit(solution)/shard_map/project/pallas_call | solution.py:249
  58.4 0.0 collective-permute-done.13.refs_5_
  58.4 3.7 %collective-permute-done.15.refs_6_ = bf16[16,2,8,512]{3,2,1,0:T(8,128)(2,1)S(1)} collective-permute-done((bf16[16,2,8,512]{3,2,1,0:T(8,128)(2,1)S(1)}, bf16[16,2,8,512]{3,2,1,0:T(8,128)(2,1)S(1)}, u32[]{:S(2)}, u32[]{:S(2)}) %collective-permute-start.15) | collective-permute-done | bytes 262176 | tf_op jit(solution)/shard_map/ppermute | solution.py:553
  62.1 6.7 %project.5 = (f32[3,256,1536]{2,1,0:T(8,128)S(1)}, f32[256,128]{1,0:T(8,128)S(1)}, bf16[3,512,1536]{2,1,0:T(8,128)(2,1)S(1)}) custom-call(s32[1]{0:T(128)} %bitcast.3.refs_0_.refs_1_, s32[1]{0:T(128)} %bitcast.5.at.refs_1_, s32[1]{0:T(128)} %bitcast.6.at.refs_2_, s32[1]{0:T(128)} %bitcast.at.refs_3_.refs_0_, ...), custom_call_target="tpu_custom_call", output_to_operand_aliasing={{0}: (9, {}), {1}: (10, {})} | custom-call | flops 3623878656 | bytes 18874368 | tf_op jit(solution)/shard_map/project/pallas_call | solution.py:249
  68.8 0.0 collective-permute-done.6.refs_2_
  68.8 2.7 %temporal.1 = bf16[16,2,8,1536]{3,2,1,0:T(8,128)(2,1)S(1)} custom-call(s32[1]{0:T(128)} %bitcast.at.refs_3_.refs_0_, s32[1]{0:T(128)} %bitcast.1.refs_1_, bf16[16,2,8,512]{3,2,1,0:T(8,128)(2,1)S(1)} %collective-permute-done.6.refs_2_, f32[1,3072]{1,0:T(1,128)S(1)} %bitcast.23, f32[3,256,1536]{2,1,0:T(8,128)S(1)} %get-tuple-element.34.refs_4_, ...), custom_call_target="tpu_custom_call" | custom-call | flops 1207959552 | bytes 786432 | tf_op jit(solution)/shard_map/temporal/pallas_call | solution.py:357
  71.5 25.7 %all_to_all.10 = bf16[32,8,1536]{2,1,0:T(8,128)(2,1)S(1)} all-to-all(bf16[32,8,1536]{2,1,0:T(8,128)(2,1)S(1)} %bitcast.16), channel_id=1, replica_groups=mesh['frame'=16,'row'=2] {'frame','row'}, dimensions={0} | all-to-all | bytes 1572864 | tf_op jit(solution)/shard_map/all_to_all | solution.py:617
  97.2 0.9 copy.15
  (6 shorter events, 0.1 us)
Async XLA Ops:
  1.1 10.9 %collective-permute-start.14 = (bf16[3,128,512]{2,1,0:T(8,128)(2,1)S(1)}, bf16[3,128,512]{2,1,0:T(8,128)(2,1)S(1)}, u32[]{:S(2)}, u32[]{:S(2)}) collective-permute-start(bf16[3,128,512]{2,1,0:T(8,128)(2,1)S(1)} %pack.5), channel_id=1, source_target_pairs={{0,1},{1,0},{2,3},{3,2},{4,5},{5,4},{6,7},{7,6},{8,9},{9,8},{10,11... | collective-permute-start | bytes 1179656 | tf_op jit(solution)/shard_map/ppermute | solution.py:553
  4.2 19.0 %collective-permute-start.7 = (bf16[3,128,512]{2,1,0:T(8,128)(2,1)S(1)}, bf16[3,128,512]{2,1,0:T(8,128)(2,1)S(1)}, u32[]{:S(2)}, u32[]{:S(2)}) collective-permute-start(bf16[3,128,512]{2,1,0:T(8,128)(2,1)S(1)} %pack.4), channel_id=1, source_target_pairs={{0,1},{1,0},{2,3},{3,2},{4,5},{5,4},{6,7},{7,6},{8,9},{9,8},{10,11... | collective-permute-start | bytes 1179656 | tf_op jit(solution)/shard_map/ppermute | solution.py:553
  5.4 23.5 %collective-permute-start = (bf16[3,128,512]{2,1,0:T(8,128)(2,1)S(1)}, bf16[3,128,512]{2,1,0:T(8,128)(2,1)S(1)}, u32[]{:S(2)}, u32[]{:S(2)}) collective-permute-start(bf16[3,128,512]{2,1,0:T(8,128)(2,1)S(1)} %pack.3), channel_id=1, source_target_pairs={{0,1},{1,0},{2,3},{3,2},{4,5},{5,4},{6,7},{7,6},{8,9},{9,8},{10,11... | collective-permute-start | bytes 1179656 | tf_op jit(solution)/shard_map/ppermute | solution.py:553
  14.7 36.7 %copy-start = (f32[3072]{0:T(1024)S(1)}, f32[3072]{0:T(1024)}, u32[]{:S(2)}) copy-start(f32[3072]{0:T(1024)} %param.8) | copy-start | bytes 36868
  14.7 35.1 %all-to-all-start = ((bf16[16,2,8,512]{3,2,1,0:T(8,128)(2,1)}), bf16[16,2,8,512]{3,2,1,0:T(8,128)(2,1)S(1)}, u32[]{:S(2)}, u32[]{:S(2)}) async-start(bf16[16,2,8,512]{3,2,1,0:T(8,128)(2,1)} %spatial.5), calls=%async_computation | async-start | bytes 524288 | tf_op jit(solution)/shard_map/all_to_all | solution.py:580
  25.2 9.3 %collective-permute-start.10 = (bf16[4,2,8,512]{3,2,1,0:T(8,128)(2,1)S(1)}, bf16[4,2,8,512]{3,2,1,0:T(8,128)(2,1)S(1)}, u32[]{:S(2)}, u32[]{:S(2)}) collective-permute-start(bf16[4,2,8,512]{3,2,1,0:T(8,128)(2,1)S(1)} %get-tuple-element.28), channel_id=1, source_target_pairs={{0,24},{2,26},{4,28},{6,30},{8,16},{10,18},{12,20},{14,22},{16,8},... | collective-permute-start | bytes 196616 | tf_op jit(solution)/shard_map/ppermute | solution.py:500
  28.4 6.1 %collective-permute-start.8 = (bf16[4,2,8,512]{3,2,1,0:T(8,128)(2,1)S(1)}, bf16[4,2,8,512]{3,2,1,0:T(8,128)(2,1)S(1)}, u32[]{:S(2)}, u32[]{:S(2)}) collective-permute-start(bf16[4,2,8,512]{3,2,1,0:T(8,128)(2,1)S(1)} %get-tuple-element.26), channel_id=1, source_target_pairs={{0,8},{2,10},{4,12},{6,14},{8,0},{10,2},{12,4},{14,6},{16,24},{18,... | collective-permute-start | bytes 196616 | tf_op jit(solution)/shard_map/ppermute | solution.py:500
  28.4 9.8 %collective-permute-start.9 = (bf16[4,2,8,512]{3,2,1,0:T(8,128)(2,1)S(1)}, bf16[4,2,8,512]{3,2,1,0:T(8,128)(2,1)S(1)}, u32[]{:S(2)}, u32[]{:S(2)}) collective-permute-start(bf16[4,2,8,512]{3,2,1,0:T(8,128)(2,1)S(1)} %get-tuple-element.27), channel_id=1, source_target_pairs={{0,16},{2,18},{4,20},{6,22},{8,24},{10,26},{12,28},{14,30},{16,0},... | collective-permute-start | bytes 196616 | tf_op jit(solution)/shard_map/ppermute | solution.py:500
  30.9 8.6 %collective-permute-start.1 = (bf16[4,2,8,512]{3,2,1,0:T(8,128)(2,1)S(1)}, bf16[4,2,8,512]{3,2,1,0:T(8,128)(2,1)S(1)}, u32[]{:S(2)}, u32[]{:S(2)}) collective-permute-start(bf16[4,2,8,512]{3,2,1,0:T(8,128)(2,1)S(1)} %get-tuple-element.22), channel_id=1, source_target_pairs={{0,8},{2,10},{4,12},{6,14},{8,0},{10,2},{12,4},{14,6},{16,24},{18,... | collective-permute-start | bytes 196616 | tf_op jit(solution)/shard_map/ppermute | solution.py:500
  32.2 8.9 %collective-permute-start.2 = (bf16[4,2,8,512]{3,2,1,0:T(8,128)(2,1)S(1)}, bf16[4,2,8,512]{3,2,1,0:T(8,128)(2,1)S(1)}, u32[]{:S(2)}, u32[]{:S(2)}) collective-permute-start(bf16[4,2,8,512]{3,2,1,0:T(8,128)(2,1)S(1)} %get-tuple-element.23), channel_id=1, source_target_pairs={{0,16},{2,18},{4,20},{6,22},{8,24},{10,26},{12,28},{14,30},{16,0},... | collective-permute-start | bytes 196616 | tf_op jit(solution)/shard_map/ppermute | solution.py:500
  34.5 6.5 %collective-permute-start.3 = (bf16[4,2,8,512]{3,2,1,0:T(8,128)(2,1)S(1)}, bf16[4,2,8,512]{3,2,1,0:T(8,128)(2,1)S(1)}, u32[]{:S(2)}, u32[]{:S(2)}) collective-permute-start(bf16[4,2,8,512]{3,2,1,0:T(8,128)(2,1)S(1)} %get-tuple-element.24), channel_id=1, source_target_pairs={{0,24},{2,26},{4,28},{6,30},{8,16},{10,18},{12,20},{14,22},{16,8},... | collective-permute-start | bytes 196616 | tf_op jit(solution)/shard_map/ppermute | solution.py:500
  38.3 4.2 %collective-permute-start.11 = (bf16[8,2,8,512]{3,2,1,0:T(8,128)(2,1)S(1)}, bf16[8,2,8,512]{3,2,1,0:T(8,128)(2,1)S(1)}, u32[]{:S(2)}, u32[]{:S(2)}) collective-permute-start(bf16[8,2,8,512]{3,2,1,0:T(8,128)(2,1)S(1)} %collect.6), channel_id=1, source_target_pairs={{0,4},{2,6},{4,0},{6,2},{8,12},{10,14},{12,8},{14,10},{16,20},{18,... | collective-permute-start | bytes 393224 | tf_op jit(solution)/shard_map/ppermute | solution.py:500
  41.1 6.1 %collective-permute-start.4 = (bf16[8,2,8,512]{3,2,1,0:T(8,128)(2,1)S(1)}, bf16[8,2,8,512]{3,2,1,0:T(8,128)(2,1)S(1)}, u32[]{:S(2)}, u32[]{:S(2)}) collective-permute-start(bf16[8,2,8,512]{3,2,1,0:T(8,128)(2,1)S(1)} %collect.4), channel_id=1, source_target_pairs={{0,4},{2,6},{4,0},{6,2},{8,12},{10,14},{12,8},{14,10},{16,20},{18,... | collective-permute-start | bytes 393224 | tf_op jit(solution)/shard_map/ppermute | solution.py:500
  42.4 6.1 %collective-permute-start.12 = (bf16[8,2,8,512]{3,2,1,0:T(8,128)(2,1)S(1)}, bf16[8,2,8,512]{3,2,1,0:T(8,128)(2,1)S(1)}, u32[]{:S(2)}, u32[]{:S(2)}) collective-permute-start(bf16[8,2,8,512]{3,2,1,0:T(8,128)(2,1)S(1)} %collect.7), channel_id=1, source_target_pairs={{0,2},{2,0},{4,6},{6,4},{8,10},{10,8},{12,14},{14,12},{16,18},{18,... | collective-permute-start | bytes 393224 | tf_op jit(solution)/shard_map/ppermute | solution.py:500
  47.1 3.0 %collective-permute-start.5 = (bf16[8,2,8,512]{3,2,1,0:T(8,128)(2,1)S(1)}, bf16[8,2,8,512]{3,2,1,0:T(8,128)(2,1)S(1)}, u32[]{:S(2)}, u32[]{:S(2)}) collective-permute-start(bf16[8,2,8,512]{3,2,1,0:T(8,128)(2,1)S(1)} %collect.5), channel_id=1, source_target_pairs={{0,2},{2,0},{4,6},{6,4},{8,10},{10,8},{12,14},{14,12},{16,18},{18,... | collective-permute-start | bytes 393224 | tf_op jit(solution)/shard_map/ppermute | solution.py:500
  48.6 9.8 %collective-permute-start.13 = (bf16[16,2,8,512]{3,2,1,0:T(8,128)(2,1)S(1)}, bf16[16,2,8,512]{3,2,1,0:T(8,128)(2,1)S(1)}, u32[]{:S(2)}, u32[]{:S(2)}) collective-permute-start(bf16[16,2,8,512]{3,2,1,0:T(8,128)(2,1)S(1)} %assemble.3.refs_1_), channel_id=1, source_target_pairs={{0,1},{1,0},{2,3},{3,2},{4,5},{5,4},{6,7},{7,6},{8,9},{9,8},{10,11... | collective-permute-start | bytes 786440 | tf_op jit(solution)/shard_map/ppermute | solution.py:553
  49.8 12.2 %collective-permute-start.15 = (bf16[16,2,8,512]{3,2,1,0:T(8,128)(2,1)S(1)}, bf16[16,2,8,512]{3,2,1,0:T(8,128)(2,1)S(1)}, u32[]{:S(2)}, u32[]{:S(2)}) collective-permute-start(bf16[16,2,8,512]{3,2,1,0:T(8,128)(2,1)S(1)} %all-to-all-done.refs_2_), channel_id=1, source_target_pairs={{0,1},{1,0},{2,3},{3,2},{4,5},{5,4},{6,7},{7,6},{8,9},{9,8},{10,11... | collective-permute-start | bytes 786440 | tf_op jit(solution)/shard_map/ppermute | solution.py:553
  50.1 18.7 %collective-permute-start.6 = (bf16[16,2,8,512]{3,2,1,0:T(8,128)(2,1)S(1)}, bf16[16,2,8,512]{3,2,1,0:T(8,128)(2,1)S(1)}, u32[]{:S(2)}, u32[]{:S(2)}) collective-permute-start(bf16[16,2,8,512]{3,2,1,0:T(8,128)(2,1)S(1)} %assemble.2.refs_4_), channel_id=1, source_target_pairs={{0,1},{1,0},{2,3},{3,2},{4,5},{5,4},{6,7},{7,6},{8,9},{9,8},{10,11... | collective-permute-start | bytes 786440 | tf_op jit(solution)/shard_map/ppermute | solution.py:553
